TPU v7x, 32 devices: a whole 2x2x4 slice. The times are simulated.
32 devices in a mesh: ctx: 2 (over x), dp: 4 (over z), tp: 4 (over y, core).
Axes of the slice: x: 2, y: 2, z: 4, core: 2. Of those that a mesh axis runs over, the one named last changes fastest.
Arguments:
- query_act: bfloat16 [4, 4096, 256], P('dp', 'tp', 'ctx'), may hold values from -6 to 6
- key_act: bfloat16 [4, 4096, 256], P('dp', 'tp', 'ctx'), may hold values from -6 to 6
- value_act: bfloat16 [4, 4096, 256], P('dp', 'tp', 'ctx'), may hold values from -6 to 6
- out_grad: bfloat16 [4, 4096, 256], P('dp', 'tp', 'ctx'), may hold values from -6 to 6
- keep_mask: int32 [4, 256], P('dp', 'ctx'), may hold values 0 or 1
- filter_taps: float32 [256, 128], P('tp'), may hold values from -0.5 to 0.5
- skip_gain: float32 [4096], P('tp'), may hold values from -4 to 4
Outputs:
- operator_out: bfloat16 [4, 4096, 256], P('dp', 'tp', 'ctx')
- query_grad: bfloat16 [4, 4096, 256], P('dp', 'tp', 'ctx')
- key_grad: bfloat16 [4, 4096, 256], P('dp', 'tp', 'ctx')
- value_grad: bfloat16 [4, 4096, 256], P('dp', 'tp', 'ctx')
- filter_grad: float32 [256, 128], P('tp')
- skip_grad: float32 [4096], P('tp')
All inputs are finite; a program needn't handle non-finite values. No bound on the sum of `keep_mask` on one device may be relied on, other than what follows from the above.
Results may differ from a plain program's by a relative error of at most 0.007.
Values may be sent and summed in bfloat16 or wider, within the bound.
No kernel may reach another device: no remote copies, remote signals or barrier semaphores. Data moves between devices by JAX's collectives and lax.ppermute only.
A program may use at most 64 MiB of HBM per device.

v0:
```python
import math

import jax
import jax.numpy as jnp
from jax import lax
from jax.sharding import PartitionSpec as P


def tap_matrices(tap_rows):
    tap_len = tap_rows.shape[1]
    source = jnp.arange(tap_len)[:, None]
    target = jnp.arange(tap_len)[None, :]
    spread = tap_rows[:, jnp.mod(target - source, tap_len)]
    nothing = jnp.zeros((), jnp.bfloat16)
    lower_part = jnp.where(target >= source, spread, nothing)
    upper_part = jnp.where(target < source, spread, nothing)
    forward = jnp.concatenate([upper_part, lower_part], axis=1)
    backward = jnp.concatenate(
        [jnp.swapaxes(lower_part, 1, 2), jnp.swapaxes(upper_part, 1, 2)], axis=1
    )
    return (forward, backward)


def diagonal_sums(gram_sums):
    groups, tap_len, double_len = gram_sums.shape
    flattened = gram_sums.reshape(groups, tap_len * double_len)
    flattened = jnp.pad(flattened, ((0, 0), (0, tap_len)))
    skewed = flattened.reshape(groups, tap_len, double_len + 1)
    columns = jnp.sum(skewed, axis=1)
    return columns[:, tap_len:0:-1]


def core(
    query_act, key_act, value_act, scaled_grad, filter_taps, skip_gain, fetch_left, fetch_right
):
    windows, channels, length = query_act.shape
    groups, tap_len = filter_taps.shape
    per_group = channels // groups
    blocks = length // tap_len
    forward, backward = tap_matrices(filter_taps.astype(jnp.bfloat16))
    joined = (key_act.astype(jnp.float32) * value_act.astype(jnp.float32)).astype(jnp.bfloat16)
    before = fetch_left(joined[:, :, length - tap_len :])
    joined_blocks = joined.reshape(windows, channels, blocks, tap_len)
    earlier = jnp.concatenate([before[:, :, None, :], joined_blocks[:, :, :-1, :]], axis=2)
    paired = jnp.concatenate([earlier, joined_blocks], axis=3).reshape(
        windows, groups, per_group, blocks, 2 * tap_len
    )
    mixed_sum = jnp.einsum("wgcbs,gst->wgcbt", paired, forward, preferred_element_type=jnp.float32)
    mixed_sum = mixed_sum.reshape(windows, channels, length) + skip_gain[
        None, :, None
    ] * joined.astype(jnp.float32)
    operator_out = (query_act.astype(jnp.float32) * mixed_sum).astype(jnp.bfloat16)
    mixed_grad = (scaled_grad.astype(jnp.float32) * query_act.astype(jnp.float32)).astype(
        jnp.bfloat16
    )
    query_grad = (scaled_grad.astype(jnp.float32) * mixed_sum).astype(jnp.bfloat16)
    following = fetch_right(mixed_grad[:, :, :tap_len])
    grad_blocks = mixed_grad.reshape(windows, channels, blocks, tap_len)
    next_blocks = jnp.concatenate([grad_blocks[:, :, 1:, :], following[:, :, None, :]], axis=2)
    paired_grad = jnp.concatenate([grad_blocks, next_blocks], axis=3).reshape(
        windows, groups, per_group, blocks, 2 * tap_len
    )
    joined_grad = jnp.einsum(
        "wgcbs,gst->wgcbt", paired_grad, backward, preferred_element_type=jnp.float32
    )
    joined_grad = joined_grad.reshape(windows, channels, length) + skip_gain[
        None, :, None
    ] * mixed_grad.astype(jnp.float32)
    key_grad = (joined_grad * value_act.astype(jnp.float32)).astype(jnp.bfloat16)
    value_grad = (joined_grad * key_act.astype(jnp.float32)).astype(jnp.bfloat16)
    grad_groups = grad_blocks.reshape(windows, groups, per_group, blocks, tap_len)
    gram_sums = jnp.einsum(
        "wgcbt,wgcbs->gts", grad_groups, paired, preferred_element_type=jnp.float32
    )
    tap_sums = diagonal_sums(gram_sums)
    skip_sums = jnp.sum(mixed_grad.astype(jnp.float32) * joined.astype(jnp.float32), axis=(0, 2))
    return (operator_out, query_grad, key_grad, value_grad, tap_sums, skip_sums)


def no_rim(border):
    return jnp.zeros_like(border)


def body(query_act, key_act, value_act, out_grad, keep_mask, filter_taps, skip_gain):
    total_windows = keep_mask.shape[0] * lax.axis_size("dp")
    total_length = query_act.shape[2] * lax.axis_size("ctx")
    per_group = query_act.shape[1] // filter_taps.shape[0]
    tap_scale = 1.0 / math.sqrt(total_windows * total_length * per_group)
    skip_scale = 1.0 / math.sqrt(total_windows * total_length)
    scaled_grad = out_grad * keep_mask.astype(jnp.bfloat16)[:, None, :]
    moved = (
        lax.all_to_all(query_act, "ctx", split_axis=1, concat_axis=2, tiled=True),
        lax.all_to_all(key_act, "ctx", split_axis=1, concat_axis=2, tiled=True),
        lax.all_to_all(value_act, "ctx", split_axis=1, concat_axis=2, tiled=True),
        lax.all_to_all(scaled_grad, "ctx", split_axis=1, concat_axis=2, tiled=True),
    )
    shards = lax.axis_size("ctx")
    position = lax.axis_index("ctx")
    group_count = filter_taps.shape[0] // shards
    own_taps = lax.dynamic_slice_in_dim(filter_taps, position * group_count, group_count, 0)
    own_skip = lax.dynamic_slice_in_dim(
        skip_gain, position * group_count * per_group, group_count * per_group, 0
    )
    results = core(moved[0], moved[1], moved[2], moved[3], own_taps, own_skip, no_rim, no_rim)
    returned = (
        lax.all_to_all(results[0], "ctx", split_axis=2, concat_axis=1, tiled=True),
        lax.all_to_all(results[1], "ctx", split_axis=2, concat_axis=1, tiled=True),
        lax.all_to_all(results[2], "ctx", split_axis=2, concat_axis=1, tiled=True),
        lax.all_to_all(results[3], "ctx", split_axis=2, concat_axis=1, tiled=True),
    )
    replica = lax.psum((results[4], results[5]), "dp")
    gathered = (
        lax.all_gather(replica[0], "ctx", axis=0, tiled=True),
        lax.all_gather(replica[1], "ctx", axis=0, tiled=True),
    )
    tap_sums = gathered[0]
    skip_sums = gathered[1]
    return (
        returned[0],
        returned[1],
        returned[2],
        returned[3],
        tap_sums * tap_scale,
        skip_sums * skip_scale,
    )


def solution(mesh):
    return jax.shard_map(
        body,
        mesh=mesh,
        in_specs=(
            P("dp", "tp", "ctx"),
            P("dp", "tp", "ctx"),
            P("dp", "tp", "ctx"),
            P("dp", "tp", "ctx"),
            P("dp", "ctx"),
            P("tp", None),
            P("tp"),
        ),
        out_specs=(
            P("dp", "tp", "ctx"),
            P("dp", "tp", "ctx"),
            P("dp", "tp", "ctx"),
            P("dp", "tp", "ctx"),
            P("tp", None),
            P("tp"),
        ),
        check_vma=False,
    )
```

profile of v0, /device:TPU:0, one launch (start us, length us, event | category | flops | bytes accessed | tf_op | source)
XLA Modules:
  0.0 214.4 jit_solution(10341014407572912905)
XLA Ops:
  3.3 2.2 %reduce.3 = bf16[1024,128]{1,0:T(8,128)(2,1)S(1)} reduce(bf16[1024,1,128]{2,1,0:T(2,128)(2,1)S(1)} %fusion.30, bf16[]{:T(256)} %broadcast.146), dimensions={1}, to_apply=%fusion.30.reduce_sub_computation | reduce | bytes 524290
  6.3 4.2 %all-to-all-start.4 = ((bf16[2,2,32768]{2,1,0:T(2,128)(2,1)}), bf16[2,2,32768]{2,1,0:T(2,128)(2,1)S(1)}, u32[]{:S(2)}, u32[]{:S(2)}) async-start(bf16[2,2,32768]{2,1,0:T(2,128)(2,1)} %reshape.430), calls=%async_computation.4 | async-start | bytes 524288 | tf_op jit(solution)/shard_map/all_to_all | solution.py:95
  10.8 57.4 %gather_fusion = bf16[16384,32]{1,0:T(8,128)(2,1)} fusion(bf16[32,128]{0,1:T(8,128)(2,1)S(1)} %copy.92, s32[16384]{0:T(1024)S(1)} %fusion.22), kind=kCustom, calls=%fused_computation | custom fusion | bytes 2162688 | tf_op jit(solution)/shard_map/gather | solution.py:13
  68.2 4.0 %copy.82 = bf16[128,128,32]{1,0,2:T(8,128)(2,1)S(1)} copy(bf16[128,128,32]{2,1,0:T(8,128)(2,1)} %bitcast.156) | data formatting | bytes 2097152 | tf_op jit(solution)/shard_map/gather | solution.py:13
  75.5 2.2 %reduce.2 = bf16[1024,128]{1,0:T(8,128)(2,1)S(1)} reduce(bf16[1024,1,128]{2,1,0:T(2,128)(2,1)S(1)} %bitcast.187, bf16[]{:T(256)} %broadcast.146), dimensions={1}, to_apply=%bitcast.153.reduce_sub_computation | reduce | bytes 524290
  78.9 2.2 %reduce.4 = bf16[1024,128]{1,0:T(8,128)(2,1)S(1)} reduce(bf16[1024,1,128]{2,1,0:T(2,128)(2,1)S(1)} %bitcast.188, bf16[]{:T(256)} %broadcast.146), dimensions={1}, to_apply=%bitcast.152.reduce_sub_computation | reduce | bytes 524290
  82.3 2.2 %reduce.1 = bf16[1024,128]{1,0:T(8,128)(2,1)S(1)} reduce(bf16[1024,1,128]{2,1,0:T(2,128)(2,1)S(1)} %bitcast.189, bf16[]{:T(256)} %broadcast.146), dimensions={1}, to_apply=%bitcast.151.reduce_sub_computation | reduce | bytes 524290
  85.4 3.5 %all-to-all-start = ((bf16[2,2,32768]{2,1,0:T(2,128)(2,1)}), bf16[2,2,32768]{2,1,0:T(2,128)(2,1)S(1)}, u32[]{:S(2)}, u32[]{:S(2)}) async-start(bf16[2,2,32768]{2,1,0:T(2,128)(2,1)} %reshape.422), calls=%async_computation | async-start | bytes 524288 | tf_op jit(solution)/shard_map/all_to_all | solution.py:92
  89.2 5.5 %all-to-all-done = bf16[2,2,32768]{2,1,0:T(2,128)(2,1)S(1)} async-done(((bf16[2,2,32768]{2,1,0:T(2,128)(2,1)}), bf16[2,2,32768]{2,1,0:T(2,128)(2,1)S(1)}, u32[]{:S(2)}, u32[]{:S(2)}) %all-to-all-start) | async-done | bytes 262176 | tf_op jit(solution)/shard_map/all_to_all | solution.py:92
  94.7 3.4 %all-to-all-start.1 = ((bf16[2,2,32768]{2,1,0:T(2,128)(2,1)}), bf16[2,2,32768]{2,1,0:T(2,128)(2,1)S(1)}, u32[]{:S(2)}, u32[]{:S(2)}) async-start(bf16[2,2,32768]{2,1,0:T(2,128)(2,1)} %reshape.424), calls=%async_computation.1 | async-start | bytes 524288 | tf_op jit(solution)/shard_map/all_to_all | solution.py:93
  98.6 4.7 %all-to-all-done.1 = bf16[2,2,32768]{2,1,0:T(2,128)(2,1)S(1)} async-done(((bf16[2,2,32768]{2,1,0:T(2,128)(2,1)}), bf16[2,2,32768]{2,1,0:T(2,128)(2,1)S(1)}, u32[]{:S(2)}, u32[]{:S(2)}) %all-to-all-start.1) | async-done | bytes 262176 | tf_op jit(solution)/shard_map/all_to_all | solution.py:93
  103.3 3.6 %all-to-all-start.2 = ((bf16[2,2,32768]{2,1,0:T(2,128)(2,1)}), bf16[2,2,32768]{2,1,0:T(2,128)(2,1)S(1)}, u32[]{:S(2)}, u32[]{:S(2)}) async-start(bf16[2,2,32768]{2,1,0:T(2,128)(2,1)} %reshape.426), calls=%async_computation.2 | async-start | bytes 524288 | tf_op jit(solution)/shard_map/all_to_all | solution.py:94
  107.3 4.6 %all-to-all-done.2 = bf16[2,2,32768]{2,1,0:T(2,128)(2,1)S(1)} async-done(((bf16[2,2,32768]{2,1,0:T(2,128)(2,1)}), bf16[2,2,32768]{2,1,0:T(2,128)(2,1)S(1)}, u32[]{:S(2)}, u32[]{:S(2)}) %all-to-all-start.2) | async-done | bytes 262176 | tf_op jit(solution)/shard_map/all_to_all | solution.py:94
  116.7 2.3 %fusion.6 = f32[1,32,16,2,128]{4,2,3,1,0:T(8,128)S(1)} fusion(bf16[32,128,128]{1,2,0:T(8,128)(2,1)} %get-tuple-element.15, bf16[32,128,128]{1,2,0:T(8,128)(2,1)} %get-tuple-element.14, bf16[1,32,16,2,128]{4,2,1,3,0:T(8,128)(2,1)S(1)} %bitcast.196, bf16[1,32,16,2,128]{4,2,1,3,0:T(8,128)(2,1)S(1)} %bitcast.170), kind=kOutput, calls=%fused_computation.9 | convolution fusion | flops 72351744 | bytes 3145728 | tf_op jit(solution)/shard_map/wgcbs,gst->wgcbt/dot_general | solution.py:63
  122.9 2.3 %fusion.16 = (bf16[1,512,256]{1,2,0:T(8,128)(2,1)}, bf16[1,512,256]{1,2,0:T(8,128)(2,1)S(1)}, bf16[1,512,256]{1,2,0:T(8,128)(2,1)}, bf16[1,512,256]{1,2,0:T(8,128)(2,1)S(1)}) fusion(f32[1,512,2,128]{1,3,2,0:T(8,128)} %copy.60, f32[1,512,256]{1,2,0:T(8,128)S(1)} %copy.74, f32[512]{0:T(512)S(1)} %dynamic_slice.7, f32[1,512,2,128]{1,3,2,0:T(8,128)S(1)} %copy.50, ...), kind=kLoop, calls=%fused_computation.30 | loop fusion | flops 1835008 | bytes 4196352 | tf_op jit(solution)/shard_map/convert_element_type | solution.py:70
  126.0 2.2 %reduce.7 = bf16[256,512]{1,0:T(8,128)(2,1)S(1)} reduce(bf16[256,1,512]{2,1,0:T(2,128)(2,1)S(1)} %bitcast.184, bf16[]{:T(256)} %broadcast.146), dimensions={1}, to_apply=%bitcast.148.reduce_sub_computation | reduce | bytes 524290
  129.1 3.4 %all-to-all-start.6 = ((bf16[2,2,32768]{2,1,0:T(2,128)(2,1)}), bf16[2,2,32768]{2,1,0:T(2,128)(2,1)S(1)}, u32[]{:S(2)}, u32[]{:S(2)}) async-start(bf16[2,2,32768]{2,1,0:T(2,128)(2,1)} %reshape.434), calls=%async_computation.6 | async-start | bytes 524288 | tf_op jit(solution)/shard_map/all_to_all | solution.py:108
  132.6 2.7 %fusion.8 = f32[32,128,256,1]{2,1,0,3:T(8,128)} fusion(bf16[32,16,2,128]{3,1,0,2:T(8,128)(2,1)S(1)} %bitcast.171, bf16[1,32,16,2,128]{4,2,1,3,0:T(8,128)(2,1)S(1)} %bitcast.167, bf16[1,32,16,2,128]{4,2,1,3,0:T(8,128)(2,1)S(1)} %bitcast.191), kind=kOutput, calls=%fused_computation.17 | convolution fusion | flops 68157440 | bytes 4980736 | tf_op jit(solution)/shard_map/wgcbt,wgcbs->gts/dot_general | solution.py:72
  135.7 2.2 %reduce.8 = bf16[256,512]{1,0:T(8,128)(2,1)S(1)} reduce(bf16[256,1,512]{2,1,0:T(2,128)(2,1)S(1)} %bitcast.185, bf16[]{:T(256)} %broadcast.146), dimensions={1}, to_apply=%bitcast.147.reduce_sub_computation | reduce | bytes 524290
  139.2 2.2 %reduce.5 = bf16[256,512]{1,0:T(8,128)(2,1)S(1)} reduce(bf16[256,1,512]{2,1,0:T(2,128)(2,1)S(1)} %bitcast.186, bf16[]{:T(256)} %broadcast.146), dimensions={1}, to_apply=%bitcast.150.reduce_sub_computation | reduce | bytes 524290
  142.7 2.2 %reduce.6 = bf16[256,512]{1,0:T(8,128)(2,1)S(1)} reduce(bf16[256,1,512]{2,1,0:T(2,128)(2,1)S(1)} %bitcast.181, bf16[]{:T(256)} %broadcast.146), dimensions={1}, to_apply=%bitcast.149.reduce_sub_computation | reduce | bytes 524290
  145.8 4.6 %copy.93 = f32[4,8,128,256]{3,1,2,0:T(8,128)S(1)} copy(f32[4,8,128,256]{3,2,1,0:T(8,128)} %bitcast.154) | data formatting | bytes 8388608
  150.4 2.3 %pad.6 = f32[32,32896]{1,0:T(8,128)} pad(f32[32,32768]{1,0:T(8,128)S(1)} %bitcast.155, f32[]{:T(128)} %constant.40.clone.1), padding=0_0x0_128 | pad | bytes 8404996 | tf_op jit(solution)/shard_map/jit(_pad)/pad | solution.py:27
  152.8 8.0 %reshape.397 = f32[32,128,257]{2,1,0:T(8,128)} reshape(f32[32,32896]{1,0:T(8,128)} %pad.6) | data formatting | bytes 8421376 | tf_op jit(solution)/shard_map/reshape | solution.py:28
  160.7 3.3 %reduce_sum.18 = f32[32,257]{1,0:T(8,128)S(1)} reduce(f32[32,128,257]{2,1,0:T(8,128)} %reshape.397, f32[]{:T(128)} %constant.40.clone.1), dimensions={1}, to_apply=%region_0.1 | reduce | flops 1044448 | bytes 4243588 | tf_op jit(solution)/shard_map/reduce_sum | solution.py:29
  164.2 3.4 %all-to-all-start.7 = ((bf16[2,2,32768]{2,1,0:T(2,128)(2,1)}), bf16[2,2,32768]{2,1,0:T(2,128)(2,1)S(1)}, u32[]{:S(2)}, u32[]{:S(2)}) async-start(bf16[2,2,32768]{2,1,0:T(2,128)(2,1)} %reshape.436), calls=%async_computation.7 | async-start | bytes 524288 | tf_op jit(solution)/shard_map/all_to_all | solution.py:109
  167.8 19.4 %all-reduce.3 = (f32[32,128]{1,0:T(8,128)S(1)}, f32[512]{0:T(512)S(1)}) all-reduce(f32[32,128]{1,0:T(8,128)S(1)} %rev.3, f32[512]{0:T(512)S(1)} %multiply_reduce_fusion), channel_id=1, replica_groups=mesh['ctx'=2,'dp'=4,'tp'=4] {'dp'}, use_global_device_ids=true, to_apply=%region_1.2 | all-reduce | flops 4608 | bytes 36864 | tf_op jit(solution)/shard_map/psum | solution.py:111
  187.2 4.3 %all-gather = f32[2,1,512]{2,1,0:T(1,128)S(1)} all-gather(f32[1,1,512]{2,1,0:T(1,128)S(1)} %bitcast.202), channel_id=1, replica_groups=mesh['ctx'=2,'dp'=4,'tp'=4] {'ctx'}, dimensions={0}, use_global_device_ids=true | all-gather | bytes 6144 | tf_op jit(solution)/shard_map/all_gather | solution.py:114
  191.6 4.4 %all_gather.6 = f32[64,128]{1,0:T(8,128)S(1)} all-gather(f32[32,128]{1,0:T(8,128)S(1)} %get-tuple-element.6), channel_id=1, replica_groups=mesh['ctx'=2,'dp'=4,'tp'=4] {'ctx'}, dimensions={0}, use_global_device_ids=true | all-gather | bytes 49152 | tf_op jit(solution)/shard_map/all_gather | solution.py:113
  196.0 3.4 %all-to-all-start.3 = ((bf16[2,2,32768]{2,1,0:T(2,128)(2,1)}), bf16[2,2,32768]{2,1,0:T(2,128)(2,1)S(1)}, u32[]{:S(2)}, u32[]{:S(2)}) async-start(bf16[2,2,32768]{2,1,0:T(2,128)(2,1)} %reshape.428), calls=%async_computation.3 | async-start | bytes 524288 | tf_op jit(solution)/shard_map/all_to_all | solution.py:106
  200.0 4.6 %all-to-all-done.3 = bf16[2,2,32768]{2,1,0:T(2,128)(2,1)S(1)} async-done(((bf16[2,2,32768]{2,1,0:T(2,128)(2,1)}), bf16[2,2,32768]{2,1,0:T(2,128)(2,1)S(1)}, u32[]{:S(2)}, u32[]{:S(2)}) %all-to-all-start.3) | async-done | bytes 262176 | tf_op jit(solution)/shard_map/all_to_all | solution.py:106
  204.6 3.4 %all-to-all-start.5 = ((bf16[2,2,32768]{2,1,0:T(2,128)(2,1)}), bf16[2,2,32768]{2,1,0:T(2,128)(2,1)S(1)}, u32[]{:S(2)}, u32[]{:S(2)}) async-start(bf16[2,2,32768]{2,1,0:T(2,128)(2,1)} %reshape.432), calls=%async_computation.5 | async-start | bytes 524288 | tf_op jit(solution)/shard_map/all_to_all | solution.py:107
  (85 shorter events, 32.5 us)
Async XLA Ops:
  0.6 10.0 %copy-start = (f32[64,128]{1,0:T(8,128)S(1)}, f32[64,128]{1,0:T(8,128)}, u32[]{:S(2)}) copy-start(f32[64,128]{1,0:T(8,128)} %param.12) | copy-start | bytes 98308
  6.3 79.1 %all-to-all-start.4 = ((bf16[2,2,32768]{2,1,0:T(2,128)(2,1)}), bf16[2,2,32768]{2,1,0:T(2,128)(2,1)S(1)}, u32[]{:S(2)}, u32[]{:S(2)}) async-start(bf16[2,2,32768]{2,1,0:T(2,128)(2,1)} %reshape.430), calls=%async_computation.4 | async-start | bytes 524288 | tf_op jit(solution)/shard_map/all_to_all | solution.py:95
  72.2 3.0 %copy-start.3 = (bf16[1,1024,128]{2,1,0:T(8,128)(2,1)S(1)}, bf16[1,1024,128]{2,1,0:T(8,128)(2,1)}, u32[]{:S(2)}) copy-start(bf16[1,1024,128]{2,1,0:T(8,128)(2,1)} %param.7) | copy-start | bytes 786436
  72.2 6.3 %copy-start.4 = (bf16[1,1024,128]{2,1,0:T(8,128)(2,1)S(1)}, bf16[1,1024,128]{2,1,0:T(8,128)(2,1)}, u32[]{:S(2)}) copy-start(bf16[1,1024,128]{2,1,0:T(8,128)(2,1)} %param.8) | copy-start | bytes 786436
  73.7 8.2 %copy-start.5 = (bf16[1,1024,128]{2,1,0:T(8,128)(2,1)S(1)}, bf16[1,1024,128]{2,1,0:T(8,128)(2,1)}, u32[]{:S(2)}) copy-start(bf16[1,1024,128]{2,1,0:T(8,128)(2,1)} %param.9) | copy-start | bytes 786436
  73.7 11.6 %copy-start.6 = (f32[1024]{0:T(1024)S(1)}, f32[1024]{0:T(1024)}, u32[]{:S(2)}) copy-start(f32[1024]{0:T(1024)} %param.13) | copy-start | bytes 12292
  85.4 9.3 %all-to-all-start = ((bf16[2,2,32768]{2,1,0:T(2,128)(2,1)}), bf16[2,2,32768]{2,1,0:T(2,128)(2,1)S(1)}, u32[]{:S(2)}, u32[]{:S(2)}) async-start(bf16[2,2,32768]{2,1,0:T(2,128)(2,1)} %reshape.422), calls=%async_computation | async-start | bytes 524288 | tf_op jit(solution)/shard_map/all_to_all | solution.py:92
  94.7 8.6 %all-to-all-start.1 = ((bf16[2,2,32768]{2,1,0:T(2,128)(2,1)}), bf16[2,2,32768]{2,1,0:T(2,128)(2,1)S(1)}, u32[]{:S(2)}, u32[]{:S(2)}) async-start(bf16[2,2,32768]{2,1,0:T(2,128)(2,1)} %reshape.424), calls=%async_computation.1 | async-start | bytes 524288 | tf_op jit(solution)/shard_map/all_to_all | solution.py:93
  103.3 8.6 %all-to-all-start.2 = ((bf16[2,2,32768]{2,1,0:T(2,128)(2,1)}), bf16[2,2,32768]{2,1,0:T(2,128)(2,1)S(1)}, u32[]{:S(2)}, u32[]{:S(2)}) async-start(bf16[2,2,32768]{2,1,0:T(2,128)(2,1)} %reshape.426), calls=%async_computation.2 | async-start | bytes 524288 | tf_op jit(solution)/shard_map/all_to_all | solution.py:94
  125.6 9.7 %copy-start.2 = (bf16[1,512,256]{1,2,0:T(8,128)(2,1)S(1)}, bf16[1,512,256]{1,2,0:T(8,128)(2,1)}, u32[]{:S(2)}) copy-start(bf16[1,512,256]{1,2,0:T(8,128)(2,1)} %get-tuple-element.8) | copy-start | bytes 786436
  129.1 35.1 %all-to-all-start.6 = ((bf16[2,2,32768]{2,1,0:T(2,128)(2,1)}), bf16[2,2,32768]{2,1,0:T(2,128)(2,1)S(1)}, u32[]{:S(2)}, u32[]{:S(2)}) async-start(bf16[2,2,32768]{2,1,0:T(2,128)(2,1)} %reshape.434), calls=%async_computation.6 | async-start | bytes 524288 | tf_op jit(solution)/shard_map/all_to_all | solution.py:108
  132.6 9.8 %copy-start.1 = (bf16[1,512,256]{1,2,0:T(8,128)(2,1)S(1)}, bf16[1,512,256]{1,2,0:T(8,128)(2,1)}, u32[]{:S(2)}) copy-start(bf16[1,512,256]{1,2,0:T(8,128)(2,1)} %get-tuple-element.12) | copy-start | bytes 786436
  164.2 31.8 %all-to-all-start.7 = ((bf16[2,2,32768]{2,1,0:T(2,128)(2,1)}), bf16[2,2,32768]{2,1,0:T(2,128)(2,1)S(1)}, u32[]{:S(2)}, u32[]{:S(2)}) async-start(bf16[2,2,32768]{2,1,0:T(2,128)(2,1)} %reshape.436), calls=%async_computation.7 | async-start | bytes 524288 | tf_op jit(solution)/shard_map/all_to_all | solution.py:109
  196.0 8.6 %all-to-all-start.3 = ((bf16[2,2,32768]{2,1,0:T(2,128)(2,1)}), bf16[2,2,32768]{2,1,0:T(2,128)(2,1)S(1)}, u32[]{:S(2)}, u32[]{:S(2)}) async-start(bf16[2,2,32768]{2,1,0:T(2,128)(2,1)} %reshape.428), calls=%async_computation.3 | async-start | bytes 524288 | tf_op jit(solution)/shard_map/all_to_all | solution.py:106
  204.6 8.6 %all-to-all-start.5 = ((bf16[2,2,32768]{2,1,0:T(2,128)(2,1)}), bf16[2,2,32768]{2,1,0:T(2,128)(2,1)S(1)}, u32[]{:S(2)}, u32[]{:S(2)}) async-start(bf16[2,2,32768]{2,1,0:T(2,128)(2,1)} %reshape.432), calls=%async_computation.5 | async-start | bytes 524288 | tf_op jit(solution)/shard_map/all_to_all | solution.py:107
where the time goes:
time: 215 us; the launch traced here: 214 us
  local copies, waits for them, and re-layouts  97.8 us (45%)
  other arithmetic  31.3 us (15%)
  starting transfers between devices  28.5 us (13%)
  blocking collectives  28.2 us (13%)
  waiting for transfers between devices  20.6 us (10%)
  matrix products  6.98 us (3%)
    gather x2, local copies, waits for them, and re-layouts, tap_matrices(): spread = tap_rows[:, jnp.mod(target - source, tap_len)]  61.4 us
    psum x1, blocking collectives, body(): replica = lax.psum((results[4], results[5]), 'dp')  19.4 us
    unnamed x9, other arithmetic  19.2 us
    unnamed x40, local copies, waits for them, and re-layouts  15.5 us
    reshape x1, local copies, waits for them, and re-layouts, diagonal_sums(): skewed = flattened.reshape(groups, tap_len, double_len + 1)  7.98 us
    all_to_all x1, waiting for transfers between devices, body(): lax.all_to_all(query_act, 'ctx', split_axis=1, concat_axis=2, tiled=True)  5.54 us
    all_to_all x1, waiting for transfers between devices, body(): lax.all_to_all(key_act, 'ctx', split_axis=1, concat_axis=2, tiled=True)  4.75 us
    all_to_all x1, waiting for transfers between devices, body(): lax.all_to_all(value_act, 'ctx', split_axis=1, concat_axis=2, tiled=True)  4.65 us
  transfers between devices with their start and end apart: 8, of which 5 were waited for; matrix products, arithmetic and copies ran while one was open for 52% of the time, Pallas kernels for 0%

commit v1 on v0

v1 whole, which is shorter than its diff:
```python
import functools
import math

import jax
import jax.numpy as jnp
from jax import lax
from jax.experimental import pallas as pl
from jax.experimental.pallas import tpu as pltpu
from jax.sharding import PartitionSpec as P

BF16 = jnp.bfloat16
F32 = jnp.float32
ROWS_BY_ROWS = (((1,), (1,)), ((), ()))


def iotas(rows, columns):
    return (
        lax.broadcasted_iota(jnp.int32, (rows, columns), 0),
        lax.broadcasted_iota(jnp.int32, (rows, columns), 1),
    )


def flip(block):
    length = block.shape[1]
    row, column = iotas(length, length)
    mirror = (row + column == length - 1).astype(F32).astype(BF16)
    return jnp.dot(block, mirror, preferred_element_type=F32).astype(BF16)


def lag_sums(grad, joined, per_group, wanted):
    channels, length = grad.shape
    per = length // per_group
    row, column = iotas(length, length)
    kept = wanted(row + column)
    mirrored = flip(joined)
    nothing = jnp.zeros((per_group, length), BF16)
    sums = []
    for start in range(0, channels, length):
        across = grad[start : start + length].T
        for g in range(per):
            mine = mirrored[start + g * per_group : start + (g + 1) * per_group]
            spread = jnp.concatenate([nothing] * g + [mine] + [nothing] * (per - 1 - g), axis=0)
            gram = jnp.where(kept, jnp.dot(across, spread, preferred_element_type=F32), 0.0)
            turned = pltpu.roll(gram, 0, 1, stride=1, stride_axis=0)
            sums.append(jnp.sum(turned, axis=0, keepdims=True))
    return pltpu.roll(jnp.concatenate(sums, axis=0), 1, 1)


def products(keep_ref, query_ref, key_ref, value_ref, grad_ref):
    keep = keep_ref[...].astype(F32)
    joined = (key_ref[...].astype(F32) * value_ref[...].astype(F32)).astype(BF16)
    mixed = (grad_ref[...].astype(F32) * keep * query_ref[...].astype(F32)).astype(BF16)
    return joined, mixed


def local_kernel(per_group, keep_ref, query_ref, key_ref, value_ref, grad_ref, sums_ref):
    channels, length = query_ref.shape
    groups = channels // per_group
    joined, mixed = products(keep_ref, query_ref, key_ref, value_ref, grad_ref)
    sums_ref[:groups] = lag_sums(mixed, joined, per_group, lambda total: total >= length - 1)
    both = joined.astype(F32) * mixed.astype(F32)
    high = both.astype(BF16)
    low = (both - high.astype(F32)).astype(BF16)
    ones = jnp.ones((8, length), BF16)
    direct = lax.dot_general(ones, high, ROWS_BY_ROWS, preferred_element_type=F32)
    direct += lax.dot_general(ones, low, ROWS_BY_ROWS, preferred_element_type=F32)
    for block in range(channels // length):
        sums_ref[groups + block : groups + block + 1] = direct[
            :1, block * length : (block + 1) * length
        ]


def local_sums(keep, query, key, value, grad, groups):
    channels, length = query.shape
    return pl.pallas_call(
        functools.partial(local_kernel, channels // groups),
        out_shape=jax.ShapeDtypeStruct((groups + channels // length, length), F32),
        cost_estimate=pl.CostEstimate(flops=2**26, bytes_accessed=2**23, transcendentals=0),
        name="local_sums",
    )(keep, query, key, value, grad)


def cross_kernel(per_group, swap, own_ref, halo_ref, mine_ref, other_ref, sums_ref):
    groups = own_ref.shape[0] // per_group
    length = own_ref.shape[1]
    own, halo = own_ref[...], halo_ref[...]
    if swap:
        first = lax.axis_index("ctx") == 0
        own, halo = jnp.where(first, halo, own), jnp.where(first, own, halo)
    total = mine_ref[...] + other_ref[...]
    crossed = lag_sums(own, halo, per_group, lambda total: total < length - 1)
    sums_ref[:groups] = (total[:groups] + crossed).astype(sums_ref.dtype)
    sums_ref[groups:] = total[groups:].astype(sums_ref.dtype)


def cross_sums(own, halo, mine, other, groups, swap, dtype):
    return pl.pallas_call(
        functools.partial(cross_kernel, own.shape[0] // groups, swap),
        out_shape=jax.ShapeDtypeStruct(mine.shape, dtype),
        cost_estimate=pl.CostEstimate(flops=2**26, bytes_accessed=2**23, transcendentals=0),
        name="cross_sums",
    )(own, halo, mine, other)


def output_kernel(
    per_group, one_halo, keep_ref, tap_ref, skip_ref, query_ref, key_ref, value_ref, grad_ref,
    before_ref, following_ref, out_ref, query_grad_ref, key_grad_ref, value_grad_ref,
):
    channels, length = query_ref.shape
    row, column = iotas(length, length)
    causal = column >= row
    keep = keep_ref[...].astype(F32)
    skips = skip_ref[0].T
    nothing = jnp.zeros((), BF16)
    if one_halo:
        position = lax.axis_index("ctx")
    for group in range(channels // per_group):
        part = slice(group * per_group, (group + 1) * per_group)
        query = query_ref[part].astype(F32)
        key = key_ref[part].astype(F32)
        value = value_ref[part].astype(F32)
        scaled = grad_ref[part].astype(F32) * keep
        joined = (key * value).astype(BF16)
        mixed = (scaled * query).astype(BF16)
        before, following = before_ref[part], following_ref[part]
        if one_halo:
            before = jnp.where(position == 0, nothing, before)
            following = jnp.where(position == 0, following, nothing)
        taps = jnp.broadcast_to(tap_ref[group : group + 1], (length, length))
        circle = pltpu.roll(taps, 0, 1, stride=1, stride_axis=0)
        lower = jnp.where(causal, circle, 0.0).astype(BF16)
        upper = jnp.where(causal, 0.0, circle).astype(BF16)
        start = group * per_group
        skip = skips[start % length : start % length + per_group, start // length : start // length + 1]
        forward = jnp.dot(
            jnp.concatenate([before, joined], axis=1),
            jnp.concatenate([upper, lower], axis=0),
            preferred_element_type=F32,
        )
        forward += skip * joined.astype(F32)
        backward = lax.dot_general(
            jnp.concatenate([mixed, following], axis=1),
            jnp.concatenate([lower, upper], axis=1),
            ROWS_BY_ROWS,
            preferred_element_type=F32,
        )
        backward += skip * mixed.astype(F32)
        out_ref[part] = (query * forward).astype(BF16)
        query_grad_ref[part] = (scaled * forward).astype(BF16)
        key_grad_ref[part] = (backward * value).astype(BF16)
        value_grad_ref[part] = (backward * key).astype(BF16)


def outputs(keep, taps, skip, query, key, value, grad, before, following, one_halo):
    channels, length = query.shape
    groups = taps.shape[0]
    steps = 2
    large = pl.BlockSpec((channels // steps, length), lambda i: (i, 0))
    skip_rows = skip.reshape(steps, channels // length // steps, length)
    return pl.pallas_call(
        functools.partial(output_kernel, channels // groups, one_halo),
        grid=(steps,),
        in_specs=[
            pl.BlockSpec((1, length), lambda i: (0, 0)),
            pl.BlockSpec((groups // steps, length), lambda i: (i, 0)),
            pl.BlockSpec((1,) + skip_rows.shape[1:], lambda i: (i, 0, 0)),
        ]
        + [large] * 6,
        out_specs=[large] * 4,
        out_shape=[jax.ShapeDtypeStruct((channels, length), BF16)] * 4,
        cost_estimate=pl.CostEstimate(flops=2**28, bytes_accessed=2**24, transcendentals=0),
        name="outputs",
    )(keep, taps, skip_rows, query, key, value, grad, before, following)


def sum_over(sums, axis):
    size = lax.axis_size(axis)
    if size & (size - 1):
        return lax.psum(sums.astype(F32), axis)
    terms = [sums]
    for offset in range(1, size):
        terms.append(lax.ppermute(sums, axis, [(i, i ^ offset) for i in range(size)]))
    terms = [term.astype(F32) for term in terms]
    while len(terms) > 1:
        terms = [a + b for a, b in zip(terms[::2], terms[1::2])]
    return terms[0]


def body(query_act, key_act, value_act, out_grad, keep_mask, filter_taps, skip_gain):
    windows, channels, length = query_act.shape
    groups, tap_count = filter_taps.shape
    assert windows == 1 and length == tap_count
    shards = lax.axis_size("ctx")
    per_group = channels // groups
    positions = windows * lax.axis_size("dp") * length * shards
    tap_scale = 1.0 / math.sqrt(positions * per_group)
    skip_scale = 1.0 / math.sqrt(positions)
    query, key, value, grad = query_act[0], key_act[0], value_act[0], out_grad[0]
    joined = key.astype(F32) * value.astype(F32)
    mixed = grad.astype(F32) * keep_mask.astype(F32) * query.astype(F32)
    if shards == 2:
        swap = [(0, 1), (1, 0)]
        own = jnp.where(lax.axis_index("ctx") == 0, joined, mixed).astype(BF16)
        halo = lax.ppermute(own, "ctx", swap)
        mine = local_sums(keep_mask, query, key, value, grad, groups)
        other = lax.ppermute(mine, "ctx", swap)
        sums = cross_sums(own, halo, mine, other, groups, True, BF16)
        before = following = halo
    else:
        own = mixed.astype(BF16)
        before = lax.ppermute(joined.astype(BF16), "ctx", [(i, i + 1) for i in range(shards - 1)])
        following = lax.ppermute(own, "ctx", [(i + 1, i) for i in range(shards - 1)])
        mine = local_sums(keep_mask, query, key, value, grad, groups)
        sums = cross_sums(own, before, mine, jnp.zeros_like(mine), groups, False, F32)
        sums = lax.psum(sums, "ctx")
    reduced = sum_over(sums, "dp")
    results = outputs(
        keep_mask, filter_taps, skip_gain, query, key, value, grad, before, following, shards == 2
    )
    return (
        *(result[None] for result in results),
        reduced[:groups] * tap_scale,
        reduced[groups:].reshape(channels) * skip_scale,
    )


def solution(mesh):
    large = P("dp", "tp", "ctx")
    return jax.shard_map(
        body,
        mesh=mesh,
        in_specs=(large, large, large, large, P("dp", "ctx"), P("tp", None), P("tp")),
        out_specs=(large, large, large, large, P("tp", None), P("tp")),
        check_vma=False,
    )
```

time: 215 us -> 27.9 us (0.13)
  local copies, waits for them, and re-layouts: 97.8 us -> 1.98 us
  other arithmetic: 31.3 us -> 2.57 us
  blocking collectives: 28.2 us -> 0 us
  starting transfers between devices: 28.5 us -> 7.42 us
  waiting for transfers between devices: 20.6 us -> 4.15 us
  Pallas kernels: 0 us -> 10.8 us
  matrix products: 6.98 us -> 0 us
    gather x2 -> x0, local copies, waits for them, and re-layouts: 61.4 us -> none  [tap_matrices(): spread = tap_rows[:, jnp.mod(target - source, tap_len)]]
    all_to_all x8 -> x0, starting transfers between devices: 28.5 us -> none  [the longest x1 4.21 us: body(): lax.all_to_all(scaled_grad, 'ctx', split_axis=1, concat_axis=2, tiled=True)]
    all_to_all x8 -> x0, waiting for transfers between devices: 20.6 us -> none  [the longest x1 5.54 us: body(): lax.all_to_all(query_act, 'ctx', split_axis=1, concat_axis=2, tiled=True)]
    psum x1 -> x0, blocking collectives: 19.4 us -> none  [body(): replica = lax.psum((results[4], results[5]), 'dp')]
    unnamed x9 -> x0, other arithmetic: 19.2 us -> none
    unnamed x40 -> x10, local copies, waits for them, and re-layouts: 15.5 us -> 1.98 us
    pallas_call x0 -> x3, Pallas kernels: none -> 10.8 us  [the longest x1 4.2 us: outputs(): pl.pallas_call(functools.partial(output_kernel, channels // groups, one_h...]
    reshape x3 -> x0, local copies, waits for them, and re-layouts: 9.32 us -> none  [the longest x1 7.98 us: diagonal_sums(): skewed = flattened.reshape(groups, tap_len, double_len + 1)]
  transfers between devices with their start and end apart: 8 -> 5, of which waited for: 5 -> 1; matrix products, arithmetic and copies ran while one was open for 52% -> 0% of each run, Pallas kernels for 0% -> 27%
where the time goes in v1:
time: 27.9 us; the launch traced here: 27.7 us
  Pallas kernels  10.8 us (39%)
  starting transfers between devices  7.42 us (27%)
  waiting for transfers between devices  4.15 us (15%)
  other arithmetic  2.57 us (9%)
  local copies, waits for them, and re-layouts  1.98 us (7%)
  between operations  0.7 us (3%)
    ppermute x3, starting transfers between devices, sum_over(): lax.ppermute(sums, axis, [(i, i ^ offset) for i in range(size)])  4.39 us
    pallas_call x1, Pallas kernels, outputs(): pl.pallas_call(functools.partial(output_kernel, channels // groups, one_h...  4.2 us
    ppermute x1, waiting for transfers between devices, body(): other = lax.ppermute(mine, 'ctx', swap)  4.14 us
    pallas_call x1, Pallas kernels, local_sums(): pl.pallas_call(functools.partial(local_kernel, channels // groups), out_s...  3.42 us
    pallas_call x1, Pallas kernels, cross_sums(): pl.pallas_call(functools.partial(cross_kernel, own.shape[0] // groups, sw...  3.22 us
    ppermute x1, starting transfers between devices, body(): halo = lax.ppermute(own, 'ctx', swap)  3 us
    unnamed x10, local copies, waits for them, and re-layouts  1.98 us
    convert_element_type x1, other arithmetic, body(): own = jnp.where(lax.axis_index('ctx') == 0, joined, mixed).astype(BF16)  1.34 us
  transfers between devices with their start and end apart: 5, of which 1 were waited for; matrix products, arithmetic and copies ran while one was open for 0% of the time, Pallas kernels for 27%

profile of v1, /device:TPU:0, one launch (start us, length us, event | category | flops | bytes accessed | tf_op | source)
XLA Modules:
  0.0 27.7 jit_solution(3854844741683628734)
XLA Ops:
  0.6 0.0 copy-start.4
  0.6 0.6 %copy-done.4 = s32[1,128]{1,0:T(1,128)S(1)} copy-done((s32[1,128]{1,0:T(1,128)S(1)}, s32[1,128]{1,0:T(1,128)}, u32[]{:S(2)}) %copy-start.4) | copy-done | bytes 536
  1.3 1.3 %select_convert_fusion.own_ref = bf16[1024,128]{1,0:T(8,128)(2,1)S(1)} fusion(f32[128]{0:T(128)S(1)} %convert_bitcast_fusion, pred[]{:T(512)S(6)} %eq.3, bf16[1,1024,128]{2,1,0:T(8,128)(2,1)} %param.10, bf16[1,1024,128]{2,1,0:T(8,128)(2,1)} %param.9, bf16[1,1024,128]{2,1,0:T(8,128)(2,1)} %param.8, bf16[1,1024,128]{2,1,0:T(8,128)(2,1)} %param.7), kind=kLoop, calls=%fused_computation | loop fusion | flops 1179648 | bytes 1311233 | tf_op jit(solution)/shard_map/convert_element_type | solution.py:203
  2.6 0.0 copy-start.1
  2.7 3.0 %collective-permute-start = (bf16[1024,128]{1,0:T(8,128)(2,1)S(1)}, bf16[1024,128]{1,0:T(8,128)(2,1)S(1)}, u32[]{:S(2)}, u32[]{:S(2)}) collective-permute-start(bf16[1024,128]{1,0:T(8,128)(2,1)S(1)} %select_convert_fusion.own_ref), channel_id=1, source_target_pairs={{0,16},{16,0},{1,17},{17,1},{2,18},{18,2},{3,19},{19,3},{4,20},{20... | collective-permute-start | bytes 786440 | tf_op jit(solution)/shard_map/ppermute | solution.py:204
  5.7 3.4 %local_sums.1.mine_ref = f32[72,128]{1,0:T(8,128)} custom-call(s32[1,128]{1,0:T(1,128)} %keep_ref.3, bf16[1024,128]{1,0:T(8,128)(2,1)} %bitcast.17, bf16[1024,128]{1,0:T(8,128)(2,1)} %bitcast.19, bf16[1024,128]{1,0:T(8,128)(2,1)} %bitcast.21, bf16[1024,128]{1,0:T(8,128)(2,1)} %bitcast.23), custom_call_target="tpu_custom_call" | custom-call | flops 67108864 | bytes 8388608 | tf_op jit(solution)/shard_map/local_sums/pallas_call | solution.py:75
  9.1 0.0 copy-done.1
  9.1 0.0 collective-permute-start.1
  9.1 4.1 %collective-permute-done.1.other_ref = f32[72,128]{1,0:T(8,128)S(1)} collective-permute-done((f32[72,128]{1,0:T(8,128)}, f32[72,128]{1,0:T(8,128)S(1)}, u32[]{:S(2)}, u32[]{:S(2)}) %collective-permute-start.1) | collective-permute-done | bytes 36896 | tf_op jit(solution)/shard_map/ppermute | solution.py:206
  13.3 0.0 copy-start.3
  13.3 0.0 collective-permute-done.before_ref.following_ref.halo_ref
  13.3 0.6 %copy-done.3 = f32[72,128]{1,0:T(8,128)} copy-done((f32[72,128]{1,0:T(8,128)}, f32[72,128]{1,0:T(8,128)S(1)}, u32[]{:S(2)}) %copy-start.3) | copy-done | bytes 36888
  13.9 0.0 copy-start
  13.9 0.7 %copy-done = bf16[1024,128]{1,0:T(8,128)(2,1)} copy-done((bf16[1024,128]{1,0:T(8,128)(2,1)}, bf16[1024,128]{1,0:T(8,128)(2,1)S(1)}, u32[]{:S(2)}) %copy-start) | copy-done | bytes 262168
  14.6 3.2 %cross_sums.1 = bf16[72,128]{1,0:T(8,128)(2,1)} custom-call(bf16[1024,128]{1,0:T(8,128)(2,1)} %copy-done.1, bf16[1024,128]{1,0:T(8,128)(2,1)} %copy-done, f32[72,128]{1,0:T(8,128)} %local_sums.1.mine_ref, f32[72,128]{1,0:T(8,128)} %copy-done.3), custom_call_target="tpu_custom_call" | custom-call | flops 67108864 | bytes 8388608 | tf_op jit(solution)/shard_map/cross_sums/pallas_call | solution.py:97
  17.8 3.6 %collective-permute-start.4 = (bf16[72,128]{1,0:T(8,128)(2,1)}, bf16[72,128]{1,0:T(8,128)(2,1)S(1)}, u32[]{:S(2)}, u32[]{:S(2)}) collective-permute-start(bf16[72,128]{1,0:T(8,128)(2,1)} %cross_sums.1), channel_id=1, source_target_pairs={{0,12},{4,8},{8,4},{12,0},{1,13},{5,9},{9,5},{13,1},{2,14},{6,10},... | collective-permute-start | bytes 55304 | tf_op jit(solution)/shard_map/ppermute | solution.py:182
  21.4 0.0 collective-permute-start.3
  21.4 0.8 %collective-permute-start.2 = (bf16[72,128]{1,0:T(8,128)(2,1)}, bf16[72,128]{1,0:T(8,128)(2,1)S(1)}, u32[]{:S(2)}, u32[]{:S(2)}) collective-permute-start(bf16[72,128]{1,0:T(8,128)(2,1)} %cross_sums.1), channel_id=1, source_target_pairs={{0,4},{4,0},{8,12},{12,8},{1,5},{5,1},{9,13},{13,9},{2,6},{6,2},{1... | collective-permute-start | bytes 55304 | tf_op jit(solution)/shard_map/ppermute | solution.py:182
  22.2 0.0 copy-start.2
  22.2 4.2 %outputs.1 = (bf16[1024,128]{1,0:T(8,128)(2,1)}, bf16[1024,128]{1,0:T(8,128)(2,1)}, bf16[1024,128]{1,0:T(8,128)(2,1)}, bf16[1024,128]{1,0:T(8,128)(2,1)}) custom-call(s32[1,128]{1,0:T(1,128)} %keep_ref.3, f32[64,128]{1,0:T(8,128)} %tap_ref.1, f32[2,4,128]{2,1,0:T(4,128)} %bitcast.25, bf16[1024,128]{1,0:T(8,128)(2,1)} %bitcast.18, ...), custom_call_target="tpu_custom_call" | custom-call | flops 268435456 | bytes 16777216 | tf_op jit(solution)/shard_map/outputs/pallas_call | solution.py:160
  26.4 0.0 collective-permute-done.4
  26.4 0.0 collective-permute-done.3
  26.4 0.0 collective-permute-done.2
  26.4 0.0 copy-done.2
  26.5 0.6 %fusion = f32[1024]{0:T(1024)} fusion(f32[72,128]{1,0:T(8,128)S(1)} %add_add_fusion), kind=kLoop, calls=%fused_computation.4 | loop fusion | flops 1024 | bytes 8192 | tf_op jit(solution)/shard_map/mul | solution.py:223
  27.1 0.6 %slice_multiply_fusion = f32[64,128]{1,0:T(8,128)} fusion(f32[72,128]{1,0:T(8,128)S(1)} %add_add_fusion), kind=kLoop, calls=%fused_computation.2 | loop fusion | flops 8192 | bytes 65536 | tf_op jit(solution)/shard_map/mul | solution.py:222
  (2 shorter events, 0.0 us)
Async XLA Ops:
  0.6 0.7 %copy-start.4 = (s32[1,128]{1,0:T(1,128)S(1)}, s32[1,128]{1,0:T(1,128)}, u32[]{:S(2)}) copy-start(s32[1,128]{1,0:T(1,128)} %keep_ref.3) | copy-start | bytes 1540
  2.6 6.4 %copy-start.1 = (bf16[1024,128]{1,0:T(8,128)(2,1)}, bf16[1024,128]{1,0:T(8,128)(2,1)S(1)}, u32[]{:S(2)}) copy-start(bf16[1024,128]{1,0:T(8,128)(2,1)S(1)} %select_convert_fusion.own_ref) | copy-start | bytes 786436
  2.7 10.6 %collective-permute-start = (bf16[1024,128]{1,0:T(8,128)(2,1)S(1)}, bf16[1024,128]{1,0:T(8,128)(2,1)S(1)}, u32[]{:S(2)}, u32[]{:S(2)}) collective-permute-start(bf16[1024,128]{1,0:T(8,128)(2,1)S(1)} %select_convert_fusion.own_ref), channel_id=1, source_target_pairs={{0,16},{16,0},{1,17},{17,1},{2,18},{18,2},{3,19},{19,3},{4,20},{20... | collective-permute-start | bytes 786440 | tf_op jit(solution)/shard_map/ppermute | solution.py:204
  9.1 4.2 %collective-permute-start.1 = (f32[72,128]{1,0:T(8,128)}, f32[72,128]{1,0:T(8,128)S(1)}, u32[]{:S(2)}, u32[]{:S(2)}) collective-permute-start(f32[72,128]{1,0:T(8,128)} %local_sums.1.mine_ref), channel_id=1, source_target_pairs={{0,16},{16,0},{1,17},{17,1},{2,18},{18,2},{3,19},{19,3},{4,20},{20... | collective-permute-start | bytes 110600 | tf_op jit(solution)/shard_map/ppermute | solution.py:206
  13.3 0.6 %copy-start.3 = (f32[72,128]{1,0:T(8,128)}, f32[72,128]{1,0:T(8,128)S(1)}, u32[]{:S(2)}) copy-start(f32[72,128]{1,0:T(8,128)S(1)} %collective-permute-done.1.other_ref) | copy-start | bytes 110596
  13.9 0.7 %copy-start = (bf16[1024,128]{1,0:T(8,128)(2,1)}, bf16[1024,128]{1,0:T(8,128)(2,1)S(1)}, u32[]{:S(2)}) copy-start(bf16[1024,128]{1,0:T(8,128)(2,1)S(1)} %collective-permute-done.before_ref.following_ref.halo_ref) | copy-start | bytes 786436
  17.8 8.6 %collective-permute-start.4 = (bf16[72,128]{1,0:T(8,128)(2,1)}, bf16[72,128]{1,0:T(8,128)(2,1)S(1)}, u32[]{:S(2)}, u32[]{:S(2)}) collective-permute-start(bf16[72,128]{1,0:T(8,128)(2,1)} %cross_sums.1), channel_id=1, source_target_pairs={{0,12},{4,8},{8,4},{12,0},{1,13},{5,9},{9,5},{13,1},{2,14},{6,10},... | collective-permute-start | bytes 55304 | tf_op jit(solution)/shard_map/ppermute | solution.py:182
  21.4 5.0 %collective-permute-start.3 = (bf16[72,128]{1,0:T(8,128)(2,1)}, bf16[72,128]{1,0:T(8,128)(2,1)S(1)}, u32[]{:S(2)}, u32[]{:S(2)}) collective-permute-start(bf16[72,128]{1,0:T(8,128)(2,1)} %cross_sums.1), channel_id=1, source_target_pairs={{0,8},{4,12},{8,0},{12,4},{1,9},{5,13},{9,1},{13,5},{2,10},{6,14},... | collective-permute-start | bytes 55304 | tf_op jit(solution)/shard_map/ppermute | solution.py:182
  21.4 5.0 %collective-permute-start.2 = (bf16[72,128]{1,0:T(8,128)(2,1)}, bf16[72,128]{1,0:T(8,128)(2,1)S(1)}, u32[]{:S(2)}, u32[]{:S(2)}) collective-permute-start(bf16[72,128]{1,0:T(8,128)(2,1)} %cross_sums.1), channel_id=1, source_target_pairs={{0,4},{4,0},{8,12},{12,8},{1,5},{5,1},{9,13},{13,9},{2,6},{6,2},{1... | collective-permute-start | bytes 55304 | tf_op jit(solution)/shard_map/ppermute | solution.py:182
  22.2 4.2 %copy-start.2 = (bf16[72,128]{1,0:T(8,128)(2,1)S(1)}, bf16[72,128]{1,0:T(8,128)(2,1)}, u32[]{:S(2)}) copy-start(bf16[72,128]{1,0:T(8,128)(2,1)} %cross_sums.1) | copy-start | bytes 55300

commit v2 on v1

--- a/solution.py
+++ b/solution.py
@@ -27,23 +27,40 @@
     return jnp.dot(block, mirror, preferred_element_type=F32).astype(BF16)
 
 
-def lag_sums(grad, joined, per_group, wanted):
+def lag_sums(grad, joined, per_group, crossing):
     channels, length = grad.shape
     per = length // per_group
-    row, column = iotas(length, length)
-    kept = wanted(row + column)
+    phases = 4
+    span = length // phases
+    row, column = iotas(span, length)
+    near = row + column >= span - 1
+    lane = iotas(1, length)[1]
+    owner = iotas(1, phases * length)[1] % length // per_group
+    nothing = jnp.zeros((), BF16)
     mirrored = flip(joined)
-    nothing = jnp.zeros((per_group, length), BF16)
     sums = []
     for start in range(0, channels, length):
         across = grad[start : start + length].T
+        block = mirrored[start : start + length].astype(F32)
+        left, right = [], []
+        for phase in range(phases):
+            left.append(across[phase * span : (phase + 1) * span])
+            shift = span * (phase + 1)
+            turned = (block if shift == length else pltpu.roll(block, shift, 1)).astype(BF16)
+            if crossing:
+                earlier = jnp.where(lane >= shift, turned, nothing)
+                right.append(jnp.concatenate([earlier, turned], axis=1))
+            else:
+                right.append(jnp.where(lane < shift, turned, nothing))
+        left = jnp.concatenate(left, axis=1)
+        left = jnp.concatenate([jnp.where(owner == g, left, nothing) for g in range(per)], axis=0)
+        grams = jnp.dot(left, jnp.concatenate(right, axis=0), preferred_element_type=F32)
         for g in range(per):
-            mine = mirrored[start + g * per_group : start + (g + 1) * per_group]
-            spread = jnp.concatenate([nothing] * g + [mine] + [nothing] * (per - 1 - g), axis=0)
-            gram = jnp.where(kept, jnp.dot(across, spread, preferred_element_type=F32), 0.0)
+            gram = grams[g * span : (g + 1) * span]
+            gram = jnp.where(near, gram[:, :length], gram[:, length:] if crossing else 0.0)
             turned = pltpu.roll(gram, 0, 1, stride=1, stride_axis=0)
             sums.append(jnp.sum(turned, axis=0, keepdims=True))
-    return pltpu.roll(jnp.concatenate(sums, axis=0), 1, 1)
+    return pltpu.roll(jnp.concatenate(sums, axis=0), length - span + 1, 1)
 
 
 def products(keep_ref, query_ref, key_ref, value_ref, grad_ref):
@@ -53,11 +70,70 @@
     return joined, mixed
 
 
+def own_kernel(
+    keep_hbm, query_hbm, key_hbm, value_hbm, grad_hbm, own_ref, one_ref, two_ref, keep_ref, sems
+):
+    first = lax.axis_index("ctx") == 0
+    parts = 2
+    rows = own_ref.shape[0] // parts
+
+    def copies(source_one, source_two):
+        made = []
+        for part in range(parts):
+            window = pl.ds(part * rows, rows)
+            for side, (source, target) in enumerate(((source_one, one_ref), (source_two, two_ref))):
+                made.append(
+                    pltpu.make_async_copy(
+                        source.at[window], target.at[window], sems.at[2 * part + side]
+                    )
+                )
+        return made
+
+    keep_copy = pltpu.make_async_copy(keep_hbm, keep_ref, sems.at[2 * parts])
+
+    @pl.when(first)
+    def _():
+        for copy in copies(key_hbm, value_hbm):
+            copy.start()
+
+    @pl.when(jnp.logical_not(first))
+    def _():
+        for copy in copies(query_hbm, grad_hbm):
+            copy.start()
+
+    keep_copy.start()
+    keep_copy.wait()
+    keep = jnp.where(first, 1.0, keep_ref[...].astype(F32))
+    waits = copies(key_hbm, value_hbm)
+    for part in range(parts):
+        waits[2 * part].wait()
+        waits[2 * part + 1].wait()
+        window = pl.ds(part * rows, rows)
+        scaled = two_ref[window].astype(F32) * keep
+        own_ref[window] = (scaled * one_ref[window].astype(F32)).astype(BF16)
+
+
+def own_block(keep, query, key, value, grad):
+    return pl.pallas_call(
+        own_kernel,
+        in_specs=[pl.BlockSpec(memory_space=pl.ANY)] * 5,
+        out_specs=pl.BlockSpec(memory_space=pltpu.VMEM),
+        out_shape=pltpu.VMEM(query.shape, BF16),
+        scratch_shapes=[
+            pltpu.VMEM(query.shape, BF16),
+            pltpu.VMEM(query.shape, BF16),
+            pltpu.VMEM(keep.shape, keep.dtype),
+            pltpu.SemaphoreType.DMA((5,)),
+        ],
+        name="own_block",
+    )(keep, query, key, value, grad)
+
+
 def local_kernel(per_group, keep_ref, query_ref, key_ref, value_ref, grad_ref, sums_ref):
     channels, length = query_ref.shape
     groups = channels // per_group
     joined, mixed = products(keep_ref, query_ref, key_ref, value_ref, grad_ref)
-    sums_ref[:groups] = lag_sums(mixed, joined, per_group, lambda total: total >= length - 1)
+    sums_ref[:groups] = lag_sums(mixed, joined, per_group, False).astype(sums_ref.dtype)
     both = joined.astype(F32) * mixed.astype(F32)
     high = both.astype(BF16)
     low = (both - high.astype(F32)).astype(BF16)
@@ -67,39 +143,43 @@
     for block in range(channels // length):
         sums_ref[groups + block : groups + block + 1] = direct[
             :1, block * length : (block + 1) * length
-        ]
-
-
-def local_sums(keep, query, key, value, grad, groups):
+        ].astype(sums_ref.dtype)
+
+
+def local_sums(keep, query, key, value, grad, groups, dtype):
     channels, length = query.shape
     return pl.pallas_call(
         functools.partial(local_kernel, channels // groups),
-        out_shape=jax.ShapeDtypeStruct((groups + channels // length, length), F32),
+        out_specs=pl.BlockSpec(memory_space=pltpu.VMEM),
+        out_shape=pltpu.VMEM((groups + channels // length, length), dtype),
         cost_estimate=pl.CostEstimate(flops=2**26, bytes_accessed=2**23, transcendentals=0),
         name="local_sums",
     )(keep, query, key, value, grad)
 
 
-def cross_kernel(per_group, swap, own_ref, halo_ref, mine_ref, other_ref, sums_ref):
-    groups = own_ref.shape[0] // per_group
-    length = own_ref.shape[1]
+def cross_kernel(per_group, swap, own_ref, halo_ref, sums_ref):
     own, halo = own_ref[...], halo_ref[...]
     if swap:
         first = lax.axis_index("ctx") == 0
         own, halo = jnp.where(first, halo, own), jnp.where(first, own, halo)
-    total = mine_ref[...] + other_ref[...]
-    crossed = lag_sums(own, halo, per_group, lambda total: total < length - 1)
-    sums_ref[:groups] = (total[:groups] + crossed).astype(sums_ref.dtype)
-    sums_ref[groups:] = total[groups:].astype(sums_ref.dtype)
-
-
-def cross_sums(own, halo, mine, other, groups, swap, dtype):
-    return pl.pallas_call(
-        functools.partial(cross_kernel, own.shape[0] // groups, swap),
-        out_shape=jax.ShapeDtypeStruct(mine.shape, dtype),
+    sums_ref[...] = lag_sums(own, halo, per_group, True)
+
+
+def in_vmem(array):
+    return pltpu.with_memory_space_constraint(array, pltpu.VMEM)
+
+
+def cross_sums(own, halo, groups, swap):
+    channels, length = own.shape
+    whole = pl.BlockSpec(memory_space=pltpu.VMEM)
+    return pl.pallas_call(
+        functools.partial(cross_kernel, channels // groups, swap),
+        in_specs=[whole] * 2,
+        out_specs=whole,
+        out_shape=pltpu.VMEM((groups, length), F32),
         cost_estimate=pl.CostEstimate(flops=2**26, bytes_accessed=2**23, transcendentals=0),
         name="cross_sums",
-    )(own, halo, mine, other)
+    )(in_vmem(own), in_vmem(halo))
 
 
 def output_kernel(
@@ -173,17 +253,36 @@
     )(keep, taps, skip_rows, query, key, value, grad, before, following)
 
 
-def sum_over(sums, axis):
+def gather_terms(sums, axis):
     size = lax.axis_size(axis)
     if size & (size - 1):
-        return lax.psum(sums.astype(F32), axis)
-    terms = [sums]
-    for offset in range(1, size):
-        terms.append(lax.ppermute(sums, axis, [(i, i ^ offset) for i in range(size)]))
-    terms = [term.astype(F32) for term in terms]
+        return [lax.psum(sums, axis)]
+    taken = {0: sums}
+    for offset in reversed(range(1, size)):
+        taken[offset] = lax.ppermute(sums, axis, [(i, i ^ offset) for i in range(size)])
+    return [taken[offset] for offset in range(size)]
+
+
+def total_kernel(groups, tap_scale, skip_scale, *refs):
+    *term_refs, tap_ref, skip_ref = refs
+    terms = [ref[...].astype(F32) for ref in term_refs]
     while len(terms) > 1:
         terms = [a + b for a, b in zip(terms[::2], terms[1::2])]
-    return terms[0]
+    tap_ref[...] = terms[0][:groups] * tap_scale
+    skip_ref[...] = terms[0][groups:] * skip_scale
+
+
+def totals(terms, groups, tap_scale, skip_scale):
+    rows, length = terms[0].shape
+    return pl.pallas_call(
+        functools.partial(total_kernel, groups, tap_scale, skip_scale),
+        in_specs=[pl.BlockSpec(memory_space=pltpu.VMEM)] * len(terms),
+        out_shape=[
+            jax.ShapeDtypeStruct((groups, length), F32),
+            jax.ShapeDtypeStruct((rows - groups, length), F32),
+        ],
+        name="totals",
+    )(*(in_vmem(term) for term in terms))
 
 
 def body(query_act, key_act, value_act, out_grad, keep_mask, filter_taps, skip_gain):
@@ -196,32 +295,30 @@
     tap_scale = 1.0 / math.sqrt(positions * per_group)
     skip_scale = 1.0 / math.sqrt(positions)
     query, key, value, grad = query_act[0], key_act[0], value_act[0], out_grad[0]
-    joined = key.astype(F32) * value.astype(F32)
-    mixed = grad.astype(F32) * keep_mask.astype(F32) * query.astype(F32)
     if shards == 2:
         swap = [(0, 1), (1, 0)]
-        own = jnp.where(lax.axis_index("ctx") == 0, joined, mixed).astype(BF16)
+        own = own_block(keep_mask, query, key, value, grad)
         halo = lax.ppermute(own, "ctx", swap)
-        mine = local_sums(keep_mask, query, key, value, grad, groups)
+        mine = local_sums(keep_mask, query, key, value, grad, groups, BF16)
         other = lax.ppermute(mine, "ctx", swap)
-        sums = cross_sums(own, halo, mine, other, groups, True, BF16)
+        crossed = cross_sums(own, halo, groups, True)
+        sums = mine.astype(F32).at[:groups].add(crossed) + other.astype(F32)
+        sums = lax.reduce_precision(sums, 8, 7).astype(BF16)
         before = following = halo
     else:
-        own = mixed.astype(BF16)
-        before = lax.ppermute(joined.astype(BF16), "ctx", [(i, i + 1) for i in range(shards - 1)])
+        joined = (key.astype(F32) * value.astype(F32)).astype(BF16)
+        own = (grad.astype(F32) * keep_mask.astype(F32) * query.astype(F32)).astype(BF16)
+        before = lax.ppermute(joined, "ctx", [(i, i + 1) for i in range(shards - 1)])
         following = lax.ppermute(own, "ctx", [(i + 1, i) for i in range(shards - 1)])
-        mine = local_sums(keep_mask, query, key, value, grad, groups)
-        sums = cross_sums(own, before, mine, jnp.zeros_like(mine), groups, False, F32)
-        sums = lax.psum(sums, "ctx")
-    reduced = sum_over(sums, "dp")
+        mine = local_sums(keep_mask, query, key, value, grad, groups, F32)
+        crossed = cross_sums(own, before, groups, False)
+        sums = lax.psum(mine.at[:groups].add(crossed), "ctx")
+    terms = gather_terms(sums, "dp")
     results = outputs(
         keep_mask, filter_taps, skip_gain, query, key, value, grad, before, following, shards == 2
     )
-    return (
-        *(result[None] for result in results),
-        reduced[:groups] * tap_scale,
-        reduced[groups:].reshape(channels) * skip_scale,
-    )
+    filter_grad, skip_grad = totals(terms, groups, tap_scale, skip_scale)
+    return (*(result[None] for result in results), filter_grad, skip_grad.reshape(channels))
 
 
 def solution(mesh):

time: 27.9 us -> 22.1 us (0.79)
  other arithmetic: 2.57 us -> 0.02 us
  local copies, waits for them, and re-layouts: 1.98 us -> 0.01 us
  Pallas kernels: 10.8 us -> 9.46 us
    ppermute x1, waiting for transfers between devices: 4.14 us -> 0.01 us  [body(): other = lax.ppermute(mine, 'ctx', swap)]
    ppermute x1, waiting for transfers between devices: 0.01 us -> 4.11 us  [body(): halo = lax.ppermute(own, 'ctx', swap)]
    unnamed x10 -> x2, local copies, waits for them, and re-layouts: 1.98 us -> 0.01 us
    convert_element_type x1 -> x2, other arithmetic: 1.34 us -> 0.01 us  [the longest x1 0.01 us: body(): sums = lax.reduce_precision(sums, 8, 7).astype(BF16)]
    mul x3 -> x0, other arithmetic: 1.22 us -> none  [the longest x1 0.62 us: body(): reduced[:groups] * tap_scale]
    pallas_call x1, Pallas kernels: 3.42 us -> 2.33 us  [local_sums(): pl.pallas_call(functools.partial(local_kernel, channels // groups), out_s...]
    pallas_call x1 -> x3, Pallas kernels: 3.22 us -> 2.93 us  [the longest x1 1.19 us: own_block(): pl.pallas_call(own_kernel, in_specs=[pl.BlockSpec(memory_space=pl.ANY)] *...]
  transfers between devices with their start and end apart: 5 -> 5, of which waited for: 1 -> 1; matrix products, arithmetic and copies ran while one was open for 0% -> 0% of each run, Pallas kernels for 27% -> 35%
where the time goes in v2:
time: 22.1 us; the launch traced here: 21.9 us
  Pallas kernels  9.46 us (43%)
  starting transfers between devices  7.61 us (34%)
  waiting for transfers between devices  4.12 us (19%)
  between operations  0.7 us (3%)
    ppermute x3, starting transfers between devices, gather_terms(): lax.ppermute(sums, axis, [(i, i ^ offset) for i in range(size)])  4.55 us
    pallas_call x1, Pallas kernels, outputs(): pl.pallas_call(functools.partial(output_kernel, channels // groups, one_h...  4.2 us
    ppermute x1, waiting for transfers between devices, body(): halo = lax.ppermute(own, 'ctx', swap)  4.11 us
    ppermute x1, starting transfers between devices, body(): halo = lax.ppermute(own, 'ctx', swap)  3.01 us
    pallas_call x1, Pallas kernels, local_sums(): pl.pallas_call(functools.partial(local_kernel, channels // groups), out_s...  2.33 us
    pallas_call x1, Pallas kernels, own_block(): pl.pallas_call(own_kernel, in_specs=[pl.BlockSpec(memory_space=pl.ANY)] *...  1.19 us
    pallas_call x1, Pallas kernels, cross_sums(): pl.pallas_call(functools.partial(cross_kernel, channels // groups, swap),...  1.11 us
    pallas_call x1, Pallas kernels, totals(): pl.pallas_call(functools.partial(total_kernel, groups, tap_scale, skip_sc...  0.63 us
  transfers between devices with their start and end apart: 5, of which 1 were waited for; matrix products, arithmetic and copies ran while one was open for 0% of the time, Pallas kernels for 35%

profile of v2, /device:TPU:0, one launch (start us, length us, event | category | flops | bytes accessed | tf_op | source)
XLA Modules:
  0.0 21.9 jit_solution(16691449870624134398)
XLA Ops:
  0.6 1.2 %own_block.1.own_ref = bf16[1024,128]{1,0:T(8,128)(2,1)S(1)} custom-call(s32[1,128]{1,0:T(1,128)} %keep_ref.3, bf16[1024,128]{1,0:T(8,128)(2,1)} %bitcast.10, bf16[1024,128]{1,0:T(8,128)(2,1)} %bitcast.13, bf16[1024,128]{1,0:T(8,128)(2,1)} %bitcast.16, bf16[1024,128]{1,0:T(8,128)(2,1)} %bitcast.19), custom_call_target="tpu_custom_call" | custom-call | tf_op jit(solution)/shard_map/own_block/pallas_call | solution.py:117
  1.8 3.0 %collective-permute-start = (bf16[1024,128]{1,0:T(8,128)(2,1)S(1)}, bf16[1024,128]{1,0:T(8,128)(2,1)S(1)}, u32[]{:S(2)}, u32[]{:S(2)}) collective-permute-start(bf16[1024,128]{1,0:T(8,128)(2,1)S(1)} %own_block.1.own_ref), channel_id=1, source_target_pairs={{0,16},{16,0},{1,17},{17,1},{2,18},{18,2},{3,19},{19,3},{4,20},{20... | collective-permute-start | bytes 786440 | tf_op jit(solution)/shard_map/ppermute | solution.py:301
  4.8 2.3 %local_sums.1 = bf16[72,128]{1,0:T(8,128)(2,1)S(1)} custom-call(s32[1,128]{1,0:T(1,128)} %keep_ref.3, bf16[1024,128]{1,0:T(8,128)(2,1)} %bitcast.11, bf16[1024,128]{1,0:T(8,128)(2,1)} %bitcast.14, bf16[1024,128]{1,0:T(8,128)(2,1)} %bitcast.17, bf16[1024,128]{1,0:T(8,128)(2,1)} %bitcast.20), custom_call_target="tpu_custom_call" | custom-call | flops 67108864 | bytes 8388608 | tf_op jit(solution)/shard_map/local_sums/pallas_call | solution.py:151
  7.2 0.1 collective-permute-start.1
  7.2 4.1 %collective-permute-done.before_ref.following_ref.halo_ref = bf16[1024,128]{1,0:T(8,128)(2,1)S(1)} collective-permute-done((bf16[1024,128]{1,0:T(8,128)(2,1)S(1)}, bf16[1024,128]{1,0:T(8,128)(2,1)S(1)}, u32[]{:S(2)}, u32[]{:S(2)}) %collective-permute-start) | collective-permute-done | bytes 262176 | tf_op jit(solution)/shard_map/ppermute | solution.py:301
  11.3 0.0 copy-start
  11.3 1.1 %cross_sums.1 = f32[64,128]{1,0:T(8,128)S(1)} custom-call(bf16[1024,128]{1,0:T(8,128)(2,1)S(1)} %own_block.1.own_ref, bf16[1024,128]{1,0:T(8,128)(2,1)S(1)} %collective-permute-done.before_ref.following_ref.halo_ref), custom_call_target="tpu_custom_call" | custom-call | flops 67108864 | bytes 8388608 | tf_op jit(solution)/shard_map/cross_sums/pallas_call | solution.py:175
  12.4 0.0 copy-done
  12.5 0.0 collective-permute-done.1
  12.5 3.9 %collective-permute-start.4 = (bf16[72,128]{1,0:T(8,128)(2,1)S(1)}, bf16[72,128]{1,0:T(8,128)(2,1)S(1)}, u32[]{:S(2)}, u32[]{:S(2)}) collective-permute-start(bf16[72,128]{1,0:T(8,128)(2,1)S(1)} %reduce-precision_convert_fusion.refs_0_), channel_id=1, source_target_pairs={{0,12},{4,8},{8,4},{12,0},{1,13},{5,9},{9,5},{13,1},{2,14},{6,10},... | collective-permute-start | bytes 55304 | tf_op jit(solution)/shard_map/ppermute | solution.py:262
  16.4 0.0 collective-permute-start.3
  16.4 0.6 %collective-permute-start.2 = (bf16[72,128]{1,0:T(8,128)(2,1)S(1)}, bf16[72,128]{1,0:T(8,128)(2,1)S(1)}, u32[]{:S(2)}, u32[]{:S(2)}) collective-permute-start(bf16[72,128]{1,0:T(8,128)(2,1)S(1)} %reduce-precision_convert_fusion.refs_0_), channel_id=1, source_target_pairs={{0,4},{4,0},{8,12},{12,8},{1,5},{5,1},{9,13},{13,9},{2,6},{6,2},{1... | collective-permute-start | bytes 55304 | tf_op jit(solution)/shard_map/ppermute | solution.py:262
  17.0 4.2 %outputs.1 = (bf16[1024,128]{1,0:T(8,128)(2,1)}, bf16[1024,128]{1,0:T(8,128)(2,1)}, bf16[1024,128]{1,0:T(8,128)(2,1)}, bf16[1024,128]{1,0:T(8,128)(2,1)}) custom-call(s32[1,128]{1,0:T(1,128)} %keep_ref.3, f32[64,128]{1,0:T(8,128)} %tap_ref.1, f32[2,4,128]{2,1,0:T(4,128)} %bitcast.22, bf16[1024,128]{1,0:T(8,128)(2,1)} %bitcast.12, ...), custom_call_target="tpu_custom_call" | custom-call | flops 268435456 | bytes 16777216 | tf_op jit(solution)/shard_map/outputs/pallas_call | solution.py:240
  21.2 0.0 collective-permute-done.4.refs_3_
  21.3 0.0 collective-permute-done.3.refs_2_
  21.3 0.0 collective-permute-done.2.refs_1_
  21.3 0.6 %totals.1 = (f32[64,128]{1,0:T(8,128)}, f32[8,128]{1,0:T(8,128)}) custom-call(bf16[72,128]{1,0:T(8,128)(2,1)S(1)} %reduce-precision_convert_fusion.refs_0_, bf16[72,128]{1,0:T(8,128)(2,1)S(1)} %collective-permute-done.2.refs_1_, bf16[72,128]{1,0:T(8,128)(2,1)S(1)} %collective-permute-done.3.refs_2_, bf16[72,128]{1,0:T(8,128)(2,1)S(1)} %collective-permute-done.4.refs_3_), custom_call_target="tpu_custom_call" | custom-call | tf_op jit(solution)/shard_map/totals/pallas_call | solution.py:277
  (3 shorter events, 0.0 us)
Async XLA Ops:
  1.8 9.5 %collective-permute-start = (bf16[1024,128]{1,0:T(8,128)(2,1)S(1)}, bf16[1024,128]{1,0:T(8,128)(2,1)S(1)}, u32[]{:S(2)}, u32[]{:S(2)}) collective-permute-start(bf16[1024,128]{1,0:T(8,128)(2,1)S(1)} %own_block.1.own_ref), channel_id=1, source_target_pairs={{0,16},{16,0},{1,17},{17,1},{2,18},{18,2},{3,19},{19,3},{4,20},{20... | collective-permute-start | bytes 786440 | tf_op jit(solution)/shard_map/ppermute | solution.py:301
  7.2 5.3 %collective-permute-start.1 = (bf16[72,128]{1,0:T(8,128)(2,1)S(1)}, bf16[72,128]{1,0:T(8,128)(2,1)S(1)}, u32[]{:S(2)}, u32[]{:S(2)}) collective-permute-start(bf16[72,128]{1,0:T(8,128)(2,1)S(1)} %local_sums.1), channel_id=1, source_target_pairs={{0,16},{16,0},{1,17},{17,1},{2,18},{18,2},{3,19},{19,3},{4,20},{20... | collective-permute-start | bytes 55304 | tf_op jit(solution)/shard_map/ppermute | solution.py:303
  11.3 1.1 %copy-start = (bf16[1024,128]{1,0:T(8,128)(2,1)}, bf16[1024,128]{1,0:T(8,128)(2,1)S(1)}, u32[]{:S(2)}) copy-start(bf16[1024,128]{1,0:T(8,128)(2,1)S(1)} %collective-permute-done.before_ref.following_ref.halo_ref) | copy-start | bytes 786436
  12.5 8.8 %collective-permute-start.4 = (bf16[72,128]{1,0:T(8,128)(2,1)S(1)}, bf16[72,128]{1,0:T(8,128)(2,1)S(1)}, u32[]{:S(2)}, u32[]{:S(2)}) collective-permute-start(bf16[72,128]{1,0:T(8,128)(2,1)S(1)} %reduce-precision_convert_fusion.refs_0_), channel_id=1, source_target_pairs={{0,12},{4,8},{8,4},{12,0},{1,13},{5,9},{9,5},{13,1},{2,14},{6,10},... | collective-permute-start | bytes 55304 | tf_op jit(solution)/shard_map/ppermute | solution.py:262
  16.4 4.9 %collective-permute-start.3 = (bf16[72,128]{1,0:T(8,128)(2,1)S(1)}, bf16[72,128]{1,0:T(8,128)(2,1)S(1)}, u32[]{:S(2)}, u32[]{:S(2)}) collective-permute-start(bf16[72,128]{1,0:T(8,128)(2,1)S(1)} %reduce-precision_convert_fusion.refs_0_), channel_id=1, source_target_pairs={{0,8},{4,12},{8,0},{12,4},{1,9},{5,13},{9,1},{13,5},{2,10},{6,14},... | collective-permute-start | bytes 55304 | tf_op jit(solution)/shard_map/ppermute | solution.py:262
  16.4 4.9 %collective-permute-start.2 = (bf16[72,128]{1,0:T(8,128)(2,1)S(1)}, bf16[72,128]{1,0:T(8,128)(2,1)S(1)}, u32[]{:S(2)}, u32[]{:S(2)}) collective-permute-start(bf16[72,128]{1,0:T(8,128)(2,1)S(1)} %reduce-precision_convert_fusion.refs_0_), channel_id=1, source_target_pairs={{0,4},{4,0},{8,12},{12,8},{1,5},{5,1},{9,13},{13,9},{2,6},{6,2},{1... | collective-permute-start | bytes 55304 | tf_op jit(solution)/shard_map/ppermute | solution.py:262

commit v3 on v2

--- a/solution.py
+++ b/solution.py
@@ -11,6 +11,14 @@
 BF16 = jnp.bfloat16
 F32 = jnp.float32
 ROWS_BY_ROWS = (((1,), (1,)), ((), ()))
+
+
+def in_hbm(array):
+    return pltpu.with_memory_space_constraint(array, pltpu.HBM)
+
+
+def in_vmem(array):
+    return pltpu.with_memory_space_constraint(array, pltpu.VMEM)
 
 
 def iotas(rows, columns):
@@ -63,13 +71,6 @@
     return pltpu.roll(jnp.concatenate(sums, axis=0), length - span + 1, 1)
 
 
-def products(keep_ref, query_ref, key_ref, value_ref, grad_ref):
-    keep = keep_ref[...].astype(F32)
-    joined = (key_ref[...].astype(F32) * value_ref[...].astype(F32)).astype(BF16)
-    mixed = (grad_ref[...].astype(F32) * keep * query_ref[...].astype(F32)).astype(BF16)
-    return joined, mixed
-
-
 def own_kernel(
     keep_hbm, query_hbm, key_hbm, value_hbm, grad_hbm, own_ref, one_ref, two_ref, keep_ref, sems
 ):
@@ -116,7 +117,7 @@
 def own_block(keep, query, key, value, grad):
     return pl.pallas_call(
         own_kernel,
-        in_specs=[pl.BlockSpec(memory_space=pl.ANY)] * 5,
+        in_specs=[pl.BlockSpec(memory_space=pltpu.HBM)] * 5,
         out_specs=pl.BlockSpec(memory_space=pltpu.VMEM),
         out_shape=pltpu.VMEM(query.shape, BF16),
         scratch_shapes=[
@@ -125,14 +126,27 @@
             pltpu.VMEM(keep.shape, keep.dtype),
             pltpu.SemaphoreType.DMA((5,)),
         ],
+        compiler_params=pltpu.CompilerParams(vmem_limit_bytes=12 * 2**20),
         name="own_block",
-    )(keep, query, key, value, grad)
-
-
-def local_kernel(per_group, keep_ref, query_ref, key_ref, value_ref, grad_ref, sums_ref):
+    )(*map(in_hbm, (keep, query, key, value, grad)))
+
+
+def local_kernel(per_group, *refs):
+    sources, sums_ref, (*held, sems) = refs[:5], refs[5], refs[6:]
+    copies = [
+        pltpu.make_async_copy(source, target, sems.at[index])
+        for index, (source, target) in enumerate(zip(sources, held))
+    ]
+    for copy in copies:
+        copy.start()
+    for copy in copies:
+        copy.wait()
+    keep_ref, query_ref, key_ref, value_ref, grad_ref = held
     channels, length = query_ref.shape
     groups = channels // per_group
-    joined, mixed = products(keep_ref, query_ref, key_ref, value_ref, grad_ref)
+    joined = (key_ref[...].astype(F32) * value_ref[...].astype(F32)).astype(BF16)
+    scaled = grad_ref[...].astype(F32) * keep_ref[...].astype(F32)
+    mixed = (scaled * query_ref[...].astype(F32)).astype(BF16)
     sums_ref[:groups] = lag_sums(mixed, joined, per_group, False).astype(sums_ref.dtype)
     both = joined.astype(F32) * mixed.astype(F32)
     high = both.astype(BF16)
@@ -148,13 +162,18 @@
 
 def local_sums(keep, query, key, value, grad, groups, dtype):
     channels, length = query.shape
+    sources = (keep, query, key, value, grad)
     return pl.pallas_call(
         functools.partial(local_kernel, channels // groups),
-        out_specs=pl.BlockSpec(memory_space=pltpu.VMEM),
-        out_shape=pltpu.VMEM((groups + channels // length, length), dtype),
+        in_specs=[pl.BlockSpec(memory_space=pltpu.HBM)] * 5,
+        out_specs=[pl.BlockSpec(memory_space=pltpu.VMEM)] * 6,
+        out_shape=[pltpu.VMEM((groups + channels // length, length), dtype)]
+        + [pltpu.VMEM(source.shape, source.dtype) for source in sources],
+        scratch_shapes=[pltpu.SemaphoreType.DMA((5,))],
         cost_estimate=pl.CostEstimate(flops=2**26, bytes_accessed=2**23, transcendentals=0),
+        compiler_params=pltpu.CompilerParams(vmem_limit_bytes=12 * 2**20),
         name="local_sums",
-    )(keep, query, key, value, grad)
+    )(*map(in_hbm, sources))
 
 
 def cross_kernel(per_group, swap, own_ref, halo_ref, sums_ref):
@@ -165,10 +184,6 @@
     sums_ref[...] = lag_sums(own, halo, per_group, True)
 
 
-def in_vmem(array):
-    return pltpu.with_memory_space_constraint(array, pltpu.VMEM)
-
-
 def cross_sums(own, halo, groups, swap):
     channels, length = own.shape
     whole = pl.BlockSpec(memory_space=pltpu.VMEM)
@@ -178,12 +193,13 @@
         out_specs=whole,
         out_shape=pltpu.VMEM((groups, length), F32),
         cost_estimate=pl.CostEstimate(flops=2**26, bytes_accessed=2**23, transcendentals=0),
+        compiler_params=pltpu.CompilerParams(vmem_limit_bytes=12 * 2**20),
         name="cross_sums",
     )(in_vmem(own), in_vmem(halo))
 
 
 def output_kernel(
-    per_group, one_halo, keep_ref, tap_ref, skip_ref, query_ref, key_ref, value_ref, grad_ref,
+    per_group, keep_ref, tap_ref, skip_ref, query_ref, key_ref, value_ref, grad_ref,
     before_ref, following_ref, out_ref, query_grad_ref, key_grad_ref, value_grad_ref,
 ):
     channels, length = query_ref.shape
@@ -191,9 +207,6 @@
     causal = column >= row
     keep = keep_ref[...].astype(F32)
     skips = skip_ref[0].T
-    nothing = jnp.zeros((), BF16)
-    if one_halo:
-        position = lax.axis_index("ctx")
     for group in range(channels // per_group):
         part = slice(group * per_group, (group + 1) * per_group)
         query = query_ref[part].astype(F32)
@@ -203,9 +216,6 @@
         joined = (key * value).astype(BF16)
         mixed = (scaled * query).astype(BF16)
         before, following = before_ref[part], following_ref[part]
-        if one_halo:
-            before = jnp.where(position == 0, nothing, before)
-            following = jnp.where(position == 0, following, nothing)
         taps = jnp.broadcast_to(tap_ref[group : group + 1], (length, length))
         circle = pltpu.roll(taps, 0, 1, stride=1, stride_axis=0)
         lower = jnp.where(causal, circle, 0.0).astype(BF16)
@@ -231,14 +241,14 @@
         value_grad_ref[part] = (backward * key).astype(BF16)
 
 
-def outputs(keep, taps, skip, query, key, value, grad, before, following, one_halo):
+def outputs(keep, taps, skip, query, key, value, grad, before, following):
     channels, length = query.shape
     groups = taps.shape[0]
     steps = 2
     large = pl.BlockSpec((channels // steps, length), lambda i: (i, 0))
     skip_rows = skip.reshape(steps, channels // length // steps, length)
     return pl.pallas_call(
-        functools.partial(output_kernel, channels // groups, one_halo),
+        functools.partial(output_kernel, channels // groups),
         grid=(steps,),
         in_specs=[
             pl.BlockSpec((1, length), lambda i: (0, 0)),
@@ -249,8 +259,156 @@
         out_specs=[large] * 4,
         out_shape=[jax.ShapeDtypeStruct((channels, length), BF16)] * 4,
         cost_estimate=pl.CostEstimate(flops=2**28, bytes_accessed=2**24, transcendentals=0),
+        compiler_params=pltpu.CompilerParams(vmem_limit_bytes=12 * 2**20),
         name="outputs",
     )(keep, taps, skip_rows, query, key, value, grad, before, following)
+
+
+def row_copies(parts, part, made_refs, out_refs, sems):
+    rows = made_refs[0].shape[0] // parts
+    window = pl.ds(part * rows, rows)
+    return [
+        pltpu.make_async_copy(made.at[window], out.at[window], sems.at[2 * part + side])
+        for side, (made, out) in enumerate(zip(made_refs, out_refs))
+    ]
+
+
+def early_kernel(
+    per_group, parts, keep_ref, tap_ref, skip_ref, query_ref, key_ref, value_ref, grad_ref,
+    out_ref, query_grad_ref, key_grad_ref, value_grad_ref, rest_ref, one_ref, two_ref, upper_ref,
+    made_one_ref, made_two_ref, sems,
+):
+    channels, length = query_ref.shape
+    groups = channels // per_group
+    row, column = iotas(length, length)
+    causal = column >= row
+    keep = keep_ref[...].astype(F32)
+    skips = skip_ref[...].T
+    first = lax.axis_index("ctx") == 0
+    made_refs = (made_one_ref, made_two_ref)
+
+    def send(part, *refs):
+        for copy in row_copies(parts, part, made_refs, refs, sems):
+            copy.start()
+
+    for group in range(groups):
+        part = slice(group * per_group, (group + 1) * per_group)
+        query = query_ref[part].astype(F32)
+        key = key_ref[part].astype(F32)
+        value = value_ref[part].astype(F32)
+        scaled = grad_ref[part].astype(F32) * keep
+        joined = (key * value).astype(BF16)
+        mixed = (scaled * query).astype(BF16)
+        taps = jnp.broadcast_to(tap_ref[group : group + 1], (length, length))
+        circle = pltpu.roll(taps, 0, 1, stride=1, stride_axis=0)
+        lower = jnp.where(causal, circle, 0.0).astype(BF16)
+        upper_ref[group] = jnp.where(causal, 0.0, circle).astype(BF16)
+        start = group * per_group
+        skip = skips[start % length : start % length + per_group, start // length : start // length + 1]
+        forward = jnp.dot(joined, lower, preferred_element_type=F32)
+        forward += skip * joined.astype(F32)
+        backward = lax.dot_general(mixed, lower, ROWS_BY_ROWS, preferred_element_type=F32)
+        backward += skip * mixed.astype(F32)
+        done = jnp.where(first, forward, backward)
+        made_one_ref[part] = (done * jnp.where(first, query, value)).astype(BF16)
+        made_two_ref[part] = (done * jnp.where(first, scaled, key)).astype(BF16)
+        rest_ref[part] = jnp.where(first, backward, forward)
+        one_ref[part] = jnp.where(first, value, query).astype(BF16)
+        two_ref[part] = jnp.where(first, key, scaled).astype(BF16)
+        if (group + 1) % (groups // parts) == 0:
+            part = group // (groups // parts)
+            pl.when(first)(functools.partial(send, part, out_ref, query_grad_ref))
+            pl.when(jnp.logical_not(first))(
+                functools.partial(send, part, key_grad_ref, value_grad_ref)
+            )
+    for part in range(parts):
+        for copy in row_copies(parts, part, made_refs, (out_ref, query_grad_ref), sems):
+            copy.wait()
+
+
+def early_outputs(keep, taps, skip, query, key, value, grad):
+    channels, length = query.shape
+    groups = taps.shape[0]
+    parts = 2
+    whole = pl.BlockSpec(memory_space=pltpu.VMEM)
+    return pl.pallas_call(
+        functools.partial(early_kernel, channels // groups, parts),
+        in_specs=[whole] * 7,
+        out_specs=[pl.BlockSpec(memory_space=pltpu.HBM)] * 4 + [whole] * 4,
+        out_shape=[jax.ShapeDtypeStruct((channels, length), BF16)] * 4
+        + [
+            pltpu.VMEM((channels, length), F32),
+            pltpu.VMEM((channels, length), BF16),
+            pltpu.VMEM((channels, length), BF16),
+            pltpu.VMEM((groups, length, length), BF16),
+        ],
+        scratch_shapes=[
+            pltpu.VMEM((channels, length), BF16),
+            pltpu.VMEM((channels, length), BF16),
+            pltpu.SemaphoreType.DMA((2 * parts,)),
+        ],
+        cost_estimate=pl.CostEstimate(flops=2**28, bytes_accessed=2**23, transcendentals=0),
+        compiler_params=pltpu.CompilerParams(vmem_limit_bytes=12 * 2**20),
+        name="early_outputs",
+    )(in_vmem(keep), taps, skip.reshape(channels // length, length), *map(in_vmem, (query, key, value, grad)))
+
+
+def late_kernel(
+    per_group, parts, halo_ref, rest_ref, one_ref, two_ref, upper_ref, _out, _query_grad, _key_grad,
+    _value_grad, out_ref, query_grad_ref, key_grad_ref, value_grad_ref, made_one_ref, made_two_ref, sems,
+):
+    groups = halo_ref.shape[0] // per_group
+    first = lax.axis_index("ctx") == 0
+    made_refs = (made_one_ref, made_two_ref)
+
+    def run(transposed, *out_refs):
+        for group in range(groups):
+            part = slice(group * per_group, (group + 1) * per_group)
+            halo, upper = halo_ref[part], upper_ref[group]
+            if transposed:
+                crossed = lax.dot_general(halo, upper, ROWS_BY_ROWS, preferred_element_type=F32)
+            else:
+                crossed = jnp.dot(halo, upper, preferred_element_type=F32)
+            total = rest_ref[part] + crossed
+            made_one_ref[part] = (total * one_ref[part].astype(F32)).astype(BF16)
+            made_two_ref[part] = (total * two_ref[part].astype(F32)).astype(BF16)
+            if (group + 1) % (groups // parts) == 0:
+                part = group // (groups // parts)
+                for copy in row_copies(parts, part, made_refs, out_refs, sems):
+                    copy.start()
+        for part in range(parts):
+            for copy in row_copies(parts, part, made_refs, out_refs, sems):
+                copy.wait()
+
+    @pl.when(first)
+    def _():
+        run(True, key_grad_ref, value_grad_ref)
+
+    @pl.when(jnp.logical_not(first))
+    def _():
+        run(False, out_ref, query_grad_ref)
+
+
+def late_outputs(halo, rest, one, two, upper, *results):
+    channels, length = halo.shape
+    groups = upper.shape[0]
+    parts = 2
+    whole = pl.BlockSpec(memory_space=pltpu.VMEM)
+    return pl.pallas_call(
+        functools.partial(late_kernel, channels // groups, parts),
+        in_specs=[whole] * 5 + [pl.BlockSpec(memory_space=pltpu.HBM)] * 4,
+        out_specs=[pl.BlockSpec(memory_space=pltpu.HBM)] * 4,
+        out_shape=[jax.ShapeDtypeStruct((channels, length), BF16)] * 4,
+        input_output_aliases={5: 0, 6: 1, 7: 2, 8: 3},
+        scratch_shapes=[
+            pltpu.VMEM((channels, length), BF16),
+            pltpu.VMEM((channels, length), BF16),
+            pltpu.SemaphoreType.DMA((2 * parts,)),
+        ],
+        cost_estimate=pl.CostEstimate(flops=2**28, bytes_accessed=2**23, transcendentals=0),
+        compiler_params=pltpu.CompilerParams(vmem_limit_bytes=12 * 2**20),
+        name="late_outputs",
+    )(in_vmem(halo), in_vmem(rest), in_vmem(one), in_vmem(two), in_vmem(upper), *results)
 
 
 def gather_terms(sums, axis):
@@ -281,6 +439,7 @@
             jax.ShapeDtypeStruct((groups, length), F32),
             jax.ShapeDtypeStruct((rows - groups, length), F32),
         ],
+        compiler_params=pltpu.CompilerParams(vmem_limit_bytes=12 * 2**20),
         name="totals",
     )(*(in_vmem(term) for term in terms))
 
@@ -299,24 +458,24 @@
         swap = [(0, 1), (1, 0)]
         own = own_block(keep_mask, query, key, value, grad)
         halo = lax.ppermute(own, "ctx", swap)
-        mine = local_sums(keep_mask, query, key, value, grad, groups, BF16)
+        mine, *near = local_sums(keep_mask, query, key, value, grad, groups, BF16)
         other = lax.ppermute(mine, "ctx", swap)
         crossed = cross_sums(own, halo, groups, True)
         sums = mine.astype(F32).at[:groups].add(crossed) + other.astype(F32)
         sums = lax.reduce_precision(sums, 8, 7).astype(BF16)
-        before = following = halo
+        early = early_outputs(near[0], filter_taps, skip_gain, *near[1:])
+        terms = gather_terms(sums, "dp")
+        results = late_outputs(halo, *early[4:], *early[:4])
     else:
         joined = (key.astype(F32) * value.astype(F32)).astype(BF16)
         own = (grad.astype(F32) * keep_mask.astype(F32) * query.astype(F32)).astype(BF16)
         before = lax.ppermute(joined, "ctx", [(i, i + 1) for i in range(shards - 1)])
         following = lax.ppermute(own, "ctx", [(i + 1, i) for i in range(shards - 1)])
-        mine = local_sums(keep_mask, query, key, value, grad, groups, F32)
+        mine, *_ = local_sums(keep_mask, query, key, value, grad, groups, F32)
         crossed = cross_sums(own, before, groups, False)
         sums = lax.psum(mine.at[:groups].add(crossed), "ctx")
-    terms = gather_terms(sums, "dp")
-    results = outputs(
-        keep_mask, filter_taps, skip_gain, query, key, value, grad, before, following, shards == 2
-    )
+        terms = gather_terms(sums, "dp")
+        results = outputs(keep_mask, filter_taps, skip_gain, query, key, value, grad, before, following)
     filter_grad, skip_grad = totals(terms, groups, tap_scale, skip_scale)
     return (*(result[None] for result in results), filter_grad, skip_grad.reshape(channels))
 

time: 22.1 us -> 21.9 us (level)
  waiting for transfers between devices: 4.12 us -> 3.34 us
  Pallas kernels: 9.46 us -> 9.96 us
    ppermute x1, waiting for transfers between devices: 4.11 us -> 1.27 us  [body(): halo = lax.ppermute(own, 'ctx', swap)]
    ppermute x3, waiting for transfers between devices: 0.01 us -> 2.06 us  [gather_terms(): lax.ppermute(sums, axis, [(i, i ^ offset) for i in range(size)])]
    pallas_call x3 -> x4, Pallas kernels: 7.72 us -> 8.23 us  [the longest x1 2.72 us: early_outputs(): pl.pallas_call(functools.partial(early_kernel, channels // groups, parts)...]
  transfers between devices with their start and end apart: 5 -> 5, of which waited for: 1 -> 2; matrix products, arithmetic and copies ran while one was open for 0% -> 0% of each run, Pallas kernels for 35% -> 38%
where the time goes in v3:
time: 21.9 us; the launch traced here: 21.7 us
  Pallas kernels  9.96 us (45%)
  starting transfers between devices  7.65 us (35%)
  waiting for transfers between devices  3.34 us (15%)
  between operations  0.72 us (3%)
    ppermute x3, starting transfers between devices, gather_terms(): lax.ppermute(sums, axis, [(i, i ^ offset) for i in range(size)])  4.56 us
    ppermute x1, starting transfers between devices, body(): halo = lax.ppermute(own, 'ctx', swap)  3.01 us
    pallas_call x1, Pallas kernels, early_outputs(): pl.pallas_call(functools.partial(early_kernel, channels // groups, parts)...  2.72 us
    pallas_call x1, Pallas kernels, local_sums(): pl.pallas_call(functools.partial(local_kernel, channels // groups), in_sp...  2.38 us
    ppermute x3, waiting for transfers between devices, gather_terms(): lax.ppermute(sums, axis, [(i, i ^ offset) for i in range(size)])  2.06 us
    pallas_call x1, Pallas kernels, late_outputs(): pl.pallas_call(functools.partial(late_kernel, channels // groups, parts),...  1.94 us
    ppermute x1, waiting for transfers between devices, body(): halo = lax.ppermute(own, 'ctx', swap)  1.27 us
    pallas_call x1, Pallas kernels, own_block(): pl.pallas_call(own_kernel, in_specs=[pl.BlockSpec(memory_space=pltpu.HBM)...  1.19 us
  transfers between devices with their start and end apart: 5, of which 2 were waited for; matrix products, arithmetic and copies ran while one was open for 0% of the time, Pallas kernels for 38%

profile of v3, /device:TPU:0, one launch (start us, length us, event | category | flops | bytes accessed | tf_op | source)
XLA Modules:
  0.0 21.7 jit_solution(4555427708610960680)
XLA Ops:
  0.6 0.0 copy-start.1
  0.6 0.0 copy-start
  0.7 1.2 %own_block.1.own_ref = bf16[1024,128]{1,0:T(8,128)(2,1)S(1)} custom-call(s32[1,128]{1,0:T(1,128)} %refs_0_.1, bf16[1024,128]{1,0:T(8,128)(2,1)} %bitcast.11, bf16[1024,128]{1,0:T(8,128)(2,1)} %bitcast.13, bf16[1024,128]{1,0:T(8,128)(2,1)} %bitcast.15, bf16[1024,128]{1,0:T(8,128)(2,1)} %bitcast.17), custom_call_target="tpu_custom_call" | custom-call | tf_op jit(solution)/shard_map/own_block/pallas_call | solution.py:118
  1.9 3.0 %collective-permute-start = (bf16[1024,128]{1,0:T(8,128)(2,1)S(1)}, bf16[1024,128]{1,0:T(8,128)(2,1)S(1)}, u32[]{:S(2)}, u32[]{:S(2)}) collective-permute-start(bf16[1024,128]{1,0:T(8,128)(2,1)S(1)} %own_block.1.own_ref), channel_id=1, source_target_pairs={{0,16},{16,0},{1,17},{17,1},{2,18},{18,2},{3,19},{19,3},{4,20},{20... | collective-permute-start | bytes 786440 | tf_op jit(solution)/shard_map/ppermute | solution.py:460
  4.9 2.4 %local_sums.1 = (bf16[72,128]{1,0:T(8,128)(2,1)S(1)}, s32[1,128]{1,0:T(1,128)S(1)}, bf16[1024,128]{1,0:T(8,128)(2,1)S(1)}, bf16[1024,128]{1,0:T(8,128)(2,1)S(1)}...) custom-call(s32[1,128]{1,0:T(1,128)} %refs_0_.1, bf16[1024,128]{1,0:T(8,128)(2,1)} %bitcast.12, ...), custom_call_target="tpu_custom_call" | custom-call | flops 67108864 | bytes 8388608 | tf_op jit(solution)/shard_map/local_sums/pallas_call | solution.py:166
  7.2 0.1 collective-permute-start.1
  7.3 0.0 copy-done.1
  7.3 0.0 copy-done
  7.4 2.7 %early_outputs.1 = (bf16[1024,128]{1,0:T(8,128)(2,1)}, bf16[1024,128]{1,0:T(8,128)(2,1)}, bf16[1024,128]{1,0:T(8,128)(2,1)}, bf16[1024,128]{1,0:T(8,128)(2,1)}, ...) custom-call(s32[1,128]{1,0:T(1,128)S(1)} %get-tuple-element.38.keep_, ...), custom_call_target="tpu_custom_call" | custom-call | flops 268435456 | bytes 8388608 | tf_op jit(solution)/shard_map/early_outputs/pallas_call | solution.py:334
  10.1 1.3 %collective-permute-done.halo_ref = bf16[1024,128]{1,0:T(8,128)(2,1)S(1)} collective-permute-done((bf16[1024,128]{1,0:T(8,128)(2,1)S(1)}, bf16[1024,128]{1,0:T(8,128)(2,1)S(1)}, u32[]{:S(2)}, u32[]{:S(2)}) %collective-permute-start) | collective-permute-done | bytes 262176 | tf_op jit(solution)/shard_map/ppermute | solution.py:460
  11.4 1.1 %cross_sums.1 = f32[64,128]{1,0:T(8,128)S(1)} custom-call(bf16[1024,128]{1,0:T(8,128)(2,1)S(1)} %own_block.1.own_ref, bf16[1024,128]{1,0:T(8,128)(2,1)S(1)} %collective-permute-done.halo_ref), custom_call_target="tpu_custom_call" | custom-call | flops 67108864 | bytes 8388608 | tf_op jit(solution)/shard_map/cross_sums/pallas_call | solution.py:190
  12.5 0.0 collective-permute-done.1
  12.5 3.9 %collective-permute-start.4 = (bf16[72,128]{1,0:T(8,128)(2,1)S(1)}, bf16[72,128]{1,0:T(8,128)(2,1)S(1)}, u32[]{:S(2)}, u32[]{:S(2)}) collective-permute-start(bf16[72,128]{1,0:T(8,128)(2,1)S(1)} %reduce-precision_convert_fusion.refs_0_), channel_id=1, source_target_pairs={{0,12},{4,8},{8,4},{12,0},{1,13},{5,9},{9,5},{13,1},{2,14},{6,10},... | collective-permute-start | bytes 55304 | tf_op jit(solution)/shard_map/ppermute | solution.py:420
  16.4 0.0 collective-permute-start.3
  16.4 0.6 %collective-permute-start.2 = (bf16[72,128]{1,0:T(8,128)(2,1)S(1)}, bf16[72,128]{1,0:T(8,128)(2,1)S(1)}, u32[]{:S(2)}, u32[]{:S(2)}) collective-permute-start(bf16[72,128]{1,0:T(8,128)(2,1)S(1)} %reduce-precision_convert_fusion.refs_0_), channel_id=1, source_target_pairs={{0,4},{4,0},{8,12},{12,8},{1,5},{5,1},{9,13},{13,9},{2,6},{6,2},{1... | collective-permute-start | bytes 55304 | tf_op jit(solution)/shard_map/ppermute | solution.py:420
  17.1 1.9 %late_outputs.1 = (bf16[1024,128]{1,0:T(8,128)(2,1)}, bf16[1024,128]{1,0:T(8,128)(2,1)}, bf16[1024,128]{1,0:T(8,128)(2,1)}, bf16[1024,128]{1,0:T(8,128)(2,1)}) custom-call(bf16[1024,128]{1,0:T(8,128)(2,1)S(1)} %collective-permute-done.halo_ref, ...), custom_call_target="tpu_custom_call", output_to_operand_aliasing={{0}: (5, {}), {1}: (6, {}), {2}: (7, {}), {3}: (8, {})} | custom-call | flops 268435456 | bytes 8388608 | tf_op jit(solution)/shard_map/late_outputs/pallas_call | solution.py:397
  19.0 0.0 collective-permute-done.4.refs_3_
  19.0 2.1 %collective-permute-done.3.refs_2_ = bf16[72,128]{1,0:T(8,128)(2,1)S(1)} collective-permute-done((bf16[72,128]{1,0:T(8,128)(2,1)S(1)}, bf16[72,128]{1,0:T(8,128)(2,1)S(1)}, u32[]{:S(2)}, u32[]{:S(2)}) %collective-permute-start.3) | collective-permute-done | bytes 18464 | tf_op jit(solution)/shard_map/ppermute | solution.py:420
  21.1 0.0 collective-permute-done.2.refs_1_
  21.1 0.6 %totals.1 = (f32[64,128]{1,0:T(8,128)}, f32[8,128]{1,0:T(8,128)}) custom-call(bf16[72,128]{1,0:T(8,128)(2,1)S(1)} %reduce-precision_convert_fusion.refs_0_, bf16[72,128]{1,0:T(8,128)(2,1)S(1)} %collective-permute-done.2.refs_1_, bf16[72,128]{1,0:T(8,128)(2,1)S(1)} %collective-permute-done.3.refs_2_, bf16[72,128]{1,0:T(8,128)(2,1)S(1)} %collective-permute-done.4.refs_3_), custom_call_target="tpu_custom_call" | custom-call | tf_op jit(solution)/shard_map/totals/pallas_call | solution.py:435
  (3 shorter events, 0.0 us)
Async XLA Ops:
  0.6 6.7 %copy-start.1 = (f32[1024]{0:T(1024)S(1)}, f32[1024]{0:T(1024)}, u32[]{:S(2)}) copy-start(f32[1024]{0:T(1024)} %param.15) | copy-start | bytes 12292
  0.6 6.7 %copy-start = (f32[64,128]{1,0:T(8,128)S(1)}, f32[64,128]{1,0:T(8,128)}, u32[]{:S(2)}) copy-start(f32[64,128]{1,0:T(8,128)} %tap_ref.1) | copy-start | bytes 98308
  1.9 9.5 %collective-permute-start = (bf16[1024,128]{1,0:T(8,128)(2,1)S(1)}, bf16[1024,128]{1,0:T(8,128)(2,1)S(1)}, u32[]{:S(2)}, u32[]{:S(2)}) collective-permute-start(bf16[1024,128]{1,0:T(8,128)(2,1)S(1)} %own_block.1.own_ref), channel_id=1, source_target_pairs={{0,16},{16,0},{1,17},{17,1},{2,18},{18,2},{3,19},{19,3},{4,20},{20... | collective-permute-start | bytes 786440 | tf_op jit(solution)/shard_map/ppermute | solution.py:460
  7.2 5.2 %collective-permute-start.1 = (bf16[72,128]{1,0:T(8,128)(2,1)S(1)}, bf16[72,128]{1,0:T(8,128)(2,1)S(1)}, u32[]{:S(2)}, u32[]{:S(2)}) collective-permute-start(bf16[72,128]{1,0:T(8,128)(2,1)S(1)} %get-tuple-element.55), channel_id=1, source_target_pairs={{0,16},{16,0},{1,17},{17,1},{2,18},{18,2},{3,19},{19,3},{4,20},{20... | collective-permute-start | bytes 55304 | tf_op jit(solution)/shard_map/ppermute | solution.py:462
  12.5 6.5 %collective-permute-start.4 = (bf16[72,128]{1,0:T(8,128)(2,1)S(1)}, bf16[72,128]{1,0:T(8,128)(2,1)S(1)}, u32[]{:S(2)}, u32[]{:S(2)}) collective-permute-start(bf16[72,128]{1,0:T(8,128)(2,1)S(1)} %reduce-precision_convert_fusion.refs_0_), channel_id=1, source_target_pairs={{0,12},{4,8},{8,4},{12,0},{1,13},{5,9},{9,5},{13,1},{2,14},{6,10},... | collective-permute-start | bytes 55304 | tf_op jit(solution)/shard_map/ppermute | solution.py:420
  16.4 4.7 %collective-permute-start.3 = (bf16[72,128]{1,0:T(8,128)(2,1)S(1)}, bf16[72,128]{1,0:T(8,128)(2,1)S(1)}, u32[]{:S(2)}, u32[]{:S(2)}) collective-permute-start(bf16[72,128]{1,0:T(8,128)(2,1)S(1)} %reduce-precision_convert_fusion.refs_0_), channel_id=1, source_target_pairs={{0,8},{4,12},{8,0},{12,4},{1,9},{5,13},{9,1},{13,5},{2,10},{6,14},... | collective-permute-start | bytes 55304 | tf_op jit(solution)/shard_map/ppermute | solution.py:420
  16.4 4.7 %collective-permute-start.2 = (bf16[72,128]{1,0:T(8,128)(2,1)S(1)}, bf16[72,128]{1,0:T(8,128)(2,1)S(1)}, u32[]{:S(2)}, u32[]{:S(2)}) collective-permute-start(bf16[72,128]{1,0:T(8,128)(2,1)S(1)} %reduce-precision_convert_fusion.refs_0_), channel_id=1, source_target_pairs={{0,4},{4,0},{8,12},{12,8},{1,5},{5,1},{9,13},{13,9},{2,6},{6,2},{1... | collective-permute-start | bytes 55304 | tf_op jit(solution)/shard_map/ppermute | solution.py:420

commit v4 on v3

--- a/solution.py
+++ b/solution.py
@@ -411,29 +411,41 @@
     )(in_vmem(halo), in_vmem(rest), in_vmem(one), in_vmem(two), in_vmem(upper), *results)
 
 
+def exchanges(size):
+    if size == 4:
+        return [(2, 3, 1, 0), (3, 2, 0, 1), (1, 0, 3, 2)]
+    return [tuple((i + step) % size for i in range(size)) for step in range(1, size)]
+
+
 def gather_terms(sums, axis):
+    return [sums] + [
+        lax.ppermute(sums, axis, list(enumerate(targets)))
+        for targets in exchanges(lax.axis_size(axis))
+    ]
+
+
+def total_kernel(groups, tap_scale, skip_scale, axis, order, *refs):
+    *term_refs, tap_ref, skip_ref = refs
+    taken = [term_refs[order.index(place)][...].astype(F32) for place in range(len(term_refs))]
     size = lax.axis_size(axis)
-    if size & (size - 1):
-        return [lax.psum(sums, axis)]
-    taken = {0: sums}
-    for offset in reversed(range(1, size)):
-        taken[offset] = lax.ppermute(sums, axis, [(i, i ^ offset) for i in range(size)])
-    return [taken[offset] for offset in range(size)]
-
-
-def total_kernel(groups, tap_scale, skip_scale, *refs):
-    *term_refs, tap_ref, skip_ref = refs
-    terms = [ref[...].astype(F32) for ref in term_refs]
-    while len(terms) > 1:
-        terms = [a + b for a, b in zip(terms[::2], terms[1::2])]
-    tap_ref[...] = terms[0][:groups] * tap_scale
-    skip_ref[...] = terms[0][groups:] * skip_scale
-
-
-def totals(terms, groups, tap_scale, skip_scale):
+    here = lax.axis_index(axis)
+    terms = [taken[0]] * size
+    for received, targets in zip(taken[1:], exchanges(size)):
+        for source, target in enumerate(targets):
+            if source != target:
+                terms[source] = jnp.where(here == target, received, terms[source])
+    total = terms[0]
+    for term in terms[1:]:
+        total = total + term
+    tap_ref[...] = total[:groups] * tap_scale
+    skip_ref[...] = total[groups:] * skip_scale
+
+
+def totals(terms, groups, tap_scale, skip_scale, axis):
     rows, length = terms[0].shape
-    return pl.pallas_call(
-        functools.partial(total_kernel, groups, tap_scale, skip_scale),
+    order = list(reversed(range(len(terms))))
+    return pl.pallas_call(
+        functools.partial(total_kernel, groups, tap_scale, skip_scale, axis, order),
         in_specs=[pl.BlockSpec(memory_space=pltpu.VMEM)] * len(terms),
         out_shape=[
             jax.ShapeDtypeStruct((groups, length), F32),
@@ -441,7 +453,7 @@
         ],
         compiler_params=pltpu.CompilerParams(vmem_limit_bytes=12 * 2**20),
         name="totals",
-    )(*(in_vmem(term) for term in terms))
+    )(*(in_vmem(terms[place]) for place in order))
 
 
 def body(query_act, key_act, value_act, out_grad, keep_mask, filter_taps, skip_gain):
@@ -476,7 +488,7 @@
         sums = lax.psum(mine.at[:groups].add(crossed), "ctx")
         terms = gather_terms(sums, "dp")
         results = outputs(keep_mask, filter_taps, skip_gain, query, key, value, grad, before, following)
-    filter_grad, skip_grad = totals(terms, groups, tap_scale, skip_scale)
+    filter_grad, skip_grad = totals(terms, groups, tap_scale, skip_scale, "dp")
     return (*(result[None] for result in results), filter_grad, skip_grad.reshape(channels))
 
 

time: 21.9 us -> 21 us (0.959)
  waiting for transfers between devices: 3.34 us -> 2.6 us
    ppermute x3, waiting for transfers between devices: 2.06 us -> 1.32 us  [gather_terms(): lax.ppermute(sums, axis, list(enumerate(targets)))]
  transfers between devices with their start and end apart: 5 -> 5, of which waited for: 2 -> 3; matrix products, arithmetic and copies ran while one was open for 0% -> 0% of each run, Pallas kernels for 38% -> 39%
where the time goes in v4:
time: 21 us; the launch traced here: 20.9 us
  Pallas kernels  9.98 us (48%)
  starting transfers between devices  7.56 us (36%)
  waiting for transfers between devices  2.6 us (12%)
  between operations  0.72 us (3%)
    ppermute x3, starting transfers between devices, gather_terms(): lax.ppermute(sums, axis, list(enumerate(targets)))  4.47 us
    ppermute x1, starting transfers between devices, body(): halo = lax.ppermute(own, 'ctx', swap)  3.01 us
    pallas_call x1, Pallas kernels, early_outputs(): pl.pallas_call(functools.partial(early_kernel, channels // groups, parts)...  2.72 us
    pallas_call x1, Pallas kernels, local_sums(): pl.pallas_call(functools.partial(local_kernel, channels // groups), in_sp...  2.38 us
    pallas_call x1, Pallas kernels, late_outputs(): pl.pallas_call(functools.partial(late_kernel, channels // groups, parts),...  1.94 us
    ppermute x3, waiting for transfers between devices, gather_terms(): lax.ppermute(sums, axis, list(enumerate(targets)))  1.32 us
    ppermute x1, waiting for transfers between devices, body(): halo = lax.ppermute(own, 'ctx', swap)  1.27 us
    pallas_call x1, Pallas kernels, own_block(): pl.pallas_call(own_kernel, in_specs=[pl.BlockSpec(memory_space=pltpu.HBM)...  1.19 us
  transfers between devices with their start and end apart: 5, of which 3 were waited for; matrix products, arithmetic and copies ran while one was open for 0% of the time, Pallas kernels for 39%

profile of v4, /device:TPU:0, one launch (start us, length us, event | category | flops | bytes accessed | tf_op | source)
XLA Modules:
  0.0 20.9 jit_solution(10236022976388994018)
XLA Ops:
  0.6 0.0 copy-start.1
  0.6 0.0 copy-start
  0.7 1.2 %own_block.1.own_ref = bf16[1024,128]{1,0:T(8,128)(2,1)S(1)} custom-call(s32[1,128]{1,0:T(1,128)} %refs_0_.1, bf16[1024,128]{1,0:T(8,128)(2,1)} %bitcast.11, bf16[1024,128]{1,0:T(8,128)(2,1)} %bitcast.13, bf16[1024,128]{1,0:T(8,128)(2,1)} %bitcast.15, bf16[1024,128]{1,0:T(8,128)(2,1)} %bitcast.17), custom_call_target="tpu_custom_call" | custom-call | tf_op jit(solution)/shard_map/own_block/pallas_call | solution.py:118
  1.9 3.0 %collective-permute-start = (bf16[1024,128]{1,0:T(8,128)(2,1)S(1)}, bf16[1024,128]{1,0:T(8,128)(2,1)S(1)}, u32[]{:S(2)}, u32[]{:S(2)}) collective-permute-start(bf16[1024,128]{1,0:T(8,128)(2,1)S(1)} %own_block.1.own_ref), channel_id=1, source_target_pairs={{0,16},{16,0},{1,17},{17,1},{2,18},{18,2},{3,19},{19,3},{4,20},{20... | collective-permute-start | bytes 786440 | tf_op jit(solution)/shard_map/ppermute | solution.py:472
  4.9 2.4 %local_sums.1 = (bf16[72,128]{1,0:T(8,128)(2,1)S(1)}, s32[1,128]{1,0:T(1,128)S(1)}, bf16[1024,128]{1,0:T(8,128)(2,1)S(1)}, bf16[1024,128]{1,0:T(8,128)(2,1)S(1)}...) custom-call(s32[1,128]{1,0:T(1,128)} %refs_0_.1, bf16[1024,128]{1,0:T(8,128)(2,1)} %bitcast.12, ...), custom_call_target="tpu_custom_call" | custom-call | flops 67108864 | bytes 8388608 | tf_op jit(solution)/shard_map/local_sums/pallas_call | solution.py:166
  7.2 0.1 collective-permute-start.1
  7.3 0.0 copy-done.1
  7.3 0.0 copy-done
  7.4 2.7 %early_outputs.1 = (bf16[1024,128]{1,0:T(8,128)(2,1)}, bf16[1024,128]{1,0:T(8,128)(2,1)}, bf16[1024,128]{1,0:T(8,128)(2,1)}, bf16[1024,128]{1,0:T(8,128)(2,1)}, ...) custom-call(s32[1,128]{1,0:T(1,128)S(1)} %get-tuple-element.38.keep_, ...), custom_call_target="tpu_custom_call" | custom-call | flops 268435456 | bytes 8388608 | tf_op jit(solution)/shard_map/early_outputs/pallas_call | solution.py:334
  10.1 1.3 %collective-permute-done.halo_ref = bf16[1024,128]{1,0:T(8,128)(2,1)S(1)} collective-permute-done((bf16[1024,128]{1,0:T(8,128)(2,1)S(1)}, bf16[1024,128]{1,0:T(8,128)(2,1)S(1)}, u32[]{:S(2)}, u32[]{:S(2)}) %collective-permute-start) | collective-permute-done | bytes 262176 | tf_op jit(solution)/shard_map/ppermute | solution.py:472
  11.4 1.1 %cross_sums.1 = f32[64,128]{1,0:T(8,128)S(1)} custom-call(bf16[1024,128]{1,0:T(8,128)(2,1)S(1)} %own_block.1.own_ref, bf16[1024,128]{1,0:T(8,128)(2,1)S(1)} %collective-permute-done.halo_ref), custom_call_target="tpu_custom_call" | custom-call | flops 67108864 | bytes 8388608 | tf_op jit(solution)/shard_map/cross_sums/pallas_call | solution.py:190
  12.5 0.0 collective-permute-done.1
  12.5 2.9 %collective-permute-start.4 = (bf16[72,128]{1,0:T(8,128)(2,1)S(1)}, bf16[72,128]{1,0:T(8,128)(2,1)S(1)}, u32[]{:S(2)}, u32[]{:S(2)}) collective-permute-start(bf16[72,128]{1,0:T(8,128)(2,1)S(1)} %reduce-precision_convert_fusion.refs_3_), channel_id=1, source_target_pairs={{0,8},{4,12},{8,4},{12,0},{1,9},{5,13},{9,5},{13,1},{2,10},{6,14},... | collective-permute-start | bytes 55304 | tf_op jit(solution)/shard_map/ppermute | solution.py:422
  15.4 1.1 %collective-permute-start.3 = (bf16[72,128]{1,0:T(8,128)(2,1)S(1)}, bf16[72,128]{1,0:T(8,128)(2,1)S(1)}, u32[]{:S(2)}, u32[]{:S(2)}) collective-permute-start(bf16[72,128]{1,0:T(8,128)(2,1)S(1)} %reduce-precision_convert_fusion.refs_3_), channel_id=1, source_target_pairs={{0,12},{4,8},{8,0},{12,4},{1,13},{5,9},{9,1},{13,5},{2,14},{6,10},... | collective-permute-start | bytes 55304 | tf_op jit(solution)/shard_map/ppermute | solution.py:422
  16.5 0.5 %collective-permute-start.2 = (bf16[72,128]{1,0:T(8,128)(2,1)S(1)}, bf16[72,128]{1,0:T(8,128)(2,1)S(1)}, u32[]{:S(2)}, u32[]{:S(2)}) collective-permute-start(bf16[72,128]{1,0:T(8,128)(2,1)S(1)} %reduce-precision_convert_fusion.refs_3_), channel_id=1, source_target_pairs={{0,4},{4,0},{8,12},{12,8},{1,5},{5,1},{9,13},{13,9},{2,6},{6,2},{1... | collective-permute-start | bytes 55304 | tf_op jit(solution)/shard_map/ppermute | solution.py:422
  17.0 1.9 %late_outputs.1 = (bf16[1024,128]{1,0:T(8,128)(2,1)}, bf16[1024,128]{1,0:T(8,128)(2,1)}, bf16[1024,128]{1,0:T(8,128)(2,1)}, bf16[1024,128]{1,0:T(8,128)(2,1)}) custom-call(bf16[1024,128]{1,0:T(8,128)(2,1)S(1)} %collective-permute-done.halo_ref, ...), custom_call_target="tpu_custom_call", output_to_operand_aliasing={{0}: (5, {}), {1}: (6, {}), {2}: (7, {}), {3}: (8, {})} | custom-call | flops 268435456 | bytes 8388608 | tf_op jit(solution)/shard_map/late_outputs/pallas_call | solution.py:397
  18.9 0.0 collective-permute-done.4.refs_2_
  18.9 1.1 %collective-permute-done.3.refs_1_ = bf16[72,128]{1,0:T(8,128)(2,1)S(1)} collective-permute-done((bf16[72,128]{1,0:T(8,128)(2,1)S(1)}, bf16[72,128]{1,0:T(8,128)(2,1)S(1)}, u32[]{:S(2)}, u32[]{:S(2)}) %collective-permute-start.3) | collective-permute-done | bytes 18464 | tf_op jit(solution)/shard_map/ppermute | solution.py:422
  20.0 0.2 collective-permute-done.2.refs_0_
  20.2 0.6 %totals.1 = (f32[64,128]{1,0:T(8,128)}, f32[8,128]{1,0:T(8,128)}) custom-call(bf16[72,128]{1,0:T(8,128)(2,1)S(1)} %collective-permute-done.2.refs_0_, bf16[72,128]{1,0:T(8,128)(2,1)S(1)} %collective-permute-done.3.refs_1_, bf16[72,128]{1,0:T(8,128)(2,1)S(1)} %collective-permute-done.4.refs_2_, bf16[72,128]{1,0:T(8,128)(2,1)S(1)} %reduce-precision_convert_fusion.refs_3_), custom_call_target="tpu_custom_call" | custom-call | tf_op jit(solution)/shard_map/totals/pallas_call | solution.py:447
  (3 shorter events, 0.0 us)
Async XLA Ops:
  0.6 6.7 %copy-start.1 = (f32[1024]{0:T(1024)S(1)}, f32[1024]{0:T(1024)}, u32[]{:S(2)}) copy-start(f32[1024]{0:T(1024)} %param.15) | copy-start | bytes 12292
  0.6 6.7 %copy-start = (f32[64,128]{1,0:T(8,128)S(1)}, f32[64,128]{1,0:T(8,128)}, u32[]{:S(2)}) copy-start(f32[64,128]{1,0:T(8,128)} %tap_ref.1) | copy-start | bytes 98308
  1.9 9.5 %collective-permute-start = (bf16[1024,128]{1,0:T(8,128)(2,1)S(1)}, bf16[1024,128]{1,0:T(8,128)(2,1)S(1)}, u32[]{:S(2)}, u32[]{:S(2)}) collective-permute-start(bf16[1024,128]{1,0:T(8,128)(2,1)S(1)} %own_block.1.own_ref), channel_id=1, source_target_pairs={{0,16},{16,0},{1,17},{17,1},{2,18},{18,2},{3,19},{19,3},{4,20},{20... | collective-permute-start | bytes 786440 | tf_op jit(solution)/shard_map/ppermute | solution.py:472
  7.2 5.2 %collective-permute-start.1 = (bf16[72,128]{1,0:T(8,128)(2,1)S(1)}, bf16[72,128]{1,0:T(8,128)(2,1)S(1)}, u32[]{:S(2)}, u32[]{:S(2)}) collective-permute-start(bf16[72,128]{1,0:T(8,128)(2,1)S(1)} %get-tuple-element.55), channel_id=1, source_target_pairs={{0,16},{16,0},{1,17},{17,1},{2,18},{18,2},{3,19},{19,3},{4,20},{20... | collective-permute-start | bytes 55304 | tf_op jit(solution)/shard_map/ppermute | solution.py:474
  12.5 6.4 %collective-permute-start.4 = (bf16[72,128]{1,0:T(8,128)(2,1)S(1)}, bf16[72,128]{1,0:T(8,128)(2,1)S(1)}, u32[]{:S(2)}, u32[]{:S(2)}) collective-permute-start(bf16[72,128]{1,0:T(8,128)(2,1)S(1)} %reduce-precision_convert_fusion.refs_3_), channel_id=1, source_target_pairs={{0,8},{4,12},{8,4},{12,0},{1,9},{5,13},{9,5},{13,1},{2,10},{6,14},... | collective-permute-start | bytes 55304 | tf_op jit(solution)/shard_map/ppermute | solution.py:422
  15.4 4.7 %collective-permute-start.3 = (bf16[72,128]{1,0:T(8,128)(2,1)S(1)}, bf16[72,128]{1,0:T(8,128)(2,1)S(1)}, u32[]{:S(2)}, u32[]{:S(2)}) collective-permute-start(bf16[72,128]{1,0:T(8,128)(2,1)S(1)} %reduce-precision_convert_fusion.refs_3_), channel_id=1, source_target_pairs={{0,12},{4,8},{8,0},{12,4},{1,13},{5,9},{9,1},{13,5},{2,14},{6,10},... | collective-permute-start | bytes 55304 | tf_op jit(solution)/shard_map/ppermute | solution.py:422
  16.5 3.8 %collective-permute-start.2 = (bf16[72,128]{1,0:T(8,128)(2,1)S(1)}, bf16[72,128]{1,0:T(8,128)(2,1)S(1)}, u32[]{:S(2)}, u32[]{:S(2)}) collective-permute-start(bf16[72,128]{1,0:T(8,128)(2,1)S(1)} %reduce-precision_convert_fusion.refs_3_), channel_id=1, source_target_pairs={{0,4},{4,0},{8,12},{12,8},{1,5},{5,1},{9,13},{13,9},{2,6},{6,2},{1... | collective-permute-start | bytes 55304 | tf_op jit(solution)/shard_map/ppermute | solution.py:422

commit v5 on v4

--- a/solution.py
+++ b/solution.py
@@ -72,11 +72,12 @@
 
 
 def own_kernel(
-    keep_hbm, query_hbm, key_hbm, value_hbm, grad_hbm, own_ref, one_ref, two_ref, keep_ref, sems
+    keep_hbm, query_hbm, key_hbm, value_hbm, grad_hbm, large_ref, small_ref, one_ref, two_ref, keep_ref,
+    sems,
 ):
     first = lax.axis_index("ctx") == 0
-    parts = 2
-    rows = own_ref.shape[0] // parts
+    parts = 4
+    rows = small_ref.shape[0]
 
     def copies(source_one, source_two):
         made = []
@@ -111,37 +112,46 @@
         waits[2 * part + 1].wait()
         window = pl.ds(part * rows, rows)
         scaled = two_ref[window].astype(F32) * keep
-        own_ref[window] = (scaled * one_ref[window].astype(F32)).astype(BF16)
+        own = (scaled * one_ref[window].astype(F32)).astype(BF16)
+        if part < parts - 1:
+            large_ref[window] = own
+        else:
+            small_ref[...] = own
 
 
 def own_block(keep, query, key, value, grad):
+    channels, length = query.shape
+    whole = pl.BlockSpec(memory_space=pltpu.VMEM)
     return pl.pallas_call(
         own_kernel,
         in_specs=[pl.BlockSpec(memory_space=pltpu.HBM)] * 5,
-        out_specs=pl.BlockSpec(memory_space=pltpu.VMEM),
-        out_shape=pltpu.VMEM(query.shape, BF16),
+        out_specs=[whole] * 2,
+        out_shape=[
+            pltpu.VMEM((channels * 3 // 4, length), BF16),
+            pltpu.VMEM((channels // 4, length), BF16),
+        ],
         scratch_shapes=[
             pltpu.VMEM(query.shape, BF16),
             pltpu.VMEM(query.shape, BF16),
             pltpu.VMEM(keep.shape, keep.dtype),
-            pltpu.SemaphoreType.DMA((5,)),
+            pltpu.SemaphoreType.DMA((9,)),
         ],
         compiler_params=pltpu.CompilerParams(vmem_limit_bytes=12 * 2**20),
         name="own_block",
     )(*map(in_hbm, (keep, query, key, value, grad)))
 
 
-def local_kernel(per_group, *refs):
-    sources, sums_ref, (*held, sems) = refs[:5], refs[5], refs[6:]
+def local_kernel(per_group, count, *refs):
+    sources, sums_ref, (*held, sems) = refs[:count], refs[count], refs[count + 1 :]
     copies = [
         pltpu.make_async_copy(source, target, sems.at[index])
         for index, (source, target) in enumerate(zip(sources, held))
     ]
     for copy in copies:
         copy.start()
-    for copy in copies:
+    for copy in copies[:5]:
         copy.wait()
-    keep_ref, query_ref, key_ref, value_ref, grad_ref = held
+    keep_ref, query_ref, key_ref, value_ref, grad_ref = held[:5]
     channels, length = query_ref.shape
     groups = channels // per_group
     joined = (key_ref[...].astype(F32) * value_ref[...].astype(F32)).astype(BF16)
@@ -158,30 +168,60 @@
         sums_ref[groups + block : groups + block + 1] = direct[
             :1, block * length : (block + 1) * length
         ].astype(sums_ref.dtype)
-
-
-def local_sums(keep, query, key, value, grad, groups, dtype):
-    channels, length = query.shape
-    sources = (keep, query, key, value, grad)
-    return pl.pallas_call(
-        functools.partial(local_kernel, channels // groups),
-        in_specs=[pl.BlockSpec(memory_space=pltpu.HBM)] * 5,
-        out_specs=[pl.BlockSpec(memory_space=pltpu.VMEM)] * 6,
+    for copy in copies[5:]:
+        copy.wait()
+
+
+def local_sums(groups, dtype, *sources):
+    channels, length = sources[1].shape
+    count = len(sources)
+    return pl.pallas_call(
+        functools.partial(local_kernel, channels // groups, count),
+        in_specs=[pl.BlockSpec(memory_space=pltpu.HBM)] * count,
+        out_specs=[pl.BlockSpec(memory_space=pltpu.VMEM)] * (count + 1),
         out_shape=[pltpu.VMEM((groups + channels // length, length), dtype)]
         + [pltpu.VMEM(source.shape, source.dtype) for source in sources],
-        scratch_shapes=[pltpu.SemaphoreType.DMA((5,))],
+        scratch_shapes=[pltpu.SemaphoreType.DMA((count,))],
         cost_estimate=pl.CostEstimate(flops=2**26, bytes_accessed=2**23, transcendentals=0),
         compiler_params=pltpu.CompilerParams(vmem_limit_bytes=12 * 2**20),
         name="local_sums",
     )(*map(in_hbm, sources))
 
 
+def by_role(own, halo):
+    first = lax.axis_index("ctx") == 0
+    return jnp.where(first, halo, own), jnp.where(first, own, halo)
+
+
+def last_kernel(per_group, own_ref, halo_ref, crossed_ref, mine_ref, other_ref, sums_ref):
+    grad, joined = by_role(own_ref[...], halo_ref[...])
+    crossed = lag_sums(grad, joined, per_group, True)
+    sums = mine_ref[...].astype(F32) + other_ref[...].astype(F32)
+    done = crossed_ref.shape[0]
+    groups = done + crossed.shape[0]
+    sums_ref[:done] = (sums[:done] + crossed_ref[...]).astype(BF16)
+    sums_ref[done:groups] = (sums[done:groups] + crossed).astype(BF16)
+    sums_ref[groups:] = sums[groups:].astype(BF16)
+
+
+def last_sums(per_group, *arrays):
+    whole = pl.BlockSpec(memory_space=pltpu.VMEM)
+    return pl.pallas_call(
+        functools.partial(last_kernel, per_group),
+        in_specs=[whole] * len(arrays),
+        out_specs=whole,
+        out_shape=pltpu.VMEM(arrays[-1].shape, BF16),
+        cost_estimate=pl.CostEstimate(flops=2**26, bytes_accessed=2**23, transcendentals=0),
+        compiler_params=pltpu.CompilerParams(vmem_limit_bytes=12 * 2**20),
+        name="last_sums",
+    )(*map(in_vmem, arrays))
+
+
 def cross_kernel(per_group, swap, own_ref, halo_ref, sums_ref):
-    own, halo = own_ref[...], halo_ref[...]
+    grad, joined = own_ref[...], halo_ref[...]
     if swap:
-        first = lax.axis_index("ctx") == 0
-        own, halo = jnp.where(first, halo, own), jnp.where(first, own, halo)
-    sums_ref[...] = lag_sums(own, halo, per_group, True)
+        grad, joined = by_role(grad, joined)
+    sums_ref[...] = lag_sums(grad, joined, per_group, True)
 
 
 def cross_sums(own, halo, groups, swap):
@@ -268,147 +308,89 @@
     rows = made_refs[0].shape[0] // parts
     window = pl.ds(part * rows, rows)
     return [
-        pltpu.make_async_copy(made.at[window], out.at[window], sems.at[2 * part + side])
+        pltpu.make_async_copy(
+            made.at[window], out.at[window], sems.at[part * len(out_refs) + side]
+        )
         for side, (made, out) in enumerate(zip(made_refs, out_refs))
     ]
 
 
-def early_kernel(
-    per_group, parts, keep_ref, tap_ref, skip_ref, query_ref, key_ref, value_ref, grad_ref,
-    out_ref, query_grad_ref, key_grad_ref, value_grad_ref, rest_ref, one_ref, two_ref, upper_ref,
-    made_one_ref, made_two_ref, sems,
+def pair_kernel(
+    per_group, parts, keep_ref, query_ref, key_ref, value_ref, grad_ref, tap_ref, skip_ref, *refs
 ):
+    halo_refs, out_refs, made_refs, sems = refs[:2], refs[2:6], refs[6:10], refs[10]
+    cut = halo_refs[0].shape[0]
     channels, length = query_ref.shape
     groups = channels // per_group
-    row, column = iotas(length, length)
-    causal = column >= row
-    keep = keep_ref[...].astype(F32)
-    skips = skip_ref[...].T
-    first = lax.axis_index("ctx") == 0
-    made_refs = (made_one_ref, made_two_ref)
-
-    def send(part, *refs):
-        for copy in row_copies(parts, part, made_refs, refs, sems):
-            copy.start()
-
-    for group in range(groups):
-        part = slice(group * per_group, (group + 1) * per_group)
-        query = query_ref[part].astype(F32)
-        key = key_ref[part].astype(F32)
-        value = value_ref[part].astype(F32)
-        scaled = grad_ref[part].astype(F32) * keep
-        joined = (key * value).astype(BF16)
-        mixed = (scaled * query).astype(BF16)
-        taps = jnp.broadcast_to(tap_ref[group : group + 1], (length, length))
-        circle = pltpu.roll(taps, 0, 1, stride=1, stride_axis=0)
-        lower = jnp.where(causal, circle, 0.0).astype(BF16)
-        upper_ref[group] = jnp.where(causal, 0.0, circle).astype(BF16)
-        start = group * per_group
-        skip = skips[start % length : start % length + per_group, start // length : start // length + 1]
-        forward = jnp.dot(joined, lower, preferred_element_type=F32)
-        forward += skip * joined.astype(F32)
-        backward = lax.dot_general(mixed, lower, ROWS_BY_ROWS, preferred_element_type=F32)
-        backward += skip * mixed.astype(F32)
-        done = jnp.where(first, forward, backward)
-        made_one_ref[part] = (done * jnp.where(first, query, value)).astype(BF16)
-        made_two_ref[part] = (done * jnp.where(first, scaled, key)).astype(BF16)
-        rest_ref[part] = jnp.where(first, backward, forward)
-        one_ref[part] = jnp.where(first, value, query).astype(BF16)
-        two_ref[part] = jnp.where(first, key, scaled).astype(BF16)
-        if (group + 1) % (groups // parts) == 0:
-            part = group // (groups // parts)
-            pl.when(first)(functools.partial(send, part, out_ref, query_grad_ref))
-            pl.when(jnp.logical_not(first))(
-                functools.partial(send, part, key_grad_ref, value_grad_ref)
-            )
-    for part in range(parts):
-        for copy in row_copies(parts, part, made_refs, (out_ref, query_grad_ref), sems):
-            copy.wait()
-
-
-def early_outputs(keep, taps, skip, query, key, value, grad):
-    channels, length = query.shape
-    groups = taps.shape[0]
-    parts = 2
-    whole = pl.BlockSpec(memory_space=pltpu.VMEM)
-    return pl.pallas_call(
-        functools.partial(early_kernel, channels // groups, parts),
-        in_specs=[whole] * 7,
-        out_specs=[pl.BlockSpec(memory_space=pltpu.HBM)] * 4 + [whole] * 4,
-        out_shape=[jax.ShapeDtypeStruct((channels, length), BF16)] * 4
-        + [
-            pltpu.VMEM((channels, length), F32),
-            pltpu.VMEM((channels, length), BF16),
-            pltpu.VMEM((channels, length), BF16),
-            pltpu.VMEM((groups, length, length), BF16),
-        ],
-        scratch_shapes=[
-            pltpu.VMEM((channels, length), BF16),
-            pltpu.VMEM((channels, length), BF16),
-            pltpu.SemaphoreType.DMA((2 * parts,)),
-        ],
-        cost_estimate=pl.CostEstimate(flops=2**28, bytes_accessed=2**23, transcendentals=0),
-        compiler_params=pltpu.CompilerParams(vmem_limit_bytes=12 * 2**20),
-        name="early_outputs",
-    )(in_vmem(keep), taps, skip.reshape(channels // length, length), *map(in_vmem, (query, key, value, grad)))
-
-
-def late_kernel(
-    per_group, parts, halo_ref, rest_ref, one_ref, two_ref, upper_ref, _out, _query_grad, _key_grad,
-    _value_grad, out_ref, query_grad_ref, key_grad_ref, value_grad_ref, made_one_ref, made_two_ref, sems,
-):
-    groups = halo_ref.shape[0] // per_group
-    first = lax.axis_index("ctx") == 0
-    made_refs = (made_one_ref, made_two_ref)
-
-    def run(transposed, *out_refs):
+    size = groups // parts
+
+    def run(first):
+        row, column = iotas(length, length)
+        causal = column >= row
+        keep = keep_ref[...].astype(F32)
+        skips = skip_ref[...].T
         for group in range(groups):
             part = slice(group * per_group, (group + 1) * per_group)
-            halo, upper = halo_ref[part], upper_ref[group]
-            if transposed:
-                crossed = lax.dot_general(halo, upper, ROWS_BY_ROWS, preferred_element_type=F32)
+            query = query_ref[part].astype(F32)
+            key = key_ref[part].astype(F32)
+            value = value_ref[part].astype(F32)
+            scaled = grad_ref[part].astype(F32) * keep
+            joined = (key * value).astype(BF16)
+            mixed = (scaled * query).astype(BF16)
+            if part.start < cut:
+                halo = halo_refs[0][part]
             else:
-                crossed = jnp.dot(halo, upper, preferred_element_type=F32)
-            total = rest_ref[part] + crossed
-            made_one_ref[part] = (total * one_ref[part].astype(F32)).astype(BF16)
-            made_two_ref[part] = (total * two_ref[part].astype(F32)).astype(BF16)
-            if (group + 1) % (groups // parts) == 0:
-                part = group // (groups // parts)
-                for copy in row_copies(parts, part, made_refs, out_refs, sems):
+                halo = halo_refs[1][part.start - cut : part.stop - cut]
+            taps = jnp.broadcast_to(tap_ref[group : group + 1], (length, length))
+            circle = pltpu.roll(taps, 0, 1, stride=1, stride_axis=0)
+            lower = jnp.where(causal, circle, 0.0).astype(BF16)
+            upper = jnp.where(causal, 0.0, circle).astype(BF16)
+            start = group * per_group
+            skip = skips[
+                start % length : start % length + per_group, start // length : start // length + 1
+            ]
+            if first:
+                ahead, ahead_taps = joined, lower
+                back = jnp.concatenate([mixed, halo], axis=1)
+                back_taps = jnp.concatenate([lower, upper], axis=1)
+            else:
+                ahead = jnp.concatenate([halo, joined], axis=1)
+                ahead_taps = jnp.concatenate([upper, lower], axis=0)
+                back, back_taps = mixed, lower
+            forward = jnp.dot(ahead, ahead_taps, preferred_element_type=F32)
+            forward += skip * joined.astype(F32)
+            backward = lax.dot_general(back, back_taps, ROWS_BY_ROWS, preferred_element_type=F32)
+            backward += skip * mixed.astype(F32)
+            results = (query * forward, scaled * forward, backward * value, backward * key)
+            for made, result in zip(made_refs, results):
+                made[part] = result.astype(BF16)
+            if (group + 1) % size == 0:
+                for copy in row_copies(parts, group // size, made_refs, out_refs, sems):
                     copy.start()
         for part in range(parts):
             for copy in row_copies(parts, part, made_refs, out_refs, sems):
                 copy.wait()
 
-    @pl.when(first)
-    def _():
-        run(True, key_grad_ref, value_grad_ref)
-
-    @pl.when(jnp.logical_not(first))
-    def _():
-        run(False, out_ref, query_grad_ref)
-
-
-def late_outputs(halo, rest, one, two, upper, *results):
-    channels, length = halo.shape
-    groups = upper.shape[0]
+    first = lax.axis_index("ctx") == 0
+    pl.when(first)(functools.partial(run, True))
+    pl.when(jnp.logical_not(first))(functools.partial(run, False))
+
+
+def pair_outputs(keep, query, key, value, grad, taps, skips, halos):
+    channels, length = query.shape
     parts = 2
-    whole = pl.BlockSpec(memory_space=pltpu.VMEM)
-    return pl.pallas_call(
-        functools.partial(late_kernel, channels // groups, parts),
-        in_specs=[whole] * 5 + [pl.BlockSpec(memory_space=pltpu.HBM)] * 4,
+    arrays = (keep, query, key, value, grad, taps, skips, *halos)
+    return pl.pallas_call(
+        functools.partial(pair_kernel, channels // taps.shape[0], parts),
+        in_specs=[pl.BlockSpec(memory_space=pltpu.VMEM)] * len(arrays),
         out_specs=[pl.BlockSpec(memory_space=pltpu.HBM)] * 4,
         out_shape=[jax.ShapeDtypeStruct((channels, length), BF16)] * 4,
-        input_output_aliases={5: 0, 6: 1, 7: 2, 8: 3},
-        scratch_shapes=[
-            pltpu.VMEM((channels, length), BF16),
-            pltpu.VMEM((channels, length), BF16),
-            pltpu.SemaphoreType.DMA((2 * parts,)),
-        ],
+        scratch_shapes=[pltpu.VMEM((channels, length), BF16)] * 4
+        + [pltpu.SemaphoreType.DMA((4 * parts,))],
         cost_estimate=pl.CostEstimate(flops=2**28, bytes_accessed=2**23, transcendentals=0),
         compiler_params=pltpu.CompilerParams(vmem_limit_bytes=12 * 2**20),
-        name="late_outputs",
-    )(in_vmem(halo), in_vmem(rest), in_vmem(one), in_vmem(two), in_vmem(upper), *results)
+        name="pair_outputs",
+    )(*map(in_vmem, arrays))
 
 
 def exchanges(size):
@@ -443,7 +425,7 @@
 
 def totals(terms, groups, tap_scale, skip_scale, axis):
     rows, length = terms[0].shape
-    order = list(reversed(range(len(terms))))
+    order = list(range(len(terms)))
     return pl.pallas_call(
         functools.partial(total_kernel, groups, tap_scale, skip_scale, axis, order),
         in_specs=[pl.BlockSpec(memory_space=pltpu.VMEM)] * len(terms),
@@ -469,21 +451,22 @@
     if shards == 2:
         swap = [(0, 1), (1, 0)]
         own = own_block(keep_mask, query, key, value, grad)
-        halo = lax.ppermute(own, "ctx", swap)
-        mine, *near = local_sums(keep_mask, query, key, value, grad, groups, BF16)
+        halo = [lax.ppermute(part, "ctx", swap) for part in own]
+        skips = skip_gain.reshape(channels // length, length)
+        mine, *near = local_sums(
+            groups, BF16, keep_mask, query, key, value, grad, filter_taps, skips
+        )
         other = lax.ppermute(mine, "ctx", swap)
-        crossed = cross_sums(own, halo, groups, True)
-        sums = mine.astype(F32).at[:groups].add(crossed) + other.astype(F32)
-        sums = lax.reduce_precision(sums, 8, 7).astype(BF16)
-        early = early_outputs(near[0], filter_taps, skip_gain, *near[1:])
+        crossed = cross_sums(own[0], halo[0], groups * 3 // 4, True)
+        sums = last_sums(per_group, own[1], halo[1], crossed, mine, other)
         terms = gather_terms(sums, "dp")
-        results = late_outputs(halo, *early[4:], *early[:4])
+        results = pair_outputs(*near, halo)
     else:
         joined = (key.astype(F32) * value.astype(F32)).astype(BF16)
         own = (grad.astype(F32) * keep_mask.astype(F32) * query.astype(F32)).astype(BF16)
         before = lax.ppermute(joined, "ctx", [(i, i + 1) for i in range(shards - 1)])
         following = lax.ppermute(own, "ctx", [(i + 1, i) for i in range(shards - 1)])
-        mine, *_ = local_sums(keep_mask, query, key, value, grad, groups, F32)
+        mine, *_ = local_sums(groups, F32, keep_mask, query, key, value, grad)
         crossed = cross_sums(own, before, groups, False)
         sums = lax.psum(mine.at[:groups].add(crossed), "ctx")
         terms = gather_terms(sums, "dp")

time: 21 us -> 20.8 us (level)
  starting transfers between devices: 7.56 us -> 9.59 us
  Pallas kernels: 9.98 us -> 8.62 us
  waiting for transfers between devices: 2.6 us -> 1.72 us
    ppermute x1, starting transfers between devices: 0.09 us -> 2.01 us  [body(): other = lax.ppermute(mine, 'ctx', swap)]
    pallas_call x3, Pallas kernels: 7.04 us -> 5.84 us  [the longest x1 2.78 us: pair_outputs(): pl.pallas_call(functools.partial(pair_kernel, channels // taps.shape[0],...]
    ppermute x3, waiting for transfers between devices: 1.32 us -> 0.48 us  [gather_terms(): lax.ppermute(sums, axis, list(enumerate(targets)))]
    ppermute x1 -> x2, starting transfers between devices: 3.01 us -> 3.09 us  [body(): halo = [lax.ppermute(part, 'ctx', swap) for part in own]]
    ppermute x1 -> x2, waiting for transfers between devices: 1.27 us -> 1.24 us  [body(): halo = [lax.ppermute(part, 'ctx', swap) for part in own]]
  transfers between devices with their start and end apart: 5 -> 6, of which waited for: 3 -> 3; matrix products, arithmetic and copies ran while one was open for 0% -> 0% of each run, Pallas kernels for 39% -> 30%
where the time goes in v5:
time: 20.8 us; the launch traced here: 20.6 us
  starting transfers between devices  9.59 us (46%)
  Pallas kernels  8.62 us (41%)
  waiting for transfers between devices  1.72 us (8%)
  between operations  0.67 us (3%)
    ppermute x3, starting transfers between devices, gather_terms(): lax.ppermute(sums, axis, list(enumerate(targets)))  4.49 us
    ppermute x2, starting transfers between devices, body(): halo = [lax.ppermute(part, 'ctx', swap) for part in own]  3.09 us
    pallas_call x1, Pallas kernels, pair_outputs(): pl.pallas_call(functools.partial(pair_kernel, channels // taps.shape[0],...  2.78 us
    pallas_call x1, Pallas kernels, local_sums(): pl.pallas_call(functools.partial(local_kernel, channels // groups, count)...  2.4 us
    ppermute x1, starting transfers between devices, body(): other = lax.ppermute(mine, 'ctx', swap)  2.01 us
    ppermute x2, waiting for transfers between devices, body(): halo = [lax.ppermute(part, 'ctx', swap) for part in own]  1.24 us
    pallas_call x1, Pallas kernels, own_block(): pl.pallas_call(own_kernel, in_specs=[pl.BlockSpec(memory_space=pltpu.HBM)...  1.17 us
    pallas_call x1, Pallas kernels, cross_sums(): pl.pallas_call(functools.partial(cross_kernel, channels // groups, swap),...  0.96 us
  transfers between devices with their start and end apart: 6, of which 3 were waited for; matrix products, arithmetic and copies ran while one was open for 0% of the time, Pallas kernels for 30%

profile of v5, /device:TPU:0, one launch (start us, length us, event | category | flops | bytes accessed | tf_op | source)
XLA Modules:
  0.0 20.6 jit_solution(12716406796858807832)
XLA Ops:
  0.6 1.2 %own_block.1 = (bf16[768,128]{1,0:T(8,128)(2,1)S(1)}, bf16[256,128]{1,0:T(8,128)(2,1)S(1)}) custom-call(s32[1,128]{1,0:T(1,128)} %keep_hbm.1, bf16[1024,128]{1,0:T(8,128)(2,1)} %bitcast.10, bf16[1024,128]{1,0:T(8,128)(2,1)} %bitcast.12, bf16[1024,128]{1,0:T(8,128)(2,1)} %bitcast.14, bf16[1024,128]{1,0:T(8,128)(2,1)} %bitcast.16), custom_call_target="tpu_custom_call" | custom-call | tf_op jit(solution)/shard_map/own_block/pallas_call | solution.py:125
  1.8 3.0 %collective-permute-start = (bf16[768,128]{1,0:T(8,128)(2,1)S(1)}, bf16[768,128]{1,0:T(8,128)(2,1)S(1)}, u32[]{:S(2)}, u32[]{:S(2)}) collective-permute-start(bf16[768,128]{1,0:T(8,128)(2,1)S(1)} %get-tuple-element.29.own_ref), channel_id=1, source_target_pairs={{0,16},{16,0},{1,17},{17,1},{2,18},{18,2},{3,19},{19,3},{4,20},{20... | collective-permute-start | bytes 589832 | tf_op jit(solution)/shard_map/ppermute | solution.py:454
  4.8 0.1 collective-permute-start.1
  4.9 2.4 %local_sums.1 = (bf16[72,128]{1,0:T(8,128)(2,1)S(1)}, s32[1,128]{1,0:T(1,128)S(1)}, bf16[1024,128]{1,0:T(8,128)(2,1)S(1)}, bf16[1024,128]{1,0:T(8,128)(2,1)S(1)}...) custom-call(s32[1,128]{1,0:T(1,128)} %keep_hbm.1, ...), custom_call_target="tpu_custom_call" | custom-call | flops 67108864 | bytes 8388608 | tf_op jit(solution)/shard_map/local_sums/pallas_call | solution.py:178
  7.3 2.0 %collective-permute-start.2 = (bf16[72,128]{1,0:T(8,128)(2,1)S(1)}, bf16[72,128]{1,0:T(8,128)(2,1)S(1)}, u32[]{:S(2)}, u32[]{:S(2)}) collective-permute-start(bf16[72,128]{1,0:T(8,128)(2,1)S(1)} %get-tuple-element.35.mine_ref), channel_id=1, source_target_pairs={{0,16},{16,0},{1,17},{17,1},{2,18},{18,2},{3,19},{19,3},{4,20},{20... | collective-permute-start | bytes 55304 | tf_op jit(solution)/shard_map/ppermute | solution.py:459
  9.3 1.2 %collective-permute-done.refs_0_.halo_ref = bf16[768,128]{1,0:T(8,128)(2,1)S(1)} collective-permute-done((bf16[768,128]{1,0:T(8,128)(2,1)S(1)}, bf16[768,128]{1,0:T(8,128)(2,1)S(1)}, u32[]{:S(2)}, u32[]{:S(2)}) %collective-permute-start) | collective-permute-done | bytes 196640 | tf_op jit(solution)/shard_map/ppermute | solution.py:454
  10.6 1.0 %cross_sums.1.crossed_ref = f32[48,128]{1,0:T(8,128)S(1)} custom-call(bf16[768,128]{1,0:T(8,128)(2,1)S(1)} %get-tuple-element.29.own_ref, bf16[768,128]{1,0:T(8,128)(2,1)S(1)} %collective-permute-done.refs_0_.halo_ref), custom_call_target="tpu_custom_call" | custom-call | flops 67108864 | bytes 8388608 | tf_op jit(solution)/shard_map/cross_sums/pallas_call | solution.py:230
  11.5 0.0 collective-permute-done.2.other_ref
  11.5 0.0 collective-permute-done.1.refs_1_.halo_ref
  11.5 0.7 %last_sums.1.refs_0_ = bf16[72,128]{1,0:T(8,128)(2,1)S(1)} custom-call(bf16[256,128]{1,0:T(8,128)(2,1)S(1)} %get-tuple-element.30.own_ref, bf16[256,128]{1,0:T(8,128)(2,1)S(1)} %collective-permute-done.1.refs_1_.halo_ref, f32[48,128]{1,0:T(8,128)S(1)} %cross_sums.1.crossed_ref, bf16[72,128]{1,0:T(8,128)(2,1)S(1)} %get-tuple-element.35.mine_ref, ...), custom_call_target="tpu_custom_call" | custom-call | flops 67108864 | bytes 8388608 | tf_op jit(solution)/shard_map/last_sums/pallas_call | solution.py:209
  12.2 2.9 %collective-permute-start.3 = (bf16[72,128]{1,0:T(8,128)(2,1)S(1)}, bf16[72,128]{1,0:T(8,128)(2,1)S(1)}, u32[]{:S(2)}, u32[]{:S(2)}) collective-permute-start(bf16[72,128]{1,0:T(8,128)(2,1)S(1)} %last_sums.1.refs_0_), channel_id=1, source_target_pairs={{0,8},{4,12},{8,4},{12,0},{1,9},{5,13},{9,5},{13,1},{2,10},{6,14},... | collective-permute-start | bytes 55304 | tf_op jit(solution)/shard_map/ppermute | solution.py:404
  15.1 1.1 %collective-permute-start.4 = (bf16[72,128]{1,0:T(8,128)(2,1)S(1)}, bf16[72,128]{1,0:T(8,128)(2,1)S(1)}, u32[]{:S(2)}, u32[]{:S(2)}) collective-permute-start(bf16[72,128]{1,0:T(8,128)(2,1)S(1)} %last_sums.1.refs_0_), channel_id=1, source_target_pairs={{0,12},{4,8},{8,0},{12,4},{1,13},{5,9},{9,1},{13,5},{2,14},{6,10},... | collective-permute-start | bytes 55304 | tf_op jit(solution)/shard_map/ppermute | solution.py:404
  16.2 0.5 %collective-permute-start.5 = (bf16[72,128]{1,0:T(8,128)(2,1)S(1)}, bf16[72,128]{1,0:T(8,128)(2,1)S(1)}, u32[]{:S(2)}, u32[]{:S(2)}) collective-permute-start(bf16[72,128]{1,0:T(8,128)(2,1)S(1)} %last_sums.1.refs_0_), channel_id=1, source_target_pairs={{0,4},{4,0},{8,12},{12,8},{1,5},{5,1},{9,13},{13,9},{2,6},{6,2},{1... | collective-permute-start | bytes 55304 | tf_op jit(solution)/shard_map/ppermute | solution.py:404
  16.7 2.8 %pair_outputs.1 = (bf16[1024,128]{1,0:T(8,128)(2,1)}, bf16[1024,128]{1,0:T(8,128)(2,1)}, bf16[1024,128]{1,0:T(8,128)(2,1)}, bf16[1024,128]{1,0:T(8,128)(2,1)}) custom-call(s32[1,128]{1,0:T(1,128)S(1)} %get-tuple-element.22.keep_ref, bf16[1024,128]{1,0:T(8,128)(2,1)S(1)} %get-tuple-element.23.query_ref, bf16[1024,128]{1,0:T(8,128)(2,1)S(1)} %get-tuple-element.24.key_ref, ...), custom_call_target="tpu_custom_call" | custom-call | flops 268435456 | bytes 8388608 | tf_op jit(solution)/shard_map/pair_outputs/pallas_call | solution.py:383
  19.5 0.0 collective-permute-done.3.refs_1_
  19.5 0.3 %collective-permute-done.4.refs_2_ = bf16[72,128]{1,0:T(8,128)(2,1)S(1)} collective-permute-done((bf16[72,128]{1,0:T(8,128)(2,1)S(1)}, bf16[72,128]{1,0:T(8,128)(2,1)S(1)}, u32[]{:S(2)}, u32[]{:S(2)}) %collective-permute-start.4) | collective-permute-done | bytes 18464 | tf_op jit(solution)/shard_map/ppermute | solution.py:404
  19.8 0.2 collective-permute-done.5.refs_3_
  20.0 0.6 %totals.1 = (f32[64,128]{1,0:T(8,128)}, f32[8,128]{1,0:T(8,128)}) custom-call(bf16[72,128]{1,0:T(8,128)(2,1)S(1)} %last_sums.1.refs_0_, bf16[72,128]{1,0:T(8,128)(2,1)S(1)} %collective-permute-done.3.refs_1_, bf16[72,128]{1,0:T(8,128)(2,1)S(1)} %collective-permute-done.4.refs_2_, bf16[72,128]{1,0:T(8,128)(2,1)S(1)} %collective-permute-done.5.refs_3_), custom_call_target="tpu_custom_call" | custom-call | tf_op jit(solution)/shard_map/totals/pallas_call | solution.py:429
Async XLA Ops:
  1.8 8.7 %collective-permute-start = (bf16[768,128]{1,0:T(8,128)(2,1)S(1)}, bf16[768,128]{1,0:T(8,128)(2,1)S(1)}, u32[]{:S(2)}, u32[]{:S(2)}) collective-permute-start(bf16[768,128]{1,0:T(8,128)(2,1)S(1)} %get-tuple-element.29.own_ref), channel_id=1, source_target_pairs={{0,16},{16,0},{1,17},{17,1},{2,18},{18,2},{3,19},{19,3},{4,20},{20... | collective-permute-start | bytes 589832 | tf_op jit(solution)/shard_map/ppermute | solution.py:454
  4.8 6.7 %collective-permute-start.1 = (bf16[256,128]{1,0:T(8,128)(2,1)S(1)}, bf16[256,128]{1,0:T(8,128)(2,1)S(1)}, u32[]{:S(2)}, u32[]{:S(2)}) collective-permute-start(bf16[256,128]{1,0:T(8,128)(2,1)S(1)} %get-tuple-element.30.own_ref), channel_id=1, source_target_pairs={{0,16},{16,0},{1,17},{17,1},{2,18},{18,2},{3,19},{19,3},{4,20},{20... | collective-permute-start | bytes 196616 | tf_op jit(solution)/shard_map/ppermute | solution.py:454
  7.3 4.2 %collective-permute-start.2 = (bf16[72,128]{1,0:T(8,128)(2,1)S(1)}, bf16[72,128]{1,0:T(8,128)(2,1)S(1)}, u32[]{:S(2)}, u32[]{:S(2)}) collective-permute-start(bf16[72,128]{1,0:T(8,128)(2,1)S(1)} %get-tuple-element.35.mine_ref), channel_id=1, source_target_pairs={{0,16},{16,0},{1,17},{17,1},{2,18},{18,2},{3,19},{19,3},{4,20},{20... | collective-permute-start | bytes 55304 | tf_op jit(solution)/shard_map/ppermute | solution.py:459
  12.2 7.3 %collective-permute-start.3 = (bf16[72,128]{1,0:T(8,128)(2,1)S(1)}, bf16[72,128]{1,0:T(8,128)(2,1)S(1)}, u32[]{:S(2)}, u32[]{:S(2)}) collective-permute-start(bf16[72,128]{1,0:T(8,128)(2,1)S(1)} %last_sums.1.refs_0_), channel_id=1, source_target_pairs={{0,8},{4,12},{8,4},{12,0},{1,9},{5,13},{9,5},{13,1},{2,10},{6,14},... | collective-permute-start | bytes 55304 | tf_op jit(solution)/shard_map/ppermute | solution.py:404
  15.1 4.7 %collective-permute-start.4 = (bf16[72,128]{1,0:T(8,128)(2,1)S(1)}, bf16[72,128]{1,0:T(8,128)(2,1)S(1)}, u32[]{:S(2)}, u32[]{:S(2)}) collective-permute-start(bf16[72,128]{1,0:T(8,128)(2,1)S(1)} %last_sums.1.refs_0_), channel_id=1, source_target_pairs={{0,12},{4,8},{8,0},{12,4},{1,13},{5,9},{9,1},{13,5},{2,14},{6,10},... | collective-permute-start | bytes 55304 | tf_op jit(solution)/shard_map/ppermute | solution.py:404
  16.2 3.8 %collective-permute-start.5 = (bf16[72,128]{1,0:T(8,128)(2,1)S(1)}, bf16[72,128]{1,0:T(8,128)(2,1)S(1)}, u32[]{:S(2)}, u32[]{:S(2)}) collective-permute-start(bf16[72,128]{1,0:T(8,128)(2,1)S(1)} %last_sums.1.refs_0_), channel_id=1, source_target_pairs={{0,4},{4,0},{8,12},{12,8},{1,5},{5,1},{9,13},{13,9},{2,6},{6,2},{1... | collective-permute-start | bytes 55304 | tf_op jit(solution)/shard_map/ppermute | solution.py:404

commit v6 on v5

--- a/solution.py
+++ b/solution.py
@@ -10,6 +10,7 @@
 
 BF16 = jnp.bfloat16
 F32 = jnp.float32
+PARTS = 2
 ROWS_BY_ROWS = (((1,), (1,)), ((), ()))
 
 
@@ -71,86 +72,77 @@
     return pltpu.roll(jnp.concatenate(sums, axis=0), length - span + 1, 1)
 
 
-def own_kernel(
-    keep_hbm, query_hbm, key_hbm, value_hbm, grad_hbm, large_ref, small_ref, one_ref, two_ref, keep_ref,
-    sems,
-):
+def own_kernel(*refs):
+    sources, own_ref, held, sems = refs[:7], refs[7], refs[8:15], refs[15]
     first = lax.axis_index("ctx") == 0
-    parts = 4
-    rows = small_ref.shape[0]
-
-    def copies(source_one, source_two):
-        made = []
-        for part in range(parts):
-            window = pl.ds(part * rows, rows)
-            for side, (source, target) in enumerate(((source_one, one_ref), (source_two, two_ref))):
-                made.append(
-                    pltpu.make_async_copy(
-                        source.at[window], target.at[window], sems.at[2 * part + side]
-                    )
-                )
-        return made
-
-    keep_copy = pltpu.make_async_copy(keep_hbm, keep_ref, sems.at[2 * parts])
-
-    @pl.when(first)
+    keep_ref = held[0]
+    channels = own_ref.shape[0]
+
+    def run(one, two, others, masked):
+        copies = {
+            (index, part): pltpu.make_async_copy(
+                sources[index].at[pl.ds(part * channels // PARTS, channels // PARTS)],
+                held[index].at[pl.ds(part * channels // PARTS, channels // PARTS)],
+                sems.at[index * PARTS + part],
+            )
+            for index in (one, two)
+            for part in range(PARTS)
+        }
+        for index in (0, *others):
+            copies[index, 0] = pltpu.make_async_copy(
+                sources[index], held[index], sems.at[index * PARTS]
+            )
+        copies[0, 0].start()
+        for part in range(PARTS):
+            copies[one, part].start()
+            copies[two, part].start()
+        for index in others:
+            copies[index, 0].start()
+        copies[0, 0].wait()
+        for part in range(PARTS):
+            copies[one, part].wait()
+            copies[two, part].wait()
+            window = pl.ds(part * channels // PARTS, channels // PARTS)
+            scaled = held[two][window].astype(F32)
+            if masked:
+                scaled = scaled * keep_ref[...].astype(F32)
+            own_ref[window] = (scaled * held[one][window].astype(F32)).astype(BF16)
+        for index in others:
+            copies[index, 0].wait()
+
+    pl.when(first)(functools.partial(run, 2, 3, (1, 4, 5, 6), False))
+    pl.when(jnp.logical_not(first))(functools.partial(run, 1, 4, (2, 3, 5, 6), True))
+
+
+def own_block(*sources):
+    whole = pl.BlockSpec(memory_space=pltpu.VMEM)
+    return pl.pallas_call(
+        own_kernel,
+        in_specs=[pl.BlockSpec(memory_space=pltpu.HBM)] * 7,
+        out_specs=[whole] * 8,
+        out_shape=[pltpu.VMEM(sources[1].shape, BF16)]
+        + [pltpu.VMEM(source.shape, source.dtype) for source in sources],
+        scratch_shapes=[pltpu.SemaphoreType.DMA((7 * PARTS,))],
+        compiler_params=pltpu.CompilerParams(vmem_limit_bytes=12 * 2**20),
+        name="own_block",
+    )(*map(in_hbm, sources))
+
+
+def local_kernel(per_group, turn, *refs):
+    held, sums_ref = refs[:7], refs[7 if turn != 1 else 8]
+    sum_local = functools.partial(local_part, per_group, held, sums_ref)
+    if turn is None:
+        sum_local()
+        return
+
+    @pl.when(lax.axis_index("tp") % 2 == 1 - turn)
     def _():
-        for copy in copies(key_hbm, value_hbm):
-            copy.start()
-
-    @pl.when(jnp.logical_not(first))
-    def _():
-        for copy in copies(query_hbm, grad_hbm):
-            copy.start()
-
-    keep_copy.start()
-    keep_copy.wait()
-    keep = jnp.where(first, 1.0, keep_ref[...].astype(F32))
-    waits = copies(key_hbm, value_hbm)
-    for part in range(parts):
-        waits[2 * part].wait()
-        waits[2 * part + 1].wait()
-        window = pl.ds(part * rows, rows)
-        scaled = two_ref[window].astype(F32) * keep
-        own = (scaled * one_ref[window].astype(F32)).astype(BF16)
-        if part < parts - 1:
-            large_ref[window] = own
-        else:
-            small_ref[...] = own
-
-
-def own_block(keep, query, key, value, grad):
-    channels, length = query.shape
-    whole = pl.BlockSpec(memory_space=pltpu.VMEM)
-    return pl.pallas_call(
-        own_kernel,
-        in_specs=[pl.BlockSpec(memory_space=pltpu.HBM)] * 5,
-        out_specs=[whole] * 2,
-        out_shape=[
-            pltpu.VMEM((channels * 3 // 4, length), BF16),
-            pltpu.VMEM((channels // 4, length), BF16),
-        ],
-        scratch_shapes=[
-            pltpu.VMEM(query.shape, BF16),
-            pltpu.VMEM(query.shape, BF16),
-            pltpu.VMEM(keep.shape, keep.dtype),
-            pltpu.SemaphoreType.DMA((9,)),
-        ],
-        compiler_params=pltpu.CompilerParams(vmem_limit_bytes=12 * 2**20),
-        name="own_block",
-    )(*map(in_hbm, (keep, query, key, value, grad)))
-
-
-def local_kernel(per_group, count, *refs):
-    sources, sums_ref, (*held, sems) = refs[:count], refs[count], refs[count + 1 :]
-    copies = [
-        pltpu.make_async_copy(source, target, sems.at[index])
-        for index, (source, target) in enumerate(zip(sources, held))
-    ]
-    for copy in copies:
-        copy.start()
-    for copy in copies[:5]:
-        copy.wait()
+        sum_local()
+        if turn == 0:
+            filters(per_group, held, None, refs[8:12], refs[12:14], refs[14], "free")
+
+
+def local_part(per_group, held, sums_ref):
     keep_ref, query_ref, key_ref, value_ref, grad_ref = held[:5]
     channels, length = query_ref.shape
     groups = channels // per_group
@@ -168,53 +160,30 @@
         sums_ref[groups + block : groups + block + 1] = direct[
             :1, block * length : (block + 1) * length
         ].astype(sums_ref.dtype)
-    for copy in copies[5:]:
-        copy.wait()
-
-
-def local_sums(groups, dtype, *sources):
-    channels, length = sources[1].shape
-    count = len(sources)
-    return pl.pallas_call(
-        functools.partial(local_kernel, channels // groups, count),
-        in_specs=[pl.BlockSpec(memory_space=pltpu.HBM)] * count,
-        out_specs=[pl.BlockSpec(memory_space=pltpu.VMEM)] * (count + 1),
+
+
+def local_sums(groups, dtype, held, turn=None, made=()):
+    channels, length = held[1].shape
+    whole = pl.BlockSpec(memory_space=pltpu.VMEM)
+    free = turn == 0
+    return pl.pallas_call(
+        functools.partial(local_kernel, channels // groups, turn),
+        in_specs=[whole] * (7 + len(made)),
+        out_specs=[whole] + [pl.BlockSpec(memory_space=pltpu.HBM)] * (4 * free),
         out_shape=[pltpu.VMEM((groups + channels // length, length), dtype)]
-        + [pltpu.VMEM(source.shape, source.dtype) for source in sources],
-        scratch_shapes=[pltpu.SemaphoreType.DMA((count,))],
+        + [jax.ShapeDtypeStruct((channels, length), BF16)] * (4 * free),
+        input_output_aliases={7 + index: index for index in range(len(made))},
+        scratch_shapes=[pltpu.VMEM((channels, length), BF16)] * (2 * free)
+        + [pltpu.SemaphoreType.DMA((2 * PARTS,))] * free,
         cost_estimate=pl.CostEstimate(flops=2**26, bytes_accessed=2**23, transcendentals=0),
         compiler_params=pltpu.CompilerParams(vmem_limit_bytes=12 * 2**20),
         name="local_sums",
-    )(*map(in_hbm, sources))
+    )(*map(in_vmem, (*held, *made)))
 
 
 def by_role(own, halo):
     first = lax.axis_index("ctx") == 0
     return jnp.where(first, halo, own), jnp.where(first, own, halo)
-
-
-def last_kernel(per_group, own_ref, halo_ref, crossed_ref, mine_ref, other_ref, sums_ref):
-    grad, joined = by_role(own_ref[...], halo_ref[...])
-    crossed = lag_sums(grad, joined, per_group, True)
-    sums = mine_ref[...].astype(F32) + other_ref[...].astype(F32)
-    done = crossed_ref.shape[0]
-    groups = done + crossed.shape[0]
-    sums_ref[:done] = (sums[:done] + crossed_ref[...]).astype(BF16)
-    sums_ref[done:groups] = (sums[done:groups] + crossed).astype(BF16)
-    sums_ref[groups:] = sums[groups:].astype(BF16)
-
-
-def last_sums(per_group, *arrays):
-    whole = pl.BlockSpec(memory_space=pltpu.VMEM)
-    return pl.pallas_call(
-        functools.partial(last_kernel, per_group),
-        in_specs=[whole] * len(arrays),
-        out_specs=whole,
-        out_shape=pltpu.VMEM(arrays[-1].shape, BF16),
-        cost_estimate=pl.CostEstimate(flops=2**26, bytes_accessed=2**23, transcendentals=0),
-        compiler_params=pltpu.CompilerParams(vmem_limit_bytes=12 * 2**20),
-        name="last_sums",
-    )(*map(in_vmem, arrays))
 
 
 def cross_kernel(per_group, swap, own_ref, halo_ref, sums_ref):
@@ -304,8 +273,8 @@
     )(keep, taps, skip_rows, query, key, value, grad, before, following)
 
 
-def row_copies(parts, part, made_refs, out_refs, sems):
-    rows = made_refs[0].shape[0] // parts
+def row_copies(part, made_refs, out_refs, sems):
+    rows = made_refs[0].shape[0] // PARTS
     window = pl.ds(part * rows, rows)
     return [
         pltpu.make_async_copy(
@@ -315,82 +284,98 @@
     ]
 
 
-def pair_kernel(
-    per_group, parts, keep_ref, query_ref, key_ref, value_ref, grad_ref, tap_ref, skip_ref, *refs
-):
-    halo_refs, out_refs, made_refs, sems = refs[:2], refs[2:6], refs[6:10], refs[10]
-    cut = halo_refs[0].shape[0]
+def filters(per_group, held, halo_ref, out_refs, made_refs, sems, chosen):
+    first = lax.axis_index("ctx") == 0
+    for here, place in ((True, first), (False, jnp.logical_not(first))):
+        forward = chosen == "all" or (chosen == "free") == here
+        backward = chosen == "all" or (chosen == "free") != here
+        pl.when(place)(
+            functools.partial(
+                filter_groups, per_group, held, halo_ref, out_refs, made_refs, sems, here, forward, backward
+            )
+        )
+
+
+def filter_groups(per_group, held, halo_ref, out_refs, made_refs, sems, first, forward, backward):
+    keep_ref, query_ref, key_ref, value_ref, grad_ref, tap_ref, skip_ref = held
+    out_refs = out_refs[0 if forward else 2 : 4 if backward else 2]
+    made_refs = made_refs[: len(out_refs)]
     channels, length = query_ref.shape
     groups = channels // per_group
-    size = groups // parts
-
-    def run(first):
-        row, column = iotas(length, length)
-        causal = column >= row
-        keep = keep_ref[...].astype(F32)
-        skips = skip_ref[...].T
-        for group in range(groups):
-            part = slice(group * per_group, (group + 1) * per_group)
-            query = query_ref[part].astype(F32)
-            key = key_ref[part].astype(F32)
-            value = value_ref[part].astype(F32)
-            scaled = grad_ref[part].astype(F32) * keep
-            joined = (key * value).astype(BF16)
-            mixed = (scaled * query).astype(BF16)
-            if part.start < cut:
-                halo = halo_refs[0][part]
-            else:
-                halo = halo_refs[1][part.start - cut : part.stop - cut]
-            taps = jnp.broadcast_to(tap_ref[group : group + 1], (length, length))
-            circle = pltpu.roll(taps, 0, 1, stride=1, stride_axis=0)
-            lower = jnp.where(causal, circle, 0.0).astype(BF16)
-            upper = jnp.where(causal, 0.0, circle).astype(BF16)
-            start = group * per_group
-            skip = skips[
-                start % length : start % length + per_group, start // length : start // length + 1
-            ]
+    size = groups // PARTS
+    row, column = iotas(length, length)
+    causal = column >= row
+    keep = keep_ref[...].astype(F32)
+    skips = skip_ref[...].T
+    for group in range(groups):
+        start = group * per_group
+        part = slice(start, start + per_group)
+        query = query_ref[part].astype(F32)
+        key = key_ref[part].astype(F32)
+        value = value_ref[part].astype(F32)
+        scaled = grad_ref[part].astype(F32) * keep
+        joined = (key * value).astype(BF16)
+        mixed = (scaled * query).astype(BF16)
+        taps = jnp.broadcast_to(tap_ref[group : group + 1], (length, length))
+        circle = pltpu.roll(taps, 0, 1, stride=1, stride_axis=0)
+        lower = jnp.where(causal, circle, 0.0).astype(BF16)
+        upper = jnp.where(causal, 0.0, circle).astype(BF16)
+        skip = skips[
+            start % length : start % length + per_group, start // length : start // length + 1
+        ]
+        if halo_ref is not None:
+            halo = halo_ref[part]
+        results = []
+        if forward:
+            source, matrix = joined, lower
+            if not first:
+                source = jnp.concatenate([halo, joined], axis=1)
+                matrix = jnp.concatenate([upper, lower], axis=0)
+            mixed_sum = jnp.dot(source, matrix, preferred_element_type=F32)
+            mixed_sum += skip * joined.astype(F32)
+            results += [query * mixed_sum, scaled * mixed_sum]
+        if backward:
+            source, matrix = mixed, lower
             if first:
-                ahead, ahead_taps = joined, lower
-                back = jnp.concatenate([mixed, halo], axis=1)
-                back_taps = jnp.concatenate([lower, upper], axis=1)
-            else:
-                ahead = jnp.concatenate([halo, joined], axis=1)
-                ahead_taps = jnp.concatenate([upper, lower], axis=0)
-                back, back_taps = mixed, lower
-            forward = jnp.dot(ahead, ahead_taps, preferred_element_type=F32)
-            forward += skip * joined.astype(F32)
-            backward = lax.dot_general(back, back_taps, ROWS_BY_ROWS, preferred_element_type=F32)
-            backward += skip * mixed.astype(F32)
-            results = (query * forward, scaled * forward, backward * value, backward * key)
-            for made, result in zip(made_refs, results):
-                made[part] = result.astype(BF16)
-            if (group + 1) % size == 0:
-                for copy in row_copies(parts, group // size, made_refs, out_refs, sems):
-                    copy.start()
-        for part in range(parts):
-            for copy in row_copies(parts, part, made_refs, out_refs, sems):
-                copy.wait()
-
-    first = lax.axis_index("ctx") == 0
-    pl.when(first)(functools.partial(run, True))
-    pl.when(jnp.logical_not(first))(functools.partial(run, False))
-
-
-def pair_outputs(keep, query, key, value, grad, taps, skips, halos):
-    channels, length = query.shape
-    parts = 2
-    arrays = (keep, query, key, value, grad, taps, skips, *halos)
-    return pl.pallas_call(
-        functools.partial(pair_kernel, channels // taps.shape[0], parts),
-        in_specs=[pl.BlockSpec(memory_space=pltpu.VMEM)] * len(arrays),
-        out_specs=[pl.BlockSpec(memory_space=pltpu.HBM)] * 4,
+                source = jnp.concatenate([mixed, halo], axis=1)
+                matrix = jnp.concatenate([lower, upper], axis=1)
+            joined_grad = lax.dot_general(source, matrix, ROWS_BY_ROWS, preferred_element_type=F32)
+            joined_grad += skip * mixed.astype(F32)
+            results += [joined_grad * value, joined_grad * key]
+        for made, result in zip(made_refs, results):
+            made[part] = result.astype(BF16)
+        if (group + 1) % size == 0:
+            for copy in row_copies(group // size, made_refs, out_refs, sems):
+                copy.start()
+    for part in range(PARTS):
+        for copy in row_copies(part, made_refs, out_refs, sems):
+            copy.wait()
+
+
+def pair_kernel(per_group, *refs):
+    held, halo_ref, out_refs = refs[:7], refs[7], refs[12:16]
+    made_refs, sems = refs[16:20], refs[20]
+    even = lax.axis_index("tp") % 2 == 0
+    rest = (per_group, held, halo_ref, out_refs, made_refs, sems)
+    pl.when(even)(functools.partial(filters, *rest, "all"))
+    pl.when(jnp.logical_not(even))(functools.partial(filters, *rest, "bound"))
+
+
+def pair_outputs(held, halo, results):
+    channels, length = held[1].shape
+    hbm = pl.BlockSpec(memory_space=pltpu.HBM)
+    return pl.pallas_call(
+        functools.partial(pair_kernel, channels // held[5].shape[0]),
+        in_specs=[pl.BlockSpec(memory_space=pltpu.VMEM)] * 8 + [hbm] * 4,
+        out_specs=[hbm] * 4,
         out_shape=[jax.ShapeDtypeStruct((channels, length), BF16)] * 4,
+        input_output_aliases={8: 0, 9: 1, 10: 2, 11: 3},
         scratch_shapes=[pltpu.VMEM((channels, length), BF16)] * 4
-        + [pltpu.SemaphoreType.DMA((4 * parts,))],
+        + [pltpu.SemaphoreType.DMA((4 * PARTS,))],
         cost_estimate=pl.CostEstimate(flops=2**28, bytes_accessed=2**23, transcendentals=0),
         compiler_params=pltpu.CompilerParams(vmem_limit_bytes=12 * 2**20),
         name="pair_outputs",
-    )(*map(in_vmem, arrays))
+    )(*map(in_vmem, (*held, halo)), *results)
 
 
 def exchanges(size):
@@ -450,23 +435,26 @@
     query, key, value, grad = query_act[0], key_act[0], value_act[0], out_grad[0]
     if shards == 2:
         swap = [(0, 1), (1, 0)]
-        own = own_block(keep_mask, query, key, value, grad)
-        halo = [lax.ppermute(part, "ctx", swap) for part in own]
         skips = skip_gain.reshape(channels // length, length)
-        mine, *near = local_sums(
-            groups, BF16, keep_mask, query, key, value, grad, filter_taps, skips
-        )
+        own, *held = own_block(keep_mask, query, key, value, grad, filter_taps, skips)
+        mine, *free = local_sums(groups, BF16, held, 0)
+        own, mine = lax.optimization_barrier((own, mine))
+        halo = lax.ppermute(own, "ctx", swap)
+        (mine,) = local_sums(groups, BF16, held, 1, (mine,))
         other = lax.ppermute(mine, "ctx", swap)
-        crossed = cross_sums(own[0], halo[0], groups * 3 // 4, True)
-        sums = last_sums(per_group, own[1], halo[1], crossed, mine, other)
+        crossed = cross_sums(own, halo, groups, True)
+        sums = mine.astype(F32).at[:groups].add(crossed) + other.astype(F32)
+        sums = lax.reduce_precision(sums, 8, 7).astype(BF16)
         terms = gather_terms(sums, "dp")
-        results = pair_outputs(*near, halo)
+        results = pair_outputs(held, halo, free)
     else:
         joined = (key.astype(F32) * value.astype(F32)).astype(BF16)
         own = (grad.astype(F32) * keep_mask.astype(F32) * query.astype(F32)).astype(BF16)
         before = lax.ppermute(joined, "ctx", [(i, i + 1) for i in range(shards - 1)])
         following = lax.ppermute(own, "ctx", [(i + 1, i) for i in range(shards - 1)])
-        mine, *_ = local_sums(groups, F32, keep_mask, query, key, value, grad)
+        skips = skip_gain.reshape(channels // length, length)
+        sources = (keep_mask, query, key, value, grad, filter_taps, skips)
+        (mine,) = local_sums(groups, F32, sources)
         crossed = cross_sums(own, before, groups, False)
         sums = lax.psum(mine.at[:groups].add(crossed), "ctx")
         terms = gather_terms(sums, "dp")

time: 20.8 us -> 20.4 us (0.981)
  waiting for transfers between devices: 1.72 us -> 4.05 us
  Pallas kernels: 8.62 us -> 7.15 us
  starting transfers between devices: 9.59 us -> 8.32 us
    ppermute x2 -> x1, waiting for transfers between devices: 1.24 us -> 3.56 us  [body(): halo = lax.ppermute(own, 'ctx', swap)]
    ppermute x1, starting transfers between devices: 2.01 us -> 0.05 us  [body(): other = lax.ppermute(mine, 'ctx', swap)]
    pallas_call x3, Pallas kernels: 5.84 us -> 3.96 us  [the longest x1 2.78 us: pair_outputs(): pl.pallas_call(functools.partial(pair_kernel, channels // held[5].shape[0...]
    ppermute x3, starting transfers between devices: 4.49 us -> 5.26 us  [gather_terms(): lax.ppermute(sums, axis, list(enumerate(targets)))]
    pallas_call x1, Pallas kernels: 1.17 us -> 1.44 us  [own_block(): pl.pallas_call(own_kernel, in_specs=[pl.BlockSpec(memory_space=pltpu.HBM)...]
    ppermute x2 -> x1, starting transfers between devices: 3.09 us -> 3.01 us  [body(): halo = lax.ppermute(own, 'ctx', swap)]
  transfers between devices with their start and end apart: 6 -> 5, of which waited for: 3 -> 3; matrix products, arithmetic and copies ran while one was open for 0% -> 0% of each run, Pallas kernels for 30% -> 25%
where the time goes in v6:
time: 20.4 us; the launch traced here: 20.2 us
  starting transfers between devices  8.32 us (41%)
  Pallas kernels  7.15 us (35%)
  waiting for transfers between devices  4.05 us (20%)
  between operations  0.69 us (3%)
    ppermute x3, starting transfers between devices, gather_terms(): lax.ppermute(sums, axis, list(enumerate(targets)))  5.26 us
    ppermute x1, waiting for transfers between devices, body(): halo = lax.ppermute(own, 'ctx', swap)  3.56 us
    ppermute x1, starting transfers between devices, body(): halo = lax.ppermute(own, 'ctx', swap)  3.01 us
    pallas_call x1, Pallas kernels, pair_outputs(): pl.pallas_call(functools.partial(pair_kernel, channels // held[5].shape[0...  2.78 us
    pallas_call x1, Pallas kernels, own_block(): pl.pallas_call(own_kernel, in_specs=[pl.BlockSpec(memory_space=pltpu.HBM)...  1.44 us
    pallas_call x2, Pallas kernels, local_sums(): pl.pallas_call(functools.partial(local_kernel, channels // groups, turn),...  1.18 us
    pallas_call x1, Pallas kernels, cross_sums(): pl.pallas_call(functools.partial(cross_kernel, channels // groups, swap),...  1.1 us
    pallas_call x1, Pallas kernels, totals(): pl.pallas_call(functools.partial(total_kernel, groups, tap_scale, skip_sc...  0.65 us
  transfers between devices with their start and end apart: 5, of which 3 were waited for; matrix products, arithmetic and copies ran while one was open for 0% of the time, Pallas kernels for 25%

profile of v6, /device:TPU:0, one launch (start us, length us, event | category | flops | bytes accessed | tf_op | source)
XLA Modules:
  0.0 20.2 jit_solution(17413400225856315436)
XLA Ops:
  0.6 1.4 %own_block.1 = (bf16[1024,128]{1,0:T(8,128)(2,1)S(1)}, s32[1,128]{1,0:T(1,128)S(1)}, bf16[1024,128]{1,0:T(8,128)(2,1)S(1)}, bf16[1024,128]{1,0:T(8,128)(2,1)S(1)...) custom-call(s32[1,128]{1,0:T(1,128)} %refs_0_.1, ...), custom_call_target="tpu_custom_call" | custom-call | tf_op jit(solution)/shard_map/own_block/pallas_call | solution.py:119
  2.1 0.1 local_sums.2
  2.1 3.0 %collective-permute-start = (bf16[1024,128]{1,0:T(8,128)(2,1)S(1)}, bf16[1024,128]{1,0:T(8,128)(2,1)S(1)}, u32[]{:S(2)}, u32[]{:S(2)}) collective-permute-start(bf16[1024,128]{1,0:T(8,128)(2,1)S(1)} %get-tuple-element.48.own_ref), channel_id=1, source_target_pairs={{0,16},{16,0},{1,17},{17,1},{2,18},{18,2},{3,19},{19,3},{4,20},{20... | collective-permute-start | bytes 786440 | tf_op jit(solution)/shard_map/ppermute | solution.py:442
  5.2 1.1 %local_sums.3 = bf16[72,128]{1,0:T(8,128)(2,1)S(1)} custom-call(s32[1,128]{1,0:T(1,128)S(1)} %get-tuple-element.39.refs_0_, bf16[1024,128]{1,0:T(8,128)(2,1)S(1)} %get-tuple-element.40.refs_1_, bf16[1024,128]{1,0:T(8,128)(2,1)S(1)} %get-tuple-element.41.refs_2_, bf16[1024,128]{1,0:T(8,128)(2,1)S(1)} %get-tuple-element.42.refs_3_, ...), custom_call_target="tpu_custom_call", output_to_operand_aliasing={{}: (7, {})} | custom-call | flops 67108864 | bytes 8388608 | tf_op jit(solution)/shard_map/local_sums/pallas_call | solution.py:169
  6.3 0.0 collective-permute-start.1
  6.3 3.6 %collective-permute-done.refs_7_.halo_ref = bf16[1024,128]{1,0:T(8,128)(2,1)S(1)} collective-permute-done((bf16[1024,128]{1,0:T(8,128)(2,1)S(1)}, bf16[1024,128]{1,0:T(8,128)(2,1)S(1)}, u32[]{:S(2)}, u32[]{:S(2)}) %collective-permute-start) | collective-permute-done | bytes 262176 | tf_op jit(solution)/shard_map/ppermute | solution.py:442
  9.9 1.1 %cross_sums.1 = f32[64,128]{1,0:T(8,128)S(1)} custom-call(bf16[1024,128]{1,0:T(8,128)(2,1)S(1)} %get-tuple-element.48.own_ref, bf16[1024,128]{1,0:T(8,128)(2,1)S(1)} %collective-permute-done.refs_7_.halo_ref), custom_call_target="tpu_custom_call" | custom-call | flops 67108864 | bytes 8388608 | tf_op jit(solution)/shard_map/cross_sums/pallas_call | solution.py:199
  11.0 0.0 collective-permute-done.1
  11.0 3.7 %collective-permute-start.2 = (bf16[72,128]{1,0:T(8,128)(2,1)S(1)}, bf16[72,128]{1,0:T(8,128)(2,1)S(1)}, u32[]{:S(2)}, u32[]{:S(2)}) collective-permute-start(bf16[72,128]{1,0:T(8,128)(2,1)S(1)} %reduce-precision_convert_fusion.refs_0_), channel_id=1, source_target_pairs={{0,8},{4,12},{8,4},{12,0},{1,9},{5,13},{9,5},{13,1},{2,10},{6,14},... | collective-permute-start | bytes 55304 | tf_op jit(solution)/shard_map/ppermute | solution.py:389
  14.7 1.1 %collective-permute-start.3 = (bf16[72,128]{1,0:T(8,128)(2,1)S(1)}, bf16[72,128]{1,0:T(8,128)(2,1)S(1)}, u32[]{:S(2)}, u32[]{:S(2)}) collective-permute-start(bf16[72,128]{1,0:T(8,128)(2,1)S(1)} %reduce-precision_convert_fusion.refs_0_), channel_id=1, source_target_pairs={{0,12},{4,8},{8,0},{12,4},{1,13},{5,9},{9,1},{13,5},{2,14},{6,10},... | collective-permute-start | bytes 55304 | tf_op jit(solution)/shard_map/ppermute | solution.py:389
  15.8 0.5 %collective-permute-start.4 = (bf16[72,128]{1,0:T(8,128)(2,1)S(1)}, bf16[72,128]{1,0:T(8,128)(2,1)S(1)}, u32[]{:S(2)}, u32[]{:S(2)}) collective-permute-start(bf16[72,128]{1,0:T(8,128)(2,1)S(1)} %reduce-precision_convert_fusion.refs_0_), channel_id=1, source_target_pairs={{0,4},{4,0},{8,12},{12,8},{1,5},{5,1},{9,13},{13,9},{2,6},{6,2},{1... | collective-permute-start | bytes 55304 | tf_op jit(solution)/shard_map/ppermute | solution.py:389
  16.3 2.8 %pair_outputs.1 = (bf16[1024,128]{1,0:T(8,128)(2,1)}, bf16[1024,128]{1,0:T(8,128)(2,1)}, bf16[1024,128]{1,0:T(8,128)(2,1)}, bf16[1024,128]{1,0:T(8,128)(2,1)}) custom-call(s32[1,128]{1,0:T(1,128)S(1)} %get-tuple-element.39.refs_0_, ...), custom_call_target="tpu_custom_call", output_to_operand_aliasing={{0}: (8, {}), {1}: (9, {}), {2}: (10, {}), {3}: (11, {})} | custom-call | flops 268435456 | bytes 8388608 | tf_op jit(solution)/shard_map/pair_outputs/pallas_call | solution.py:367
  19.1 0.0 collective-permute-done.2.refs_1_
  19.1 0.3 %collective-permute-done.3.refs_2_ = bf16[72,128]{1,0:T(8,128)(2,1)S(1)} collective-permute-done((bf16[72,128]{1,0:T(8,128)(2,1)S(1)}, bf16[72,128]{1,0:T(8,128)(2,1)S(1)}, u32[]{:S(2)}, u32[]{:S(2)}) %collective-permute-start.3) | collective-permute-done | bytes 18464 | tf_op jit(solution)/shard_map/ppermute | solution.py:389
  19.4 0.2 collective-permute-done.4.refs_3_
  19.6 0.6 %totals.1 = (f32[64,128]{1,0:T(8,128)}, f32[8,128]{1,0:T(8,128)}) custom-call(bf16[72,128]{1,0:T(8,128)(2,1)S(1)} %reduce-precision_convert_fusion.refs_0_, bf16[72,128]{1,0:T(8,128)(2,1)S(1)} %collective-permute-done.2.refs_1_, bf16[72,128]{1,0:T(8,128)(2,1)S(1)} %collective-permute-done.3.refs_2_, bf16[72,128]{1,0:T(8,128)(2,1)S(1)} %collective-permute-done.4.refs_3_), custom_call_target="tpu_custom_call" | custom-call | tf_op jit(solution)/shard_map/totals/pallas_call | solution.py:414
  (3 shorter events, 0.0 us)
Async XLA Ops:
  2.1 7.8 %collective-permute-start = (bf16[1024,128]{1,0:T(8,128)(2,1)S(1)}, bf16[1024,128]{1,0:T(8,128)(2,1)S(1)}, u32[]{:S(2)}, u32[]{:S(2)}) collective-permute-start(bf16[1024,128]{1,0:T(8,128)(2,1)S(1)} %get-tuple-element.48.own_ref), channel_id=1, source_target_pairs={{0,16},{16,0},{1,17},{17,1},{2,18},{18,2},{3,19},{19,3},{4,20},{20... | collective-permute-start | bytes 786440 | tf_op jit(solution)/shard_map/ppermute | solution.py:442
  6.3 4.7 %collective-permute-start.1 = (bf16[72,128]{1,0:T(8,128)(2,1)S(1)}, bf16[72,128]{1,0:T(8,128)(2,1)S(1)}, u32[]{:S(2)}, u32[]{:S(2)}) collective-permute-start(bf16[72,128]{1,0:T(8,128)(2,1)S(1)} %local_sums.3), channel_id=1, source_target_pairs={{0,16},{16,0},{1,17},{17,1},{2,18},{18,2},{3,19},{19,3},{4,20},{20... | collective-permute-start | bytes 55304 | tf_op jit(solution)/shard_map/ppermute | solution.py:444
  11.0 8.0 %collective-permute-start.2 = (bf16[72,128]{1,0:T(8,128)(2,1)S(1)}, bf16[72,128]{1,0:T(8,128)(2,1)S(1)}, u32[]{:S(2)}, u32[]{:S(2)}) collective-permute-start(bf16[72,128]{1,0:T(8,128)(2,1)S(1)} %reduce-precision_convert_fusion.refs_0_), channel_id=1, source_target_pairs={{0,8},{4,12},{8,4},{12,0},{1,9},{5,13},{9,5},{13,1},{2,10},{6,14},... | collective-permute-start | bytes 55304 | tf_op jit(solution)/shard_map/ppermute | solution.py:389
  14.7 4.7 %collective-permute-start.3 = (bf16[72,128]{1,0:T(8,128)(2,1)S(1)}, bf16[72,128]{1,0:T(8,128)(2,1)S(1)}, u32[]{:S(2)}, u32[]{:S(2)}) collective-permute-start(bf16[72,128]{1,0:T(8,128)(2,1)S(1)} %reduce-precision_convert_fusion.refs_0_), channel_id=1, source_target_pairs={{0,12},{4,8},{8,0},{12,4},{1,13},{5,9},{9,1},{13,5},{2,14},{6,10},... | collective-permute-start | bytes 55304 | tf_op jit(solution)/shard_map/ppermute | solution.py:389
  15.8 3.8 %collective-permute-start.4 = (bf16[72,128]{1,0:T(8,128)(2,1)S(1)}, bf16[72,128]{1,0:T(8,128)(2,1)S(1)}, u32[]{:S(2)}, u32[]{:S(2)}) collective-permute-start(bf16[72,128]{1,0:T(8,128)(2,1)S(1)} %reduce-precision_convert_fusion.refs_0_), channel_id=1, source_target_pairs={{0,4},{4,0},{8,12},{12,8},{1,5},{5,1},{9,13},{13,9},{2,6},{6,2},{1... | collective-permute-start | bytes 55304 | tf_op jit(solution)/shard_map/ppermute | solution.py:389

commit v7 on v6

--- a/solution.py
+++ b/solution.py
@@ -73,73 +73,117 @@
 
 
 def own_kernel(*refs):
-    sources, own_ref, held, sems = refs[:7], refs[7], refs[8:15], refs[15]
+    sources, own_ref, held, sems = refs[:5], refs[5], refs[6:13], refs[13]
     first = lax.axis_index("ctx") == 0
-    keep_ref = held[0]
     channels = own_ref.shape[0]
-
-    def run(one, two, others, masked):
-        copies = {
-            (index, part): pltpu.make_async_copy(
-                sources[index].at[pl.ds(part * channels // PARTS, channels // PARTS)],
-                held[index].at[pl.ds(part * channels // PARTS, channels // PARTS)],
-                sems.at[index * PARTS + part],
-            )
-            for index in (one, two)
-            for part in range(PARTS)
-        }
-        for index in (0, *others):
-            copies[index, 0] = pltpu.make_async_copy(
-                sources[index], held[index], sems.at[index * PARTS]
-            )
-        copies[0, 0].start()
+    rows = channels // PARTS
+
+    def run(one, two, masked):
+        def copies_of(part):
+            window = pl.ds(part * rows, rows)
+            return [
+                pltpu.make_async_copy(
+                    sources[index].at[window], held[index].at[window], sems.at[2 * part + side]
+                )
+                for side, index in enumerate((one, two))
+            ]
+
+        keep_copy = pltpu.make_async_copy(sources[0], held[0], sems.at[2 * PARTS])
+        keep_copy.start()
         for part in range(PARTS):
-            copies[one, part].start()
-            copies[two, part].start()
-        for index in others:
-            copies[index, 0].start()
-        copies[0, 0].wait()
+            for copy in copies_of(part):
+                copy.start()
+        keep_copy.wait()
         for part in range(PARTS):
-            copies[one, part].wait()
-            copies[two, part].wait()
-            window = pl.ds(part * channels // PARTS, channels // PARTS)
+            for copy in copies_of(part):
+                copy.wait()
+            window = pl.ds(part * rows, rows)
             scaled = held[two][window].astype(F32)
             if masked:
-                scaled = scaled * keep_ref[...].astype(F32)
+                scaled = scaled * held[0][...].astype(F32)
             own_ref[window] = (scaled * held[one][window].astype(F32)).astype(BF16)
-        for index in others:
-            copies[index, 0].wait()
-
-    pl.when(first)(functools.partial(run, 2, 3, (1, 4, 5, 6), False))
-    pl.when(jnp.logical_not(first))(functools.partial(run, 1, 4, (2, 3, 5, 6), True))
+
+    pl.when(first)(functools.partial(run, 2, 3, False))
+    pl.when(jnp.logical_not(first))(functools.partial(run, 1, 4, True))
 
 
 def own_block(*sources):
     whole = pl.BlockSpec(memory_space=pltpu.VMEM)
     return pl.pallas_call(
         own_kernel,
-        in_specs=[pl.BlockSpec(memory_space=pltpu.HBM)] * 7,
+        in_specs=[pl.BlockSpec(memory_space=pltpu.HBM)] * 5,
         out_specs=[whole] * 8,
         out_shape=[pltpu.VMEM(sources[1].shape, BF16)]
         + [pltpu.VMEM(source.shape, source.dtype) for source in sources],
-        scratch_shapes=[pltpu.SemaphoreType.DMA((7 * PARTS,))],
+        scratch_shapes=[pltpu.SemaphoreType.DMA((2 * PARTS + 1,))],
         compiler_params=pltpu.CompilerParams(vmem_limit_bytes=12 * 2**20),
         name="own_block",
-    )(*map(in_hbm, sources))
-
-
-def local_kernel(per_group, turn, *refs):
-    held, sums_ref = refs[:7], refs[7 if turn != 1 else 8]
-    sum_local = functools.partial(local_part, per_group, held, sums_ref)
-    if turn is None:
-        sum_local()
-        return
+    )(*map(in_hbm, sources[:5]))
+
+
+def turn_kernel(per_group, turn, *refs):
+    sources = refs[:6]
+    if turn == 0:
+        held, sums_ref, out_refs = refs[13:20], refs[20], refs[21:25]
+        sems, made_refs, out_sems = refs[25], refs[26:28], refs[28]
+    else:
+        held, sums_ref, sems = refs[14:21], refs[21], refs[22]
+    query, key, value, grad, taps, skips = zip(sources, held[1:])
+
+    def load(*pairs):
+        return [
+            pltpu.make_async_copy(source, target, sems.at[index])
+            for index, (source, target) in enumerate(pairs)
+        ]
 
     @pl.when(lax.axis_index("tp") % 2 == 1 - turn)
     def _():
-        sum_local()
+        first = lax.axis_index("ctx") == 0
+
+        @pl.when(first)
+        def _():
+            for copy in load(query, grad, taps, skips):
+                copy.start()
+
+        @pl.when(jnp.logical_not(first))
+        def _():
+            for copy in load(key, value, taps, skips):
+                copy.start()
+
+        for copy in load(key, value, taps, skips):
+            copy.wait()
+        local_part(per_group, held, sums_ref)
         if turn == 0:
-            filters(per_group, held, None, refs[8:12], refs[12:14], refs[14], "free")
+            bounds = (0, 3 * held[5].shape[0] // 8, 3 * held[5].shape[0] // 4)
+            filters(per_group, held, None, out_refs, made_refs, out_sems, [("free", bounds)])
+
+
+def turn_sums(turn, sources, held, made=()):
+    channels, length = held[1].shape
+    groups = held[5].shape[0]
+    whole = pl.BlockSpec(memory_space=pltpu.VMEM)
+    hbm = pl.BlockSpec(memory_space=pltpu.HBM)
+    free = turn == 0
+    given = (*held, *made)
+    return pl.pallas_call(
+        functools.partial(turn_kernel, channels // groups, turn),
+        in_specs=[hbm] * 6 + [whole] * len(given),
+        out_specs=[whole] * 8 + [hbm] * (4 * free),
+        out_shape=[pltpu.VMEM(array.shape, array.dtype) for array in held]
+        + [pltpu.VMEM((groups + channels // length, length), BF16)]
+        + [jax.ShapeDtypeStruct((channels, length), BF16)] * (4 * free),
+        input_output_aliases={6 + index: index for index in range(len(given))},
+        scratch_shapes=[pltpu.SemaphoreType.DMA((4,))]
+        + [pltpu.VMEM((channels, length), BF16)] * (2 * free)
+        + [pltpu.SemaphoreType.DMA((8,))] * free,
+        cost_estimate=pl.CostEstimate(flops=2**26, bytes_accessed=2**23, transcendentals=0),
+        compiler_params=pltpu.CompilerParams(vmem_limit_bytes=12 * 2**20),
+        name="turn_sums",
+    )(*map(in_hbm, sources[1:]), *map(in_vmem, given))
+
+
+def local_kernel(per_group, *refs):
+    local_part(per_group, refs[:5], refs[5])
 
 
 def local_part(per_group, held, sums_ref):
@@ -162,23 +206,14 @@
         ].astype(sums_ref.dtype)
 
 
-def local_sums(groups, dtype, held, turn=None, made=()):
-    channels, length = held[1].shape
-    whole = pl.BlockSpec(memory_space=pltpu.VMEM)
-    free = turn == 0
-    return pl.pallas_call(
-        functools.partial(local_kernel, channels // groups, turn),
-        in_specs=[whole] * (7 + len(made)),
-        out_specs=[whole] + [pl.BlockSpec(memory_space=pltpu.HBM)] * (4 * free),
-        out_shape=[pltpu.VMEM((groups + channels // length, length), dtype)]
-        + [jax.ShapeDtypeStruct((channels, length), BF16)] * (4 * free),
-        input_output_aliases={7 + index: index for index in range(len(made))},
-        scratch_shapes=[pltpu.VMEM((channels, length), BF16)] * (2 * free)
-        + [pltpu.SemaphoreType.DMA((2 * PARTS,))] * free,
+def local_sums(groups, *arrays):
+    channels, length = arrays[1].shape
+    return pl.pallas_call(
+        functools.partial(local_kernel, channels // groups),
+        out_shape=jax.ShapeDtypeStruct((groups + channels // length, length), F32),
         cost_estimate=pl.CostEstimate(flops=2**26, bytes_accessed=2**23, transcendentals=0),
-        compiler_params=pltpu.CompilerParams(vmem_limit_bytes=12 * 2**20),
         name="local_sums",
-    )(*map(in_vmem, (*held, *made)))
+    )(*arrays)
 
 
 def by_role(own, halo):
@@ -273,41 +308,37 @@
     )(keep, taps, skip_rows, query, key, value, grad, before, following)
 
 
-def row_copies(part, made_refs, out_refs, sems):
-    rows = made_refs[0].shape[0] // PARTS
-    window = pl.ds(part * rows, rows)
-    return [
-        pltpu.make_async_copy(
-            made.at[window], out.at[window], sems.at[part * len(out_refs) + side]
-        )
-        for side, (made, out) in enumerate(zip(made_refs, out_refs))
-    ]
-
-
-def filters(per_group, held, halo_ref, out_refs, made_refs, sems, chosen):
+def filters(per_group, held, halo_ref, out_refs, made_refs, sems, tasks):
     first = lax.axis_index("ctx") == 0
-    for here, place in ((True, first), (False, jnp.logical_not(first))):
-        forward = chosen == "all" or (chosen == "free") == here
-        backward = chosen == "all" or (chosen == "free") != here
-        pl.when(place)(
-            functools.partial(
-                filter_groups, per_group, held, halo_ref, out_refs, made_refs, sems, here, forward, backward
+
+    def run(here):
+        copies = []
+        for index, (chosen, bounds) in enumerate(tasks):
+            forward = chosen == "all" or (chosen == "free") == here
+            backward = chosen == "all" or (chosen == "free") != here
+            copies += filter_groups(
+                per_group, held, halo_ref, out_refs, made_refs, sems, here, forward, backward, bounds, 8 * index
             )
-        )
-
-
-def filter_groups(per_group, held, halo_ref, out_refs, made_refs, sems, first, forward, backward):
+        for copy in copies:
+            copy.wait()
+
+    pl.when(first)(functools.partial(run, True))
+    pl.when(jnp.logical_not(first))(functools.partial(run, False))
+
+
+def filter_groups(
+    per_group, held, halo_ref, out_refs, made_refs, sems, first, forward, backward, bounds, sem
+):
     keep_ref, query_ref, key_ref, value_ref, grad_ref, tap_ref, skip_ref = held
     out_refs = out_refs[0 if forward else 2 : 4 if backward else 2]
     made_refs = made_refs[: len(out_refs)]
-    channels, length = query_ref.shape
-    groups = channels // per_group
-    size = groups // PARTS
+    length = query_ref.shape[1]
     row, column = iotas(length, length)
     causal = column >= row
     keep = keep_ref[...].astype(F32)
     skips = skip_ref[...].T
-    for group in range(groups):
+    copies = []
+    for group in range(bounds[0], bounds[-1]):
         start = group * per_group
         part = slice(start, start + per_group)
         query = query_ref[part].astype(F32)
@@ -344,21 +375,26 @@
             results += [joined_grad * value, joined_grad * key]
         for made, result in zip(made_refs, results):
             made[part] = result.astype(BF16)
-        if (group + 1) % size == 0:
-            for copy in row_copies(group // size, made_refs, out_refs, sems):
-                copy.start()
-    for part in range(PARTS):
-        for copy in row_copies(part, made_refs, out_refs, sems):
-            copy.wait()
+        if group + 1 in bounds:
+            begin = bounds[bounds.index(group + 1) - 1] * per_group
+            window = pl.ds(begin, start + per_group - begin)
+            for made, out in zip(made_refs, out_refs):
+                copies.append(
+                    pltpu.make_async_copy(made.at[window], out.at[window], sems.at[sem + len(copies)])
+                )
+                copies[-1].start()
+    return copies
 
 
 def pair_kernel(per_group, *refs):
     held, halo_ref, out_refs = refs[:7], refs[7], refs[12:16]
     made_refs, sems = refs[16:20], refs[20]
+    groups = held[5].shape[0]
     even = lax.axis_index("tp") % 2 == 0
     rest = (per_group, held, halo_ref, out_refs, made_refs, sems)
-    pl.when(even)(functools.partial(filters, *rest, "all"))
-    pl.when(jnp.logical_not(even))(functools.partial(filters, *rest, "bound"))
+    pl.when(even)(functools.partial(filters, *rest, [("all", (0, groups // 2, groups))]))
+    tasks = [("bound", (0, 3 * groups // 8, 3 * groups // 4)), ("all", (3 * groups // 4, groups))]
+    pl.when(jnp.logical_not(even))(functools.partial(filters, *rest, tasks))
 
 
 def pair_outputs(held, halo, results):
@@ -371,7 +407,7 @@
         out_shape=[jax.ShapeDtypeStruct((channels, length), BF16)] * 4,
         input_output_aliases={8: 0, 9: 1, 10: 2, 11: 3},
         scratch_shapes=[pltpu.VMEM((channels, length), BF16)] * 4
-        + [pltpu.SemaphoreType.DMA((4 * PARTS,))],
+        + [pltpu.SemaphoreType.DMA((16,))],
         cost_estimate=pl.CostEstimate(flops=2**28, bytes_accessed=2**23, transcendentals=0),
         compiler_params=pltpu.CompilerParams(vmem_limit_bytes=12 * 2**20),
         name="pair_outputs",
@@ -436,25 +472,24 @@
     if shards == 2:
         swap = [(0, 1), (1, 0)]
         skips = skip_gain.reshape(channels // length, length)
-        own, *held = own_block(keep_mask, query, key, value, grad, filter_taps, skips)
-        mine, *free = local_sums(groups, BF16, held, 0)
-        own, mine = lax.optimization_barrier((own, mine))
+        sources = (keep_mask, query, key, value, grad, filter_taps, skips)
+        own, *held = own_block(*sources)
+        made = turn_sums(0, sources, held)
+        own, made = lax.optimization_barrier((own, made))
         halo = lax.ppermute(own, "ctx", swap)
-        (mine,) = local_sums(groups, BF16, held, 1, (mine,))
+        *held, mine = turn_sums(1, sources, made[:7], made[7:8])
         other = lax.ppermute(mine, "ctx", swap)
         crossed = cross_sums(own, halo, groups, True)
         sums = mine.astype(F32).at[:groups].add(crossed) + other.astype(F32)
         sums = lax.reduce_precision(sums, 8, 7).astype(BF16)
         terms = gather_terms(sums, "dp")
-        results = pair_outputs(held, halo, free)
+        results = pair_outputs(held, halo, made[8:])
     else:
         joined = (key.astype(F32) * value.astype(F32)).astype(BF16)
         own = (grad.astype(F32) * keep_mask.astype(F32) * query.astype(F32)).astype(BF16)
         before = lax.ppermute(joined, "ctx", [(i, i + 1) for i in range(shards - 1)])
         following = lax.ppermute(own, "ctx", [(i + 1, i) for i in range(shards - 1)])
-        skips = skip_gain.reshape(channels // length, length)
-        sources = (keep_mask, query, key, value, grad, filter_taps, skips)
-        (mine,) = local_sums(groups, F32, sources)
+        mine = local_sums(groups, keep_mask, query, key, value, grad)
         crossed = cross_sums(own, before, groups, False)
         sums = lax.psum(mine.at[:groups].add(crossed), "ctx")
         terms = gather_terms(sums, "dp")

time: 20.4 us -> 20.3 us (level)
  the two profiles are of different devices: /device:TPU:0 before, /device:TPU:1 now
where the time goes in v7:
time: 20.3 us; the launch traced here: 20.1 us
  Pallas kernels  9.06 us (45%)
  starting transfers between devices  6.44 us (32%)
  waiting for transfers between devices  3.87 us (19%)
  between operations  0.7 us (3%)
    ppermute x3, starting transfers between devices, gather_terms(): lax.ppermute(sums, axis, list(enumerate(targets)))  3.89 us
    ppermute x1, waiting for transfers between devices, body(): halo = lax.ppermute(own, 'ctx', swap)  3.81 us
    pallas_call x2, Pallas kernels, turn_sums(): pl.pallas_call(functools.partial(turn_kernel, channels // groups, turn),...  3.79 us
    ppermute x1, starting transfers between devices, body(): halo = lax.ppermute(own, 'ctx', swap)  2.44 us
    pallas_call x1, Pallas kernels, pair_outputs(): pl.pallas_call(functools.partial(pair_kernel, channels // held[5].shape[0...  2.33 us
    pallas_call x1, Pallas kernels, own_block(): pl.pallas_call(own_kernel, in_specs=[pl.BlockSpec(memory_space=pltpu.HBM)...  1.2 us
    pallas_call x1, Pallas kernels, cross_sums(): pl.pallas_call(functools.partial(cross_kernel, channels // groups, swap),...  1.1 us
    pallas_call x1, Pallas kernels, totals(): pl.pallas_call(functools.partial(total_kernel, groups, tap_scale, skip_sc...  0.65 us
  transfers between devices with their start and end apart: 5, of which 2 were waited for; matrix products, arithmetic and copies ran while one was open for 0% of the time, Pallas kernels for 17%

profile of v7, /device:TPU:1, one launch (start us, length us, event | category | flops | bytes accessed | tf_op | source)
XLA Modules:
  0.0 20.1 jit_solution(11794842008332336537)
XLA Ops:
  0.6 1.2 %own_block.1 = (bf16[1024,128]{1,0:T(8,128)(2,1)S(1)}, s32[1,128]{1,0:T(1,128)S(1)}, bf16[1024,128]{1,0:T(8,128)(2,1)S(1)}, bf16[1024,128]{1,0:T(8,128)(2,1)S(1)...) custom-call(s32[1,128]{1,0:T(1,128)} %refs_0_.1, ...), custom_call_target="tpu_custom_call" | custom-call | tf_op jit(solution)/shard_map/own_block/pallas_call | solution.py:112
  1.8 3.8 %turn_sums.2 = (s32[1,128]{1,0:T(1,128)S(1)}, bf16[1024,128]{1,0:T(8,128)(2,1)S(1)}, bf16[1024,128]{1,0:T(8,128)(2,1)S(1)}, bf16[1024,128]{1,0:T(8,128)(2,1)S(1)...) custom-call(bf16[1024,128]{1,0:T(8,128)(2,1)} %bitcast.11, ...), custom_call_target="tpu_custom_call", output_to_operand_aliasing={{0}: (6, {}), {1}: (7, {}), {2}: (8, {}), {3}: (9, {}), {4}... | custom-call | flops 67108864 | bytes 8388608 | tf_op jit(solution)/shard_map/turn_sums/pallas_call | solution.py:168
  5.6 2.4 %collective-permute-start = (bf16[1024,128]{1,0:T(8,128)(2,1)S(1)}, bf16[1024,128]{1,0:T(8,128)(2,1)S(1)}, u32[]{:S(2)}, u32[]{:S(2)}) collective-permute-start(bf16[1024,128]{1,0:T(8,128)(2,1)S(1)} %get-tuple-element.100.own_ref), channel_id=1, source_target_pairs={{0,16},{16,0},{1,17},{17,1},{2,18},{18,2},{3,19},{19,3},{4,20},{20... | collective-permute-start | bytes 786440 | tf_op jit(solution)/shard_map/ppermute | solution.py:479
  8.1 0.1 collective-permute-start.1
  8.2 3.8 %collective-permute-done.refs_7_.halo_ref = bf16[1024,128]{1,0:T(8,128)(2,1)S(1)} collective-permute-done((bf16[1024,128]{1,0:T(8,128)(2,1)S(1)}, bf16[1024,128]{1,0:T(8,128)(2,1)S(1)}, u32[]{:S(2)}, u32[]{:S(2)}) %collective-permute-start) | collective-permute-done | bytes 262176 | tf_op jit(solution)/shard_map/ppermute | solution.py:479
  12.0 1.1 %cross_sums.1 = f32[64,128]{1,0:T(8,128)S(1)} custom-call(bf16[1024,128]{1,0:T(8,128)(2,1)S(1)} %get-tuple-element.100.own_ref, bf16[1024,128]{1,0:T(8,128)(2,1)S(1)} %collective-permute-done.refs_7_.halo_ref), custom_call_target="tpu_custom_call" | custom-call | flops 67108864 | bytes 8388608 | tf_op jit(solution)/shard_map/cross_sums/pallas_call | solution.py:234
  13.1 0.0 collective-permute-done.1
  13.1 2.6 %collective-permute-start.2 = (bf16[72,128]{1,0:T(8,128)(2,1)S(1)}, bf16[72,128]{1,0:T(8,128)(2,1)S(1)}, u32[]{:S(2)}, u32[]{:S(2)}) collective-permute-start(bf16[72,128]{1,0:T(8,128)(2,1)S(1)} %reduce-precision_convert_fusion.refs_0_), channel_id=1, source_target_pairs={{0,8},{4,12},{8,4},{12,0},{1,9},{5,13},{9,5},{13,1},{2,10},{6,14},... | collective-permute-start | bytes 55304 | tf_op jit(solution)/shard_map/ppermute | solution.py:425
  15.7 1.1 %collective-permute-start.3 = (bf16[72,128]{1,0:T(8,128)(2,1)S(1)}, bf16[72,128]{1,0:T(8,128)(2,1)S(1)}, u32[]{:S(2)}, u32[]{:S(2)}) collective-permute-start(bf16[72,128]{1,0:T(8,128)(2,1)S(1)} %reduce-precision_convert_fusion.refs_0_), channel_id=1, source_target_pairs={{0,12},{4,8},{8,0},{12,4},{1,13},{5,9},{9,1},{13,5},{2,14},{6,10},... | collective-permute-start | bytes 55304 | tf_op jit(solution)/shard_map/ppermute | solution.py:425
  16.8 0.2 %collective-permute-start.4 = (bf16[72,128]{1,0:T(8,128)(2,1)S(1)}, bf16[72,128]{1,0:T(8,128)(2,1)S(1)}, u32[]{:S(2)}, u32[]{:S(2)}) collective-permute-start(bf16[72,128]{1,0:T(8,128)(2,1)S(1)} %reduce-precision_convert_fusion.refs_0_), channel_id=1, source_target_pairs={{0,4},{4,0},{8,12},{12,8},{1,5},{5,1},{9,13},{13,9},{2,6},{6,2},{1... | collective-permute-start | bytes 55304 | tf_op jit(solution)/shard_map/ppermute | solution.py:425
  17.0 2.3 %pair_outputs.1 = (bf16[1024,128]{1,0:T(8,128)(2,1)}, bf16[1024,128]{1,0:T(8,128)(2,1)}, bf16[1024,128]{1,0:T(8,128)(2,1)}, bf16[1024,128]{1,0:T(8,128)(2,1)}) custom-call(s32[1,128]{1,0:T(1,128)S(1)} %get-tuple-element.93.refs_0_, ...), custom_call_target="tpu_custom_call", output_to_operand_aliasing={{0}: (8, {}), {1}: (9, {}), {2}: (10, {}), {3}: (11, {})} | custom-call | flops 268435456 | bytes 8388608 | tf_op jit(solution)/shard_map/pair_outputs/pallas_call | solution.py:403
  19.4 0.0 collective-permute-done.2.refs_1_
  19.4 0.0 collective-permute-done.3.refs_2_
  19.4 0.1 collective-permute-done.4.refs_3_
  19.4 0.6 %totals.1 = (f32[64,128]{1,0:T(8,128)}, f32[8,128]{1,0:T(8,128)}) custom-call(bf16[72,128]{1,0:T(8,128)(2,1)S(1)} %reduce-precision_convert_fusion.refs_0_, bf16[72,128]{1,0:T(8,128)(2,1)S(1)} %collective-permute-done.2.refs_1_, bf16[72,128]{1,0:T(8,128)(2,1)S(1)} %collective-permute-done.3.refs_2_, bf16[72,128]{1,0:T(8,128)(2,1)S(1)} %collective-permute-done.4.refs_3_), custom_call_target="tpu_custom_call" | custom-call | tf_op jit(solution)/shard_map/totals/pallas_call | solution.py:450
  (4 shorter events, 0.1 us)
Async XLA Ops:
  5.6 6.4 %collective-permute-start = (bf16[1024,128]{1,0:T(8,128)(2,1)S(1)}, bf16[1024,128]{1,0:T(8,128)(2,1)S(1)}, u32[]{:S(2)}, u32[]{:S(2)}) collective-permute-start(bf16[1024,128]{1,0:T(8,128)(2,1)S(1)} %get-tuple-element.100.own_ref), channel_id=1, source_target_pairs={{0,16},{16,0},{1,17},{17,1},{2,18},{18,2},{3,19},{19,3},{4,20},{20... | collective-permute-start | bytes 786440 | tf_op jit(solution)/shard_map/ppermute | solution.py:479
  8.1 5.0 %collective-permute-start.1 = (bf16[72,128]{1,0:T(8,128)(2,1)S(1)}, bf16[72,128]{1,0:T(8,128)(2,1)S(1)}, u32[]{:S(2)}, u32[]{:S(2)}) collective-permute-start(bf16[72,128]{1,0:T(8,128)(2,1)S(1)} %get-tuple-element.109), channel_id=1, source_target_pairs={{0,16},{16,0},{1,17},{17,1},{2,18},{18,2},{3,19},{19,3},{4,20},{20... | collective-permute-start | bytes 55304 | tf_op jit(solution)/shard_map/ppermute | solution.py:481
  13.1 6.2 %collective-permute-start.2 = (bf16[72,128]{1,0:T(8,128)(2,1)S(1)}, bf16[72,128]{1,0:T(8,128)(2,1)S(1)}, u32[]{:S(2)}, u32[]{:S(2)}) collective-permute-start(bf16[72,128]{1,0:T(8,128)(2,1)S(1)} %reduce-precision_convert_fusion.refs_0_), channel_id=1, source_target_pairs={{0,8},{4,12},{8,4},{12,0},{1,9},{5,13},{9,5},{13,1},{2,10},{6,14},... | collective-permute-start | bytes 55304 | tf_op jit(solution)/shard_map/ppermute | solution.py:425
  15.7 3.6 %collective-permute-start.3 = (bf16[72,128]{1,0:T(8,128)(2,1)S(1)}, bf16[72,128]{1,0:T(8,128)(2,1)S(1)}, u32[]{:S(2)}, u32[]{:S(2)}) collective-permute-start(bf16[72,128]{1,0:T(8,128)(2,1)S(1)} %reduce-precision_convert_fusion.refs_0_), channel_id=1, source_target_pairs={{0,12},{4,8},{8,0},{12,4},{1,13},{5,9},{9,1},{13,5},{2,14},{6,10},... | collective-permute-start | bytes 55304 | tf_op jit(solution)/shard_map/ppermute | solution.py:425
  16.8 2.6 %collective-permute-start.4 = (bf16[72,128]{1,0:T(8,128)(2,1)S(1)}, bf16[72,128]{1,0:T(8,128)(2,1)S(1)}, u32[]{:S(2)}, u32[]{:S(2)}) collective-permute-start(bf16[72,128]{1,0:T(8,128)(2,1)S(1)} %reduce-precision_convert_fusion.refs_0_), channel_id=1, source_target_pairs={{0,4},{4,0},{8,12},{12,8},{1,5},{5,1},{9,13},{13,9},{2,6},{6,2},{1... | collective-permute-start | bytes 55304 | tf_op jit(solution)/shard_map/ppermute | solution.py:425

commit v8 on v7

--- a/solution.py
+++ b/solution.py
@@ -11,6 +11,7 @@
 BF16 = jnp.bfloat16
 F32 = jnp.float32
 PARTS = 2
+PHASES = 4
 ROWS_BY_ROWS = (((1,), (1,)), ((), ()))
 
 
@@ -36,40 +37,61 @@
     return jnp.dot(block, mirror, preferred_element_type=F32).astype(BF16)
 
 
-def lag_sums(grad, joined, per_group, crossing):
-    channels, length = grad.shape
-    per = length // per_group
-    phases = 4
-    span = length // phases
+def grad_side(grad, per_group):
+    length = grad.shape[1]
+    span = length // PHASES
+    across = grad.T
+    left = jnp.concatenate([across[p * span : (p + 1) * span] for p in range(PHASES)], axis=1)
+    owner = iotas(1, PHASES * length)[1] % length // per_group
+    nothing = jnp.zeros((), BF16)
+    return jnp.concatenate(
+        [jnp.where(owner == g, left, nothing) for g in range(length // per_group)], axis=0
+    )
+
+
+def joined_side(joined, crossing):
+    length = joined.shape[1]
+    lane = iotas(1, length)[1]
+    nothing = jnp.zeros((), BF16)
+    mirrored = flip(joined).astype(F32)
+    right = []
+    for phase in range(PHASES):
+        shift = length // PHASES * (phase + 1)
+        turned = (mirrored if shift == length else pltpu.roll(mirrored, shift, 1)).astype(BF16)
+        if crossing:
+            earlier = jnp.where(lane >= shift, turned, nothing)
+            right.append(jnp.concatenate([earlier, turned], axis=1))
+        else:
+            right.append(jnp.where(lane < shift, turned, nothing))
+    return jnp.concatenate(right, axis=0)
+
+
+def side_sums(sides, length, crossing):
+    span = length // PHASES
     row, column = iotas(span, length)
     near = row + column >= span - 1
-    lane = iotas(1, length)[1]
-    owner = iotas(1, phases * length)[1] % length // per_group
-    nothing = jnp.zeros((), BF16)
-    mirrored = flip(joined)
     sums = []
-    for start in range(0, channels, length):
-        across = grad[start : start + length].T
-        block = mirrored[start : start + length].astype(F32)
-        left, right = [], []
-        for phase in range(phases):
-            left.append(across[phase * span : (phase + 1) * span])
-            shift = span * (phase + 1)
-            turned = (block if shift == length else pltpu.roll(block, shift, 1)).astype(BF16)
-            if crossing:
-                earlier = jnp.where(lane >= shift, turned, nothing)
-                right.append(jnp.concatenate([earlier, turned], axis=1))
-            else:
-                right.append(jnp.where(lane < shift, turned, nothing))
-        left = jnp.concatenate(left, axis=1)
-        left = jnp.concatenate([jnp.where(owner == g, left, nothing) for g in range(per)], axis=0)
-        grams = jnp.dot(left, jnp.concatenate(right, axis=0), preferred_element_type=F32)
-        for g in range(per):
-            gram = grams[g * span : (g + 1) * span]
+    for left, right in sides:
+        grams = jnp.dot(left, right, preferred_element_type=F32)
+        for start in range(0, grams.shape[0], span):
+            gram = grams[start : start + span]
             gram = jnp.where(near, gram[:, :length], gram[:, length:] if crossing else 0.0)
             turned = pltpu.roll(gram, 0, 1, stride=1, stride_axis=0)
             sums.append(jnp.sum(turned, axis=0, keepdims=True))
     return pltpu.roll(jnp.concatenate(sums, axis=0), length - span + 1, 1)
+
+
+def blocks_of(array):
+    length = array.shape[1]
+    return [array[start : start + length] for start in range(0, array.shape[0], length)]
+
+
+def lag_sums(grad, joined, per_group, crossing):
+    sides = [
+        (grad_side(one, per_group), joined_side(two, crossing))
+        for one, two in zip(blocks_of(grad), blocks_of(joined))
+    ]
+    return side_sums(sides, grad.shape[1], crossing)
 
 
 def own_kernel(*refs):
@@ -216,30 +238,84 @@
     )(*arrays)
 
 
-def by_role(own, halo):
+def cross_kernel(per_group, own_ref, halo_ref, sums_ref):
+    sums_ref[...] = lag_sums(own_ref[...], halo_ref[...], per_group, True)
+
+
+def cross_sums(own, halo, groups):
+    channels, length = own.shape
+    return pl.pallas_call(
+        functools.partial(cross_kernel, channels // groups),
+        out_shape=jax.ShapeDtypeStruct((groups, length), F32),
+        cost_estimate=pl.CostEstimate(flops=2**26, bytes_accessed=2**23, transcendentals=0),
+        name="cross_sums",
+    )(own, halo)
+
+
+def ready_kernel(per_group, own_ref, _, left_ref, right_ref):
     first = lax.axis_index("ctx") == 0
-    return jnp.where(first, halo, own), jnp.where(first, own, halo)
-
-
-def cross_kernel(per_group, swap, own_ref, halo_ref, sums_ref):
-    grad, joined = own_ref[...], halo_ref[...]
-    if swap:
-        grad, joined = by_role(grad, joined)
-    sums_ref[...] = lag_sums(grad, joined, per_group, True)
-
-
-def cross_sums(own, halo, groups, swap):
+
+    @pl.when(first)
+    def _():
+        for block, own in enumerate(blocks_of(own_ref[...])):
+            right_ref[block] = joined_side(own, True)
+
+    @pl.when(jnp.logical_not(first))
+    def _():
+        for block, own in enumerate(blocks_of(own_ref[...])):
+            left_ref[block] = grad_side(own, per_group)
+
+
+def halo_kernel(per_group, halo_ref, left_ref, right_ref, sums_ref):
+    length = halo_ref.shape[1]
+    first = lax.axis_index("ctx") == 0
+
+    @pl.when(first)
+    def _():
+        grads = blocks_of(halo_ref[...])
+        sides = [(grad_side(grad, per_group), right_ref[block]) for block, grad in enumerate(grads)]
+        sums_ref[...] = side_sums(sides, length, True)
+
+    @pl.when(jnp.logical_not(first))
+    def _():
+        sides = [
+            (left_ref[block], joined_side(joined, True))
+            for block, joined in enumerate(blocks_of(halo_ref[...]))
+        ]
+        sums_ref[...] = side_sums(sides, length, True)
+
+
+def ready_sides(own, per_group, after):
     channels, length = own.shape
+    blocks = channels // length
+    spread = length // PHASES * (length // per_group)
     whole = pl.BlockSpec(memory_space=pltpu.VMEM)
     return pl.pallas_call(
-        functools.partial(cross_kernel, channels // groups, swap),
+        functools.partial(ready_kernel, per_group),
         in_specs=[whole] * 2,
+        out_specs=[whole] * 2,
+        out_shape=[
+            pltpu.VMEM((blocks, spread, PHASES * length), BF16),
+            pltpu.VMEM((blocks, PHASES * length, 2 * length), BF16),
+        ],
+        cost_estimate=pl.CostEstimate(flops=2**26, bytes_accessed=2**23, transcendentals=0),
+        compiler_params=pltpu.CompilerParams(vmem_limit_bytes=12 * 2**20),
+        name="ready_sides",
+    )(in_vmem(own), in_vmem(after))
+
+
+def halo_sums(halo, sides, per_group):
+    channels, length = halo.shape
+    whole = pl.BlockSpec(memory_space=pltpu.VMEM)
+    return pl.pallas_call(
+        functools.partial(halo_kernel, per_group),
+        in_specs=[whole] * 3,
         out_specs=whole,
-        out_shape=pltpu.VMEM((groups, length), F32),
+        out_shape=pltpu.VMEM((channels // per_group, length), F32),
         cost_estimate=pl.CostEstimate(flops=2**26, bytes_accessed=2**23, transcendentals=0),
         compiler_params=pltpu.CompilerParams(vmem_limit_bytes=12 * 2**20),
-        name="cross_sums",
-    )(in_vmem(own), in_vmem(halo))
+        name="halo_sums",
+    )(in_vmem(halo), *map(in_vmem, sides))
 
 
 def output_kernel(
@@ -479,7 +555,7 @@
         halo = lax.ppermute(own, "ctx", swap)
         *held, mine = turn_sums(1, sources, made[:7], made[7:8])
         other = lax.ppermute(mine, "ctx", swap)
-        crossed = cross_sums(own, halo, groups, True)
+        crossed = halo_sums(halo, ready_sides(own, per_group, mine), per_group)
         sums = mine.astype(F32).at[:groups].add(crossed) + other.astype(F32)
         sums = lax.reduce_precision(sums, 8, 7).astype(BF16)
         terms = gather_terms(sums, "dp")
@@ -490,7 +566,7 @@
         before = lax.ppermute(joined, "ctx", [(i, i + 1) for i in range(shards - 1)])
         following = lax.ppermute(own, "ctx", [(i + 1, i) for i in range(shards - 1)])
         mine = local_sums(groups, keep_mask, query, key, value, grad)
-        crossed = cross_sums(own, before, groups, False)
+        crossed = cross_sums(own, before, groups)
         sums = lax.psum(mine.at[:groups].add(crossed), "ctx")
         terms = gather_terms(sums, "dp")
         results = outputs(keep_mask, filter_taps, skip_gain, query, key, value, grad, before, following)

time: 20.3 us -> 20.1 us (level)
  waiting for transfers between devices: 3.87 us -> 3.52 us
    ppermute x1, waiting for transfers between devices: 3.81 us -> 3.37 us  [body(): halo = lax.ppermute(own, 'ctx', swap)]
    pallas_call x1 -> x2, Pallas kernels: 1.1 us -> 1.31 us  [the longest x1 0.89 us: halo_sums(): pl.pallas_call(functools.partial(halo_kernel, per_group), in_specs=[whole...]
  transfers between devices with their start and end apart: 5 -> 5, of which waited for: 2 -> 2; matrix products, arithmetic and copies ran while one was open for 0% -> 0% of each run, Pallas kernels for 17% -> 18%
where the time goes in v8:
time: 20.1 us; the launch traced here: 20 us
  Pallas kernels  9.25 us (46%)
  starting transfers between devices  6.47 us (32%)
  waiting for transfers between devices  3.52 us (18%)
  between operations  0.71 us (4%)
    ppermute x3, starting transfers between devices, gather_terms(): lax.ppermute(sums, axis, list(enumerate(targets)))  3.92 us
    pallas_call x2, Pallas kernels, turn_sums(): pl.pallas_call(functools.partial(turn_kernel, channels // groups, turn),...  3.76 us
    ppermute x1, waiting for transfers between devices, body(): halo = lax.ppermute(own, 'ctx', swap)  3.37 us
    ppermute x1, starting transfers between devices, body(): halo = lax.ppermute(own, 'ctx', swap)  2.45 us
    pallas_call x1, Pallas kernels, pair_outputs(): pl.pallas_call(functools.partial(pair_kernel, channels // held[5].shape[0...  2.32 us
    pallas_call x1, Pallas kernels, own_block(): pl.pallas_call(own_kernel, in_specs=[pl.BlockSpec(memory_space=pltpu.HBM)...  1.2 us
    pallas_call x1, Pallas kernels, halo_sums(): pl.pallas_call(functools.partial(halo_kernel, per_group), in_specs=[whole...  0.89 us
    pallas_call x1, Pallas kernels, totals(): pl.pallas_call(functools.partial(total_kernel, groups, tap_scale, skip_sc...  0.65 us
  transfers between devices with their start and end apart: 5, of which 2 were waited for; matrix products, arithmetic and copies ran while one was open for 0% of the time, Pallas kernels for 18%

profile of v8, /device:TPU:1, one launch (start us, length us, event | category | flops | bytes accessed | tf_op | source)
XLA Modules:
  0.0 20.0 jit_solution(586383399975059379)
XLA Ops:
  0.6 1.2 %own_block.1 = (bf16[1024,128]{1,0:T(8,128)(2,1)S(1)}, s32[1,128]{1,0:T(1,128)S(1)}, bf16[1024,128]{1,0:T(8,128)(2,1)S(1)}, bf16[1024,128]{1,0:T(8,128)(2,1)S(1)...) custom-call(s32[1,128]{1,0:T(1,128)} %refs_0_.1, ...), custom_call_target="tpu_custom_call" | custom-call | tf_op jit(solution)/shard_map/own_block/pallas_call | solution.py:134
  1.8 3.7 %turn_sums.2 = (s32[1,128]{1,0:T(1,128)S(1)}, bf16[1024,128]{1,0:T(8,128)(2,1)S(1)}, bf16[1024,128]{1,0:T(8,128)(2,1)S(1)}, bf16[1024,128]{1,0:T(8,128)(2,1)S(1)...) custom-call(bf16[1024,128]{1,0:T(8,128)(2,1)} %bitcast.11, ...), custom_call_target="tpu_custom_call", output_to_operand_aliasing={{0}: (6, {}), {1}: (7, {}), {2}: (8, {}), {3}: (9, {}), {4}... | custom-call | flops 67108864 | bytes 8388608 | tf_op jit(solution)/shard_map/turn_sums/pallas_call | solution.py:190
  5.6 2.4 %collective-permute-start = (bf16[1024,128]{1,0:T(8,128)(2,1)S(1)}, bf16[1024,128]{1,0:T(8,128)(2,1)S(1)}, u32[]{:S(2)}, u32[]{:S(2)}) collective-permute-start(bf16[1024,128]{1,0:T(8,128)(2,1)S(1)} %get-tuple-element.102.own_ref), channel_id=1, source_target_pairs={{0,16},{16,0},{1,17},{17,1},{2,18},{18,2},{3,19},{19,3},{4,20},{20... | collective-permute-start | bytes 786440 | tf_op jit(solution)/shard_map/ppermute | solution.py:555
  8.1 0.1 collective-permute-start.1
  8.2 0.4 %ready_sides.1 = (bf16[8,256,512]{2,1,0:T(8,128)(2,1)S(1)}, bf16[8,512,256]{2,1,0:T(8,128)(2,1)S(1)}) custom-call(bf16[1024,128]{1,0:T(8,128)(2,1)S(1)} %get-tuple-element.102.own_ref, bf16[72,128]{1,0:T(8,128)(2,1)S(1)} %get-tuple-element.111._), custom_call_target="tpu_custom_call" | custom-call | flops 67108864 | bytes 8388608 | tf_op jit(solution)/shard_map/ready_sides/pallas_call | solution.py:293
  8.6 3.4 %collective-permute-done.refs_7_.halo_ref = bf16[1024,128]{1,0:T(8,128)(2,1)S(1)} collective-permute-done((bf16[1024,128]{1,0:T(8,128)(2,1)S(1)}, bf16[1024,128]{1,0:T(8,128)(2,1)S(1)}, u32[]{:S(2)}, u32[]{:S(2)}) %collective-permute-start) | collective-permute-done | bytes 262176 | tf_op jit(solution)/shard_map/ppermute | solution.py:555
  12.0 0.9 %halo_sums.1 = f32[64,128]{1,0:T(8,128)S(1)} custom-call(bf16[1024,128]{1,0:T(8,128)(2,1)S(1)} %collective-permute-done.refs_7_.halo_ref, bf16[8,256,512]{2,1,0:T(8,128)(2,1)S(1)} %get-tuple-element.112.left_ref, bf16[8,512,256]{2,1,0:T(8,128)(2,1)S(1)} %get-tuple-element.113.right_ref), custom_call_target="tpu_custom_call" | custom-call | flops 67108864 | bytes 8388608 | tf_op jit(solution)/shard_map/halo_sums/pallas_call | solution.py:310
  12.9 0.0 collective-permute-done.1
  12.9 2.6 %collective-permute-start.2 = (bf16[72,128]{1,0:T(8,128)(2,1)S(1)}, bf16[72,128]{1,0:T(8,128)(2,1)S(1)}, u32[]{:S(2)}, u32[]{:S(2)}) collective-permute-start(bf16[72,128]{1,0:T(8,128)(2,1)S(1)} %reduce-precision_convert_fusion.refs_0_), channel_id=1, source_target_pairs={{0,8},{4,12},{8,4},{12,0},{1,9},{5,13},{9,5},{13,1},{2,10},{6,14},... | collective-permute-start | bytes 55304 | tf_op jit(solution)/shard_map/ppermute | solution.py:501
  15.5 1.1 %collective-permute-start.3 = (bf16[72,128]{1,0:T(8,128)(2,1)S(1)}, bf16[72,128]{1,0:T(8,128)(2,1)S(1)}, u32[]{:S(2)}, u32[]{:S(2)}) collective-permute-start(bf16[72,128]{1,0:T(8,128)(2,1)S(1)} %reduce-precision_convert_fusion.refs_0_), channel_id=1, source_target_pairs={{0,12},{4,8},{8,0},{12,4},{1,13},{5,9},{9,1},{13,5},{2,14},{6,10},... | collective-permute-start | bytes 55304 | tf_op jit(solution)/shard_map/ppermute | solution.py:501
  16.6 0.2 %collective-permute-start.4 = (bf16[72,128]{1,0:T(8,128)(2,1)S(1)}, bf16[72,128]{1,0:T(8,128)(2,1)S(1)}, u32[]{:S(2)}, u32[]{:S(2)}) collective-permute-start(bf16[72,128]{1,0:T(8,128)(2,1)S(1)} %reduce-precision_convert_fusion.refs_0_), channel_id=1, source_target_pairs={{0,4},{4,0},{8,12},{12,8},{1,5},{5,1},{9,13},{13,9},{2,6},{6,2},{1... | collective-permute-start | bytes 55304 | tf_op jit(solution)/shard_map/ppermute | solution.py:501
  16.8 2.3 %pair_outputs.1 = (bf16[1024,128]{1,0:T(8,128)(2,1)}, bf16[1024,128]{1,0:T(8,128)(2,1)}, bf16[1024,128]{1,0:T(8,128)(2,1)}, bf16[1024,128]{1,0:T(8,128)(2,1)}) custom-call(s32[1,128]{1,0:T(1,128)S(1)} %get-tuple-element.95.refs_0_, ...), custom_call_target="tpu_custom_call", output_to_operand_aliasing={{0}: (8, {}), {1}: (9, {}), {2}: (10, {}), {3}: (11, {})} | custom-call | flops 268435456 | bytes 8388608 | tf_op jit(solution)/shard_map/pair_outputs/pallas_call | solution.py:479
  19.2 0.0 collective-permute-done.2.refs_1_
  19.2 0.0 collective-permute-done.3.refs_2_
  19.2 0.1 collective-permute-done.4.refs_3_
  19.3 0.6 %totals.1 = (f32[64,128]{1,0:T(8,128)}, f32[8,128]{1,0:T(8,128)}) custom-call(bf16[72,128]{1,0:T(8,128)(2,1)S(1)} %reduce-precision_convert_fusion.refs_0_, bf16[72,128]{1,0:T(8,128)(2,1)S(1)} %collective-permute-done.2.refs_1_, bf16[72,128]{1,0:T(8,128)(2,1)S(1)} %collective-permute-done.3.refs_2_, bf16[72,128]{1,0:T(8,128)(2,1)S(1)} %collective-permute-done.4.refs_3_), custom_call_target="tpu_custom_call" | custom-call | tf_op jit(solution)/shard_map/totals/pallas_call | solution.py:526
  (4 shorter events, 0.1 us)
Async XLA Ops:
  5.6 6.4 %collective-permute-start = (bf16[1024,128]{1,0:T(8,128)(2,1)S(1)}, bf16[1024,128]{1,0:T(8,128)(2,1)S(1)}, u32[]{:S(2)}, u32[]{:S(2)}) collective-permute-start(bf16[1024,128]{1,0:T(8,128)(2,1)S(1)} %get-tuple-element.102.own_ref), channel_id=1, source_target_pairs={{0,16},{16,0},{1,17},{17,1},{2,18},{18,2},{3,19},{19,3},{4,20},{20... | collective-permute-start | bytes 786440 | tf_op jit(solution)/shard_map/ppermute | solution.py:555
  8.1 4.8 %collective-permute-start.1 = (bf16[72,128]{1,0:T(8,128)(2,1)S(1)}, bf16[72,128]{1,0:T(8,128)(2,1)S(1)}, u32[]{:S(2)}, u32[]{:S(2)}) collective-permute-start(bf16[72,128]{1,0:T(8,128)(2,1)S(1)} %get-tuple-element.111._), channel_id=1, source_target_pairs={{0,16},{16,0},{1,17},{17,1},{2,18},{18,2},{3,19},{19,3},{4,20},{20... | collective-permute-start | bytes 55304 | tf_op jit(solution)/shard_map/ppermute | solution.py:557
  12.9 6.3 %collective-permute-start.2 = (bf16[72,128]{1,0:T(8,128)(2,1)S(1)}, bf16[72,128]{1,0:T(8,128)(2,1)S(1)}, u32[]{:S(2)}, u32[]{:S(2)}) collective-permute-start(bf16[72,128]{1,0:T(8,128)(2,1)S(1)} %reduce-precision_convert_fusion.refs_0_), channel_id=1, source_target_pairs={{0,8},{4,12},{8,4},{12,0},{1,9},{5,13},{9,5},{13,1},{2,10},{6,14},... | collective-permute-start | bytes 55304 | tf_op jit(solution)/shard_map/ppermute | solution.py:501
  15.5 3.6 %collective-permute-start.3 = (bf16[72,128]{1,0:T(8,128)(2,1)S(1)}, bf16[72,128]{1,0:T(8,128)(2,1)S(1)}, u32[]{:S(2)}, u32[]{:S(2)}) collective-permute-start(bf16[72,128]{1,0:T(8,128)(2,1)S(1)} %reduce-precision_convert_fusion.refs_0_), channel_id=1, source_target_pairs={{0,12},{4,8},{8,0},{12,4},{1,13},{5,9},{9,1},{13,5},{2,14},{6,10},... | collective-permute-start | bytes 55304 | tf_op jit(solution)/shard_map/ppermute | solution.py:501
  16.6 2.7 %collective-permute-start.4 = (bf16[72,128]{1,0:T(8,128)(2,1)S(1)}, bf16[72,128]{1,0:T(8,128)(2,1)S(1)}, u32[]{:S(2)}, u32[]{:S(2)}) collective-permute-start(bf16[72,128]{1,0:T(8,128)(2,1)S(1)} %reduce-precision_convert_fusion.refs_0_), channel_id=1, source_target_pairs={{0,4},{4,0},{8,12},{12,8},{1,5},{5,1},{9,13},{13,9},{2,6},{6,2},{1... | collective-permute-start | bytes 55304 | tf_op jit(solution)/shard_map/ppermute | solution.py:501

commit v9 on v8

--- a/solution.py
+++ b/solution.py
@@ -176,8 +176,7 @@
             copy.wait()
         local_part(per_group, held, sums_ref)
         if turn == 0:
-            bounds = (0, 3 * held[5].shape[0] // 8, 3 * held[5].shape[0] // 4)
-            filters(per_group, held, None, out_refs, made_refs, out_sems, [("free", bounds)])
+            filters(per_group, held, None, out_refs, made_refs, out_sems, ahead)
 
 
 def turn_sums(turn, sources, held, made=()):
@@ -384,12 +383,26 @@
     )(keep, taps, skip_rows, query, key, value, grad, before, following)
 
 
+def ahead(groups, first):
+    share = groups * (12 if first else 8) // 16
+    return [("free", (0, share // 2, share))]
+
+
+def behind(groups, first):
+    bounds = ahead(groups, first)[0][1]
+    return [("bound", bounds)] + [("all", (bounds[-1], groups))] * (bounds[-1] < groups)
+
+
+def whole(groups, first):
+    return [("all", (0, groups // 2, groups))]
+
+
 def filters(per_group, held, halo_ref, out_refs, made_refs, sems, tasks):
     first = lax.axis_index("ctx") == 0
 
     def run(here):
         copies = []
-        for index, (chosen, bounds) in enumerate(tasks):
+        for index, (chosen, bounds) in enumerate(tasks(held[5].shape[0], here)):
             forward = chosen == "all" or (chosen == "free") == here
             backward = chosen == "all" or (chosen == "free") != here
             copies += filter_groups(
@@ -465,12 +478,10 @@
 def pair_kernel(per_group, *refs):
     held, halo_ref, out_refs = refs[:7], refs[7], refs[12:16]
     made_refs, sems = refs[16:20], refs[20]
-    groups = held[5].shape[0]
     even = lax.axis_index("tp") % 2 == 0
     rest = (per_group, held, halo_ref, out_refs, made_refs, sems)
-    pl.when(even)(functools.partial(filters, *rest, [("all", (0, groups // 2, groups))]))
-    tasks = [("bound", (0, 3 * groups // 8, 3 * groups // 4)), ("all", (3 * groups // 4, groups))]
-    pl.when(jnp.logical_not(even))(functools.partial(filters, *rest, tasks))
+    pl.when(even)(functools.partial(filters, *rest, whole))
+    pl.when(jnp.logical_not(even))(functools.partial(filters, *rest, behind))
 
 
 def pair_outputs(held, halo, results):

time: 20.1 us -> 20.1 us (level)
    ppermute x1, starting transfers between devices: 2.45 us -> 2.12 us  [body(): halo = lax.ppermute(own, 'ctx', swap)]
    ppermute x3, starting transfers between devices: 3.92 us -> 4.18 us  [gather_terms(): lax.ppermute(sums, axis, list(enumerate(targets)))]
where the time goes in v9:
time: 20.1 us; the launch traced here: 20 us
  Pallas kernels  9.25 us (46%)
  starting transfers between devices  6.4 us (32%)
  waiting for transfers between devices  3.61 us (18%)
  between operations  0.71 us (4%)
    ppermute x3, starting transfers between devices, gather_terms(): lax.ppermute(sums, axis, list(enumerate(targets)))  4.18 us
    pallas_call x2, Pallas kernels, turn_sums(): pl.pallas_call(functools.partial(turn_kernel, channels // groups, turn),...  3.76 us
    ppermute x1, waiting for transfers between devices, body(): halo = lax.ppermute(own, 'ctx', swap)  3.44 us
    pallas_call x1, Pallas kernels, pair_outputs(): pl.pallas_call(functools.partial(pair_kernel, channels // held[5].shape[0...  2.32 us
    ppermute x1, starting transfers between devices, body(): halo = lax.ppermute(own, 'ctx', swap)  2.12 us
    pallas_call x1, Pallas kernels, own_block(): pl.pallas_call(own_kernel, in_specs=[pl.BlockSpec(memory_space=pltpu.HBM)...  1.2 us
    pallas_call x1, Pallas kernels, halo_sums(): pl.pallas_call(functools.partial(halo_kernel, per_group), in_specs=[whole...  0.89 us
    pallas_call x1, Pallas kernels, totals(): pl.pallas_call(functools.partial(total_kernel, groups, tap_scale, skip_sc...  0.65 us
  transfers between devices with their start and end apart: 5, of which 2 were waited for; matrix products, arithmetic and copies ran while one was open for 0% of the time, Pallas kernels for 18%

profile of v9, /device:TPU:1, one launch (start us, length us, event | category | flops | bytes accessed | tf_op | source)
XLA Modules:
  0.0 20.0 jit_solution(13092289952633276578)
XLA Ops:
  0.6 1.2 %own_block.1 = (bf16[1024,128]{1,0:T(8,128)(2,1)S(1)}, s32[1,128]{1,0:T(1,128)S(1)}, bf16[1024,128]{1,0:T(8,128)(2,1)S(1)}, bf16[1024,128]{1,0:T(8,128)(2,1)S(1)...) custom-call(s32[1,128]{1,0:T(1,128)} %refs_0_.1, ...), custom_call_target="tpu_custom_call" | custom-call | tf_op jit(solution)/shard_map/own_block/pallas_call | solution.py:134
  1.8 3.7 %turn_sums.2 = (s32[1,128]{1,0:T(1,128)S(1)}, bf16[1024,128]{1,0:T(8,128)(2,1)S(1)}, bf16[1024,128]{1,0:T(8,128)(2,1)S(1)}, bf16[1024,128]{1,0:T(8,128)(2,1)S(1)...) custom-call(bf16[1024,128]{1,0:T(8,128)(2,1)} %bitcast.11, ...), custom_call_target="tpu_custom_call", output_to_operand_aliasing={{0}: (6, {}), {1}: (7, {}), {2}: (8, {}), {3}: (9, {}), {4}... | custom-call | flops 67108864 | bytes 8388608 | tf_op jit(solution)/shard_map/turn_sums/pallas_call | solution.py:189
  5.6 2.1 %collective-permute-start = (bf16[1024,128]{1,0:T(8,128)(2,1)S(1)}, bf16[1024,128]{1,0:T(8,128)(2,1)S(1)}, u32[]{:S(2)}, u32[]{:S(2)}) collective-permute-start(bf16[1024,128]{1,0:T(8,128)(2,1)S(1)} %get-tuple-element.102.own_ref), channel_id=1, source_target_pairs={{0,16},{16,0},{1,17},{17,1},{2,18},{18,2},{3,19},{19,3},{4,20},{20... | collective-permute-start | bytes 786440 | tf_op jit(solution)/shard_map/ppermute | solution.py:566
  7.7 0.1 collective-permute-start.1
  7.8 0.4 %ready_sides.1 = (bf16[8,256,512]{2,1,0:T(8,128)(2,1)S(1)}, bf16[8,512,256]{2,1,0:T(8,128)(2,1)S(1)}) custom-call(bf16[1024,128]{1,0:T(8,128)(2,1)S(1)} %get-tuple-element.102.own_ref, bf16[72,128]{1,0:T(8,128)(2,1)S(1)} %get-tuple-element.111._), custom_call_target="tpu_custom_call" | custom-call | flops 67108864 | bytes 8388608 | tf_op jit(solution)/shard_map/ready_sides/pallas_call | solution.py:292
  8.3 3.4 %collective-permute-done.refs_7_.halo_ref = bf16[1024,128]{1,0:T(8,128)(2,1)S(1)} collective-permute-done((bf16[1024,128]{1,0:T(8,128)(2,1)S(1)}, bf16[1024,128]{1,0:T(8,128)(2,1)S(1)}, u32[]{:S(2)}, u32[]{:S(2)}) %collective-permute-start) | collective-permute-done | bytes 262176 | tf_op jit(solution)/shard_map/ppermute | solution.py:566
  11.7 0.9 %halo_sums.1 = f32[64,128]{1,0:T(8,128)S(1)} custom-call(bf16[1024,128]{1,0:T(8,128)(2,1)S(1)} %collective-permute-done.refs_7_.halo_ref, bf16[8,256,512]{2,1,0:T(8,128)(2,1)S(1)} %get-tuple-element.112.left_ref, bf16[8,512,256]{2,1,0:T(8,128)(2,1)S(1)} %get-tuple-element.113.right_ref), custom_call_target="tpu_custom_call" | custom-call | flops 67108864 | bytes 8388608 | tf_op jit(solution)/shard_map/halo_sums/pallas_call | solution.py:309
  12.6 0.0 collective-permute-done.1
  12.6 2.9 %collective-permute-start.2 = (bf16[72,128]{1,0:T(8,128)(2,1)S(1)}, bf16[72,128]{1,0:T(8,128)(2,1)S(1)}, u32[]{:S(2)}, u32[]{:S(2)}) collective-permute-start(bf16[72,128]{1,0:T(8,128)(2,1)S(1)} %reduce-precision_convert_fusion.refs_0_), channel_id=1, source_target_pairs={{0,8},{4,12},{8,4},{12,0},{1,9},{5,13},{9,5},{13,1},{2,10},{6,14},... | collective-permute-start | bytes 55304 | tf_op jit(solution)/shard_map/ppermute | solution.py:512
  15.5 1.1 %collective-permute-start.3 = (bf16[72,128]{1,0:T(8,128)(2,1)S(1)}, bf16[72,128]{1,0:T(8,128)(2,1)S(1)}, u32[]{:S(2)}, u32[]{:S(2)}) collective-permute-start(bf16[72,128]{1,0:T(8,128)(2,1)S(1)} %reduce-precision_convert_fusion.refs_0_), channel_id=1, source_target_pairs={{0,12},{4,8},{8,0},{12,4},{1,13},{5,9},{9,1},{13,5},{2,14},{6,10},... | collective-permute-start | bytes 55304 | tf_op jit(solution)/shard_map/ppermute | solution.py:512
  16.6 0.2 %collective-permute-start.4 = (bf16[72,128]{1,0:T(8,128)(2,1)S(1)}, bf16[72,128]{1,0:T(8,128)(2,1)S(1)}, u32[]{:S(2)}, u32[]{:S(2)}) collective-permute-start(bf16[72,128]{1,0:T(8,128)(2,1)S(1)} %reduce-precision_convert_fusion.refs_0_), channel_id=1, source_target_pairs={{0,4},{4,0},{8,12},{12,8},{1,5},{5,1},{9,13},{13,9},{2,6},{6,2},{1... | collective-permute-start | bytes 55304 | tf_op jit(solution)/shard_map/ppermute | solution.py:512
  16.8 2.3 %pair_outputs.1 = (bf16[1024,128]{1,0:T(8,128)(2,1)}, bf16[1024,128]{1,0:T(8,128)(2,1)}, bf16[1024,128]{1,0:T(8,128)(2,1)}, bf16[1024,128]{1,0:T(8,128)(2,1)}) custom-call(s32[1,128]{1,0:T(1,128)S(1)} %get-tuple-element.95.refs_0_, ...), custom_call_target="tpu_custom_call", output_to_operand_aliasing={{0}: (8, {}), {1}: (9, {}), {2}: (10, {}), {3}: (11, {})} | custom-call | flops 268435456 | bytes 8388608 | tf_op jit(solution)/shard_map/pair_outputs/pallas_call | solution.py:490
  19.2 0.0 collective-permute-done.2.refs_1_
  19.2 0.0 collective-permute-done.3.refs_2_
  19.2 0.2 collective-permute-done.4.refs_3_
  19.3 0.6 %totals.1 = (f32[64,128]{1,0:T(8,128)}, f32[8,128]{1,0:T(8,128)}) custom-call(bf16[72,128]{1,0:T(8,128)(2,1)S(1)} %reduce-precision_convert_fusion.refs_0_, bf16[72,128]{1,0:T(8,128)(2,1)S(1)} %collective-permute-done.2.refs_1_, bf16[72,128]{1,0:T(8,128)(2,1)S(1)} %collective-permute-done.3.refs_2_, bf16[72,128]{1,0:T(8,128)(2,1)S(1)} %collective-permute-done.4.refs_3_), custom_call_target="tpu_custom_call" | custom-call | tf_op jit(solution)/shard_map/totals/pallas_call | solution.py:537
  (4 shorter events, 0.1 us)
Async XLA Ops:
  5.6 6.2 %collective-permute-start = (bf16[1024,128]{1,0:T(8,128)(2,1)S(1)}, bf16[1024,128]{1,0:T(8,128)(2,1)S(1)}, u32[]{:S(2)}, u32[]{:S(2)}) collective-permute-start(bf16[1024,128]{1,0:T(8,128)(2,1)S(1)} %get-tuple-element.102.own_ref), channel_id=1, source_target_pairs={{0,16},{16,0},{1,17},{17,1},{2,18},{18,2},{3,19},{19,3},{4,20},{20... | collective-permute-start | bytes 786440 | tf_op jit(solution)/shard_map/ppermute | solution.py:566
  7.7 4.9 %collective-permute-start.1 = (bf16[72,128]{1,0:T(8,128)(2,1)S(1)}, bf16[72,128]{1,0:T(8,128)(2,1)S(1)}, u32[]{:S(2)}, u32[]{:S(2)}) collective-permute-start(bf16[72,128]{1,0:T(8,128)(2,1)S(1)} %get-tuple-element.111._), channel_id=1, source_target_pairs={{0,16},{16,0},{1,17},{17,1},{2,18},{18,2},{3,19},{19,3},{4,20},{20... | collective-permute-start | bytes 55304 | tf_op jit(solution)/shard_map/ppermute | solution.py:568
  12.6 6.5 %collective-permute-start.2 = (bf16[72,128]{1,0:T(8,128)(2,1)S(1)}, bf16[72,128]{1,0:T(8,128)(2,1)S(1)}, u32[]{:S(2)}, u32[]{:S(2)}) collective-permute-start(bf16[72,128]{1,0:T(8,128)(2,1)S(1)} %reduce-precision_convert_fusion.refs_0_), channel_id=1, source_target_pairs={{0,8},{4,12},{8,4},{12,0},{1,9},{5,13},{9,5},{13,1},{2,10},{6,14},... | collective-permute-start | bytes 55304 | tf_op jit(solution)/shard_map/ppermute | solution.py:512
  15.5 3.6 %collective-permute-start.3 = (bf16[72,128]{1,0:T(8,128)(2,1)S(1)}, bf16[72,128]{1,0:T(8,128)(2,1)S(1)}, u32[]{:S(2)}, u32[]{:S(2)}) collective-permute-start(bf16[72,128]{1,0:T(8,128)(2,1)S(1)} %reduce-precision_convert_fusion.refs_0_), channel_id=1, source_target_pairs={{0,12},{4,8},{8,0},{12,4},{1,13},{5,9},{9,1},{13,5},{2,14},{6,10},... | collective-permute-start | bytes 55304 | tf_op jit(solution)/shard_map/ppermute | solution.py:512
  16.6 2.7 %collective-permute-start.4 = (bf16[72,128]{1,0:T(8,128)(2,1)S(1)}, bf16[72,128]{1,0:T(8,128)(2,1)S(1)}, u32[]{:S(2)}, u32[]{:S(2)}) collective-permute-start(bf16[72,128]{1,0:T(8,128)(2,1)S(1)} %reduce-precision_convert_fusion.refs_0_), channel_id=1, source_target_pairs={{0,4},{4,0},{8,12},{12,8},{1,5},{5,1},{9,13},{13,9},{2,6},{6,2},{1... | collective-permute-start | bytes 55304 | tf_op jit(solution)/shard_map/ppermute | solution.py:512

commit v10 on v8

--- a/solution.py
+++ b/solution.py
@@ -129,27 +129,39 @@
     pl.when(jnp.logical_not(first))(functools.partial(run, 1, 4, True))
 
 
-def own_block(*sources):
+def first_kernel(per_group, *refs):
+    sources, (own_ref, *held), sums_ref, out_refs = refs[:7], refs[7:15], refs[15], refs[16:20]
+    own_sems, sems, made_refs, out_sems = refs[20], refs[21], refs[22:24], refs[24]
+    own_kernel(*sources[:5], own_ref, *held, own_sems)
+    turn_part(per_group, 0, sources[1:], held, sums_ref, sems, out_refs, made_refs, out_sems)
+
+
+def first_turn(*sources):
+    channels, length = sources[1].shape
+    groups = sources[5].shape[0]
     whole = pl.BlockSpec(memory_space=pltpu.VMEM)
-    return pl.pallas_call(
-        own_kernel,
-        in_specs=[pl.BlockSpec(memory_space=pltpu.HBM)] * 5,
-        out_specs=[whole] * 8,
-        out_shape=[pltpu.VMEM(sources[1].shape, BF16)]
-        + [pltpu.VMEM(source.shape, source.dtype) for source in sources],
-        scratch_shapes=[pltpu.SemaphoreType.DMA((2 * PARTS + 1,))],
-        compiler_params=pltpu.CompilerParams(vmem_limit_bytes=12 * 2**20),
-        name="own_block",
-    )(*map(in_hbm, sources[:5]))
-
-
-def turn_kernel(per_group, turn, *refs):
-    sources = refs[:6]
-    if turn == 0:
-        held, sums_ref, out_refs = refs[13:20], refs[20], refs[21:25]
-        sems, made_refs, out_sems = refs[25], refs[26:28], refs[28]
-    else:
-        held, sums_ref, sems = refs[14:21], refs[21], refs[22]
+    hbm = pl.BlockSpec(memory_space=pltpu.HBM)
+    return pl.pallas_call(
+        functools.partial(first_kernel, channels // groups),
+        in_specs=[hbm] * 7,
+        out_specs=[whole] * 9 + [hbm] * 4,
+        out_shape=[pltpu.VMEM((channels, length), BF16)]
+        + [pltpu.VMEM(source.shape, source.dtype) for source in sources]
+        + [pltpu.VMEM((groups + channels // length, length), BF16)]
+        + [jax.ShapeDtypeStruct((channels, length), BF16)] * 4,
+        scratch_shapes=[pltpu.SemaphoreType.DMA((2 * PARTS + 1,)), pltpu.SemaphoreType.DMA((4,))]
+        + [pltpu.VMEM((channels, length), BF16)] * 2
+        + [pltpu.SemaphoreType.DMA((8,))],
+        compiler_params=pltpu.CompilerParams(vmem_limit_bytes=12 * 2**20),
+        name="first_turn",
+    )(*map(in_hbm, sources))
+
+
+def turn_kernel(per_group, *refs):
+    turn_part(per_group, 1, refs[:6], refs[14:21], refs[21], refs[22])
+
+
+def turn_part(per_group, turn, sources, held, sums_ref, sems, out_refs=(), made_refs=(), out_sems=None):
     query, key, value, grad, taps, skips = zip(sources, held[1:])
 
     def load(*pairs):
@@ -180,24 +192,16 @@
             filters(per_group, held, None, out_refs, made_refs, out_sems, [("free", bounds)])
 
 
-def turn_sums(turn, sources, held, made=()):
-    channels, length = held[1].shape
-    groups = held[5].shape[0]
+def turn_sums(sources, *given):
+    channels = given[1].shape[0]
     whole = pl.BlockSpec(memory_space=pltpu.VMEM)
-    hbm = pl.BlockSpec(memory_space=pltpu.HBM)
-    free = turn == 0
-    given = (*held, *made)
-    return pl.pallas_call(
-        functools.partial(turn_kernel, channels // groups, turn),
-        in_specs=[hbm] * 6 + [whole] * len(given),
-        out_specs=[whole] * 8 + [hbm] * (4 * free),
-        out_shape=[pltpu.VMEM(array.shape, array.dtype) for array in held]
-        + [pltpu.VMEM((groups + channels // length, length), BF16)]
-        + [jax.ShapeDtypeStruct((channels, length), BF16)] * (4 * free),
-        input_output_aliases={6 + index: index for index in range(len(given))},
-        scratch_shapes=[pltpu.SemaphoreType.DMA((4,))]
-        + [pltpu.VMEM((channels, length), BF16)] * (2 * free)
-        + [pltpu.SemaphoreType.DMA((8,))] * free,
+    return pl.pallas_call(
+        functools.partial(turn_kernel, channels // given[5].shape[0]),
+        in_specs=[pl.BlockSpec(memory_space=pltpu.HBM)] * 6 + [whole] * 8,
+        out_specs=[whole] * 8,
+        out_shape=[pltpu.VMEM(array.shape, array.dtype) for array in given],
+        input_output_aliases={6 + index: index for index in range(8)},
+        scratch_shapes=[pltpu.SemaphoreType.DMA((4,))],
         cost_estimate=pl.CostEstimate(flops=2**26, bytes_accessed=2**23, transcendentals=0),
         compiler_params=pltpu.CompilerParams(vmem_limit_bytes=12 * 2**20),
         name="turn_sums",
@@ -549,11 +553,9 @@
         swap = [(0, 1), (1, 0)]
         skips = skip_gain.reshape(channels // length, length)
         sources = (keep_mask, query, key, value, grad, filter_taps, skips)
-        own, *held = own_block(*sources)
-        made = turn_sums(0, sources, held)
-        own, made = lax.optimization_barrier((own, made))
+        own, *made = first_turn(*sources)
         halo = lax.ppermute(own, "ctx", swap)
-        *held, mine = turn_sums(1, sources, made[:7], made[7:8])
+        *held, mine = turn_sums(sources, *made[:8])
         other = lax.ppermute(mine, "ctx", swap)
         crossed = halo_sums(halo, ready_sides(own, per_group, mine), per_group)
         sums = mine.astype(F32).at[:groups].add(crossed) + other.astype(F32)

time: 20.1 us -> 20.1 us (level)
    pallas_call x3 -> x2, Pallas kernels: 4.96 us -> 4.96 us  [the longest x1 4.92 us: first_turn(): pl.pallas_call(functools.partial(first_kernel, channels // groups), in_sp...]
  transfers between devices with their start and end apart: 5 -> 5, of which waited for: 2 -> 2; matrix products, arithmetic and copies ran while one was open for 0% -> 0% of each run, Pallas kernels for 18% -> 19%
where the time goes in v10:
time: 20.1 us; the launch traced here: 19.9 us
  Pallas kernels  9.25 us (46%)
  starting transfers between devices  6.46 us (32%)
  waiting for transfers between devices  3.51 us (17%)
  between operations  0.7 us (3%)
    pallas_call x1, Pallas kernels, first_turn(): pl.pallas_call(functools.partial(first_kernel, channels // groups), in_sp...  4.92 us
    ppermute x3, starting transfers between devices, gather_terms(): lax.ppermute(sums, axis, list(enumerate(targets)))  3.91 us
    ppermute x1, waiting for transfers between devices, body(): halo = lax.ppermute(own, 'ctx', swap)  3.37 us
    ppermute x1, starting transfers between devices, body(): halo = lax.ppermute(own, 'ctx', swap)  2.45 us
    pallas_call x1, Pallas kernels, pair_outputs(): pl.pallas_call(functools.partial(pair_kernel, channels // held[5].shape[0...  2.33 us
    pallas_call x1, Pallas kernels, halo_sums(): pl.pallas_call(functools.partial(halo_kernel, per_group), in_specs=[whole...  0.89 us
    pallas_call x1, Pallas kernels, totals(): pl.pallas_call(functools.partial(total_kernel, groups, tap_scale, skip_sc...  0.65 us
    pallas_call x1, Pallas kernels, ready_sides(): pl.pallas_call(functools.partial(ready_kernel, per_group), in_specs=[whol...  0.43 us
  transfers between devices with their start and end apart: 5, of which 2 were waited for; matrix products, arithmetic and copies ran while one was open for 0% of the time, Pallas kernels for 19%

profile of v10, /device:TPU:1, one launch (start us, length us, event | category | flops | bytes accessed | tf_op | source)
XLA Modules:
  0.0 19.9 jit_solution(16149920169200849606)
XLA Ops:
  0.6 4.9 %first_turn.1 = (bf16[1024,128]{1,0:T(8,128)(2,1)S(1)}, s32[1,128]{1,0:T(1,128)S(1)}, bf16[1024,128]{1,0:T(8,128)(2,1)S(1)}, bf16[1024,128]{1,0:T(8,128)(2,1)S(1...) custom-call(s32[1,128]{1,0:T(1,128)} %refs_0_.1, ...), custom_call_target="tpu_custom_call" | custom-call | tf_op jit(solution)/shard_map/first_turn/pallas_call | solution.py:144
  5.6 2.4 %collective-permute-start = (bf16[1024,128]{1,0:T(8,128)(2,1)S(1)}, bf16[1024,128]{1,0:T(8,128)(2,1)S(1)}, u32[]{:S(2)}, u32[]{:S(2)}) collective-permute-start(bf16[1024,128]{1,0:T(8,128)(2,1)S(1)} %get-tuple-element.62.own_ref), channel_id=1, source_target_pairs={{0,16},{16,0},{1,17},{17,1},{2,18},{18,2},{3,19},{19,3},{4,20},{20... | collective-permute-start | bytes 786440 | tf_op jit(solution)/shard_map/ppermute | solution.py:557
  8.1 0.1 collective-permute-start.1
  8.2 0.4 %ready_sides.1 = (bf16[8,256,512]{2,1,0:T(8,128)(2,1)S(1)}, bf16[8,512,256]{2,1,0:T(8,128)(2,1)S(1)}) custom-call(bf16[1024,128]{1,0:T(8,128)(2,1)S(1)} %get-tuple-element.62.own_ref, bf16[72,128]{1,0:T(8,128)(2,1)S(1)} %get-tuple-element.71._), custom_call_target="tpu_custom_call" | custom-call | flops 67108864 | bytes 8388608 | tf_op jit(solution)/shard_map/ready_sides/pallas_call | solution.py:297
  8.6 3.4 %collective-permute-done.refs_7_.halo_ref = bf16[1024,128]{1,0:T(8,128)(2,1)S(1)} collective-permute-done((bf16[1024,128]{1,0:T(8,128)(2,1)S(1)}, bf16[1024,128]{1,0:T(8,128)(2,1)S(1)}, u32[]{:S(2)}, u32[]{:S(2)}) %collective-permute-start) | collective-permute-done | bytes 262176 | tf_op jit(solution)/shard_map/ppermute | solution.py:557
  12.0 0.9 %halo_sums.1 = f32[64,128]{1,0:T(8,128)S(1)} custom-call(bf16[1024,128]{1,0:T(8,128)(2,1)S(1)} %collective-permute-done.refs_7_.halo_ref, bf16[8,256,512]{2,1,0:T(8,128)(2,1)S(1)} %get-tuple-element.72.left_ref, bf16[8,512,256]{2,1,0:T(8,128)(2,1)S(1)} %get-tuple-element.73.right_ref), custom_call_target="tpu_custom_call" | custom-call | flops 67108864 | bytes 8388608 | tf_op jit(solution)/shard_map/halo_sums/pallas_call | solution.py:314
  12.9 0.0 collective-permute-done.1
  12.9 2.6 %collective-permute-start.2 = (bf16[72,128]{1,0:T(8,128)(2,1)S(1)}, bf16[72,128]{1,0:T(8,128)(2,1)S(1)}, u32[]{:S(2)}, u32[]{:S(2)}) collective-permute-start(bf16[72,128]{1,0:T(8,128)(2,1)S(1)} %reduce-precision_convert_fusion.refs_0_), channel_id=1, source_target_pairs={{0,8},{4,12},{8,4},{12,0},{1,9},{5,13},{9,5},{13,1},{2,10},{6,14},... | collective-permute-start | bytes 55304 | tf_op jit(solution)/shard_map/ppermute | solution.py:505
  15.5 1.1 %collective-permute-start.3 = (bf16[72,128]{1,0:T(8,128)(2,1)S(1)}, bf16[72,128]{1,0:T(8,128)(2,1)S(1)}, u32[]{:S(2)}, u32[]{:S(2)}) collective-permute-start(bf16[72,128]{1,0:T(8,128)(2,1)S(1)} %reduce-precision_convert_fusion.refs_0_), channel_id=1, source_target_pairs={{0,12},{4,8},{8,0},{12,4},{1,13},{5,9},{9,1},{13,5},{2,14},{6,10},... | collective-permute-start | bytes 55304 | tf_op jit(solution)/shard_map/ppermute | solution.py:505
  16.6 0.2 %collective-permute-start.4 = (bf16[72,128]{1,0:T(8,128)(2,1)S(1)}, bf16[72,128]{1,0:T(8,128)(2,1)S(1)}, u32[]{:S(2)}, u32[]{:S(2)}) collective-permute-start(bf16[72,128]{1,0:T(8,128)(2,1)S(1)} %reduce-precision_convert_fusion.refs_0_), channel_id=1, source_target_pairs={{0,4},{4,0},{8,12},{12,8},{1,5},{5,1},{9,13},{13,9},{2,6},{6,2},{1... | collective-permute-start | bytes 55304 | tf_op jit(solution)/shard_map/ppermute | solution.py:505
  16.8 2.3 %pair_outputs.1 = (bf16[1024,128]{1,0:T(8,128)(2,1)}, bf16[1024,128]{1,0:T(8,128)(2,1)}, bf16[1024,128]{1,0:T(8,128)(2,1)}, bf16[1024,128]{1,0:T(8,128)(2,1)}) custom-call(s32[1,128]{1,0:T(1,128)S(1)} %get-tuple-element.55.refs_0_, ...), custom_call_target="tpu_custom_call", output_to_operand_aliasing={{0}: (8, {}), {1}: (9, {}), {2}: (10, {}), {3}: (11, {})} | custom-call | flops 268435456 | bytes 8388608 | tf_op jit(solution)/shard_map/pair_outputs/pallas_call | solution.py:483
  19.1 0.0 collective-permute-done.2.refs_1_
  19.2 0.0 collective-permute-done.3.refs_2_
  19.2 0.1 collective-permute-done.4.refs_3_
  19.3 0.6 %totals.1 = (f32[64,128]{1,0:T(8,128)}, f32[8,128]{1,0:T(8,128)}) custom-call(bf16[72,128]{1,0:T(8,128)(2,1)S(1)} %reduce-precision_convert_fusion.refs_0_, bf16[72,128]{1,0:T(8,128)(2,1)S(1)} %collective-permute-done.2.refs_1_, bf16[72,128]{1,0:T(8,128)(2,1)S(1)} %collective-permute-done.3.refs_2_, bf16[72,128]{1,0:T(8,128)(2,1)S(1)} %collective-permute-done.4.refs_3_), custom_call_target="tpu_custom_call" | custom-call | tf_op jit(solution)/shard_map/totals/pallas_call | solution.py:530
  (4 shorter events, 0.1 us)
Async XLA Ops:
  5.6 6.4 %collective-permute-start = (bf16[1024,128]{1,0:T(8,128)(2,1)S(1)}, bf16[1024,128]{1,0:T(8,128)(2,1)S(1)}, u32[]{:S(2)}, u32[]{:S(2)}) collective-permute-start(bf16[1024,128]{1,0:T(8,128)(2,1)S(1)} %get-tuple-element.62.own_ref), channel_id=1, source_target_pairs={{0,16},{16,0},{1,17},{17,1},{2,18},{18,2},{3,19},{19,3},{4,20},{20... | collective-permute-start | bytes 786440 | tf_op jit(solution)/shard_map/ppermute | solution.py:557
  8.1 4.8 %collective-permute-start.1 = (bf16[72,128]{1,0:T(8,128)(2,1)S(1)}, bf16[72,128]{1,0:T(8,128)(2,1)S(1)}, u32[]{:S(2)}, u32[]{:S(2)}) collective-permute-start(bf16[72,128]{1,0:T(8,128)(2,1)S(1)} %get-tuple-element.71._), channel_id=1, source_target_pairs={{0,16},{16,0},{1,17},{17,1},{2,18},{18,2},{3,19},{19,3},{4,20},{20... | collective-permute-start | bytes 55304 | tf_op jit(solution)/shard_map/ppermute | solution.py:559
  12.9 6.3 %collective-permute-start.2 = (bf16[72,128]{1,0:T(8,128)(2,1)S(1)}, bf16[72,128]{1,0:T(8,128)(2,1)S(1)}, u32[]{:S(2)}, u32[]{:S(2)}) collective-permute-start(bf16[72,128]{1,0:T(8,128)(2,1)S(1)} %reduce-precision_convert_fusion.refs_0_), channel_id=1, source_target_pairs={{0,8},{4,12},{8,4},{12,0},{1,9},{5,13},{9,5},{13,1},{2,10},{6,14},... | collective-permute-start | bytes 55304 | tf_op jit(solution)/shard_map/ppermute | solution.py:505
  15.5 3.7 %collective-permute-start.3 = (bf16[72,128]{1,0:T(8,128)(2,1)S(1)}, bf16[72,128]{1,0:T(8,128)(2,1)S(1)}, u32[]{:S(2)}, u32[]{:S(2)}) collective-permute-start(bf16[72,128]{1,0:T(8,128)(2,1)S(1)} %reduce-precision_convert_fusion.refs_0_), channel_id=1, source_target_pairs={{0,12},{4,8},{8,0},{12,4},{1,13},{5,9},{9,1},{13,5},{2,14},{6,10},... | collective-permute-start | bytes 55304 | tf_op jit(solution)/shard_map/ppermute | solution.py:505
  16.6 2.7 %collective-permute-start.4 = (bf16[72,128]{1,0:T(8,128)(2,1)S(1)}, bf16[72,128]{1,0:T(8,128)(2,1)S(1)}, u32[]{:S(2)}, u32[]{:S(2)}) collective-permute-start(bf16[72,128]{1,0:T(8,128)(2,1)S(1)} %reduce-precision_convert_fusion.refs_0_), channel_id=1, source_target_pairs={{0,4},{4,0},{8,12},{12,8},{1,5},{5,1},{9,13},{13,9},{2,6},{6,2},{1... | collective-permute-start | bytes 55304 | tf_op jit(solution)/shard_map/ppermute | solution.py:505

commit v11 on v10

--- a/solution.py
+++ b/solution.py
@@ -188,8 +188,7 @@
             copy.wait()
         local_part(per_group, held, sums_ref)
         if turn == 0:
-            bounds = (0, 3 * held[5].shape[0] // 8, 3 * held[5].shape[0] // 4)
-            filters(per_group, held, None, out_refs, made_refs, out_sems, [("free", bounds)])
+            filters(per_group, held, None, out_refs, made_refs, out_sems, ahead)
 
 
 def turn_sums(sources, *given):
@@ -388,12 +387,26 @@
     )(keep, taps, skip_rows, query, key, value, grad, before, following)
 
 
+def ahead(groups, first):
+    share = groups * (12 if first else 8) // 16
+    return [("free", (0, share // 2, share))]
+
+
+def behind(groups, first):
+    bounds = ahead(groups, first)[0][1]
+    return [("bound", bounds)] + [("all", (bounds[-1], groups))] * (bounds[-1] < groups)
+
+
+def whole(groups, first):
+    return [("all", (0, groups // 2, groups))]
+
+
 def filters(per_group, held, halo_ref, out_refs, made_refs, sems, tasks):
     first = lax.axis_index("ctx") == 0
 
     def run(here):
         copies = []
-        for index, (chosen, bounds) in enumerate(tasks):
+        for index, (chosen, bounds) in enumerate(tasks(held[5].shape[0], here)):
             forward = chosen == "all" or (chosen == "free") == here
             backward = chosen == "all" or (chosen == "free") != here
             copies += filter_groups(
@@ -469,12 +482,10 @@
 def pair_kernel(per_group, *refs):
     held, halo_ref, out_refs = refs[:7], refs[7], refs[12:16]
     made_refs, sems = refs[16:20], refs[20]
-    groups = held[5].shape[0]
     even = lax.axis_index("tp") % 2 == 0
     rest = (per_group, held, halo_ref, out_refs, made_refs, sems)
-    pl.when(even)(functools.partial(filters, *rest, [("all", (0, groups // 2, groups))]))
-    tasks = [("bound", (0, 3 * groups // 8, 3 * groups // 4)), ("all", (3 * groups // 4, groups))]
-    pl.when(jnp.logical_not(even))(functools.partial(filters, *rest, tasks))
+    pl.when(even)(functools.partial(filters, *rest, whole))
+    pl.when(jnp.logical_not(even))(functools.partial(filters, *rest, behind))
 
 
 def pair_outputs(held, halo, results):

time: 20.1 us -> 20.1 us (level)
    ppermute x1, starting transfers between devices: 2.45 us -> 2.12 us  [body(): halo = lax.ppermute(own, 'ctx', swap)]
    ppermute x3, starting transfers between devices: 3.91 us -> 4.18 us  [gather_terms(): lax.ppermute(sums, axis, list(enumerate(targets)))]
  transfers between devices with their start and end apart: 5 -> 5, of which waited for: 2 -> 2; matrix products, arithmetic and copies ran while one was open for 0% -> 0% of each run, Pallas kernels for 19% -> 18%
where the time goes in v11:
time: 20.1 us; the launch traced here: 20 us
  Pallas kernels  9.25 us (46%)
  starting transfers between devices  6.4 us (32%)
  waiting for transfers between devices  3.59 us (18%)
  between operations  0.7 us (3%)
    pallas_call x1, Pallas kernels, first_turn(): pl.pallas_call(functools.partial(first_kernel, channels // groups), in_sp...  4.92 us
    ppermute x3, starting transfers between devices, gather_terms(): lax.ppermute(sums, axis, list(enumerate(targets)))  4.18 us
    ppermute x1, waiting for transfers between devices, body(): halo = lax.ppermute(own, 'ctx', swap)  3.43 us
    pallas_call x1, Pallas kernels, pair_outputs(): pl.pallas_call(functools.partial(pair_kernel, channels // held[5].shape[0...  2.33 us
    ppermute x1, starting transfers between devices, body(): halo = lax.ppermute(own, 'ctx', swap)  2.12 us
    pallas_call x1, Pallas kernels, halo_sums(): pl.pallas_call(functools.partial(halo_kernel, per_group), in_specs=[whole...  0.88 us
    pallas_call x1, Pallas kernels, totals(): pl.pallas_call(functools.partial(total_kernel, groups, tap_scale, skip_sc...  0.65 us
    pallas_call x1, Pallas kernels, ready_sides(): pl.pallas_call(functools.partial(ready_kernel, per_group), in_specs=[whol...  0.43 us
  transfers between devices with their start and end apart: 5, of which 2 were waited for; matrix products, arithmetic and copies ran while one was open for 0% of the time, Pallas kernels for 18%

profile of v11, /device:TPU:1, one launch (start us, length us, event | category | flops | bytes accessed | tf_op | source)
XLA Modules:
  0.0 20.0 jit_solution(7175242864690532936)
XLA Ops:
  0.6 4.9 %first_turn.1 = (bf16[1024,128]{1,0:T(8,128)(2,1)S(1)}, s32[1,128]{1,0:T(1,128)S(1)}, bf16[1024,128]{1,0:T(8,128)(2,1)S(1)}, bf16[1024,128]{1,0:T(8,128)(2,1)S(1...) custom-call(s32[1,128]{1,0:T(1,128)} %refs_0_.1, ...), custom_call_target="tpu_custom_call" | custom-call | tf_op jit(solution)/shard_map/first_turn/pallas_call | solution.py:144
  5.6 2.1 %collective-permute-start = (bf16[1024,128]{1,0:T(8,128)(2,1)S(1)}, bf16[1024,128]{1,0:T(8,128)(2,1)S(1)}, u32[]{:S(2)}, u32[]{:S(2)}) collective-permute-start(bf16[1024,128]{1,0:T(8,128)(2,1)S(1)} %get-tuple-element.62.own_ref), channel_id=1, source_target_pairs={{0,16},{16,0},{1,17},{17,1},{2,18},{18,2},{3,19},{19,3},{4,20},{20... | collective-permute-start | bytes 786440 | tf_op jit(solution)/shard_map/ppermute | solution.py:568
  7.7 0.1 collective-permute-start.1
  7.8 0.4 %ready_sides.1 = (bf16[8,256,512]{2,1,0:T(8,128)(2,1)S(1)}, bf16[8,512,256]{2,1,0:T(8,128)(2,1)S(1)}) custom-call(bf16[1024,128]{1,0:T(8,128)(2,1)S(1)} %get-tuple-element.62.own_ref, bf16[72,128]{1,0:T(8,128)(2,1)S(1)} %get-tuple-element.71._), custom_call_target="tpu_custom_call" | custom-call | flops 67108864 | bytes 8388608 | tf_op jit(solution)/shard_map/ready_sides/pallas_call | solution.py:296
  8.3 3.4 %collective-permute-done.refs_7_.halo_ref = bf16[1024,128]{1,0:T(8,128)(2,1)S(1)} collective-permute-done((bf16[1024,128]{1,0:T(8,128)(2,1)S(1)}, bf16[1024,128]{1,0:T(8,128)(2,1)S(1)}, u32[]{:S(2)}, u32[]{:S(2)}) %collective-permute-start) | collective-permute-done | bytes 262176 | tf_op jit(solution)/shard_map/ppermute | solution.py:568
  11.7 0.9 %halo_sums.1 = f32[64,128]{1,0:T(8,128)S(1)} custom-call(bf16[1024,128]{1,0:T(8,128)(2,1)S(1)} %collective-permute-done.refs_7_.halo_ref, bf16[8,256,512]{2,1,0:T(8,128)(2,1)S(1)} %get-tuple-element.72.left_ref, bf16[8,512,256]{2,1,0:T(8,128)(2,1)S(1)} %get-tuple-element.73.right_ref), custom_call_target="tpu_custom_call" | custom-call | flops 67108864 | bytes 8388608 | tf_op jit(solution)/shard_map/halo_sums/pallas_call | solution.py:313
  12.6 0.0 collective-permute-done.1
  12.6 2.9 %collective-permute-start.2 = (bf16[72,128]{1,0:T(8,128)(2,1)S(1)}, bf16[72,128]{1,0:T(8,128)(2,1)S(1)}, u32[]{:S(2)}, u32[]{:S(2)}) collective-permute-start(bf16[72,128]{1,0:T(8,128)(2,1)S(1)} %reduce-precision_convert_fusion.refs_0_), channel_id=1, source_target_pairs={{0,8},{4,12},{8,4},{12,0},{1,9},{5,13},{9,5},{13,1},{2,10},{6,14},... | collective-permute-start | bytes 55304 | tf_op jit(solution)/shard_map/ppermute | solution.py:516
  15.5 1.1 %collective-permute-start.3 = (bf16[72,128]{1,0:T(8,128)(2,1)S(1)}, bf16[72,128]{1,0:T(8,128)(2,1)S(1)}, u32[]{:S(2)}, u32[]{:S(2)}) collective-permute-start(bf16[72,128]{1,0:T(8,128)(2,1)S(1)} %reduce-precision_convert_fusion.refs_0_), channel_id=1, source_target_pairs={{0,12},{4,8},{8,0},{12,4},{1,13},{5,9},{9,1},{13,5},{2,14},{6,10},... | collective-permute-start | bytes 55304 | tf_op jit(solution)/shard_map/ppermute | solution.py:516
  16.6 0.2 %collective-permute-start.4 = (bf16[72,128]{1,0:T(8,128)(2,1)S(1)}, bf16[72,128]{1,0:T(8,128)(2,1)S(1)}, u32[]{:S(2)}, u32[]{:S(2)}) collective-permute-start(bf16[72,128]{1,0:T(8,128)(2,1)S(1)} %reduce-precision_convert_fusion.refs_0_), channel_id=1, source_target_pairs={{0,4},{4,0},{8,12},{12,8},{1,5},{5,1},{9,13},{13,9},{2,6},{6,2},{1... | collective-permute-start | bytes 55304 | tf_op jit(solution)/shard_map/ppermute | solution.py:516
  16.8 2.3 %pair_outputs.1 = (bf16[1024,128]{1,0:T(8,128)(2,1)}, bf16[1024,128]{1,0:T(8,128)(2,1)}, bf16[1024,128]{1,0:T(8,128)(2,1)}, bf16[1024,128]{1,0:T(8,128)(2,1)}) custom-call(s32[1,128]{1,0:T(1,128)S(1)} %get-tuple-element.55.refs_0_, ...), custom_call_target="tpu_custom_call", output_to_operand_aliasing={{0}: (8, {}), {1}: (9, {}), {2}: (10, {}), {3}: (11, {})} | custom-call | flops 268435456 | bytes 8388608 | tf_op jit(solution)/shard_map/pair_outputs/pallas_call | solution.py:494
  19.1 0.0 collective-permute-done.2.refs_1_
  19.2 0.0 collective-permute-done.3.refs_2_
  19.2 0.1 collective-permute-done.4.refs_3_
  19.3 0.6 %totals.1 = (f32[64,128]{1,0:T(8,128)}, f32[8,128]{1,0:T(8,128)}) custom-call(bf16[72,128]{1,0:T(8,128)(2,1)S(1)} %reduce-precision_convert_fusion.refs_0_, bf16[72,128]{1,0:T(8,128)(2,1)S(1)} %collective-permute-done.2.refs_1_, bf16[72,128]{1,0:T(8,128)(2,1)S(1)} %collective-permute-done.3.refs_2_, bf16[72,128]{1,0:T(8,128)(2,1)S(1)} %collective-permute-done.4.refs_3_), custom_call_target="tpu_custom_call" | custom-call | tf_op jit(solution)/shard_map/totals/pallas_call | solution.py:541
  (4 shorter events, 0.1 us)
Async XLA Ops:
  5.6 6.1 %collective-permute-start = (bf16[1024,128]{1,0:T(8,128)(2,1)S(1)}, bf16[1024,128]{1,0:T(8,128)(2,1)S(1)}, u32[]{:S(2)}, u32[]{:S(2)}) collective-permute-start(bf16[1024,128]{1,0:T(8,128)(2,1)S(1)} %get-tuple-element.62.own_ref), channel_id=1, source_target_pairs={{0,16},{16,0},{1,17},{17,1},{2,18},{18,2},{3,19},{19,3},{4,20},{20... | collective-permute-start | bytes 786440 | tf_op jit(solution)/shard_map/ppermute | solution.py:568
  7.7 4.9 %collective-permute-start.1 = (bf16[72,128]{1,0:T(8,128)(2,1)S(1)}, bf16[72,128]{1,0:T(8,128)(2,1)S(1)}, u32[]{:S(2)}, u32[]{:S(2)}) collective-permute-start(bf16[72,128]{1,0:T(8,128)(2,1)S(1)} %get-tuple-element.71._), channel_id=1, source_target_pairs={{0,16},{16,0},{1,17},{17,1},{2,18},{18,2},{3,19},{19,3},{4,20},{20... | collective-permute-start | bytes 55304 | tf_op jit(solution)/shard_map/ppermute | solution.py:570
  12.6 6.5 %collective-permute-start.2 = (bf16[72,128]{1,0:T(8,128)(2,1)S(1)}, bf16[72,128]{1,0:T(8,128)(2,1)S(1)}, u32[]{:S(2)}, u32[]{:S(2)}) collective-permute-start(bf16[72,128]{1,0:T(8,128)(2,1)S(1)} %reduce-precision_convert_fusion.refs_0_), channel_id=1, source_target_pairs={{0,8},{4,12},{8,4},{12,0},{1,9},{5,13},{9,5},{13,1},{2,10},{6,14},... | collective-permute-start | bytes 55304 | tf_op jit(solution)/shard_map/ppermute | solution.py:516
  15.5 3.7 %collective-permute-start.3 = (bf16[72,128]{1,0:T(8,128)(2,1)S(1)}, bf16[72,128]{1,0:T(8,128)(2,1)S(1)}, u32[]{:S(2)}, u32[]{:S(2)}) collective-permute-start(bf16[72,128]{1,0:T(8,128)(2,1)S(1)} %reduce-precision_convert_fusion.refs_0_), channel_id=1, source_target_pairs={{0,12},{4,8},{8,0},{12,4},{1,13},{5,9},{9,1},{13,5},{2,14},{6,10},... | collective-permute-start | bytes 55304 | tf_op jit(solution)/shard_map/ppermute | solution.py:516
  16.6 2.7 %collective-permute-start.4 = (bf16[72,128]{1,0:T(8,128)(2,1)S(1)}, bf16[72,128]{1,0:T(8,128)(2,1)S(1)}, u32[]{:S(2)}, u32[]{:S(2)}) collective-permute-start(bf16[72,128]{1,0:T(8,128)(2,1)S(1)} %reduce-precision_convert_fusion.refs_0_), channel_id=1, source_target_pairs={{0,4},{4,0},{8,12},{12,8},{1,5},{5,1},{9,13},{13,9},{2,6},{6,2},{1... | collective-permute-start | bytes 55304 | tf_op jit(solution)/shard_map/ppermute | solution.py:516
